TPU v7x, 32 devices: a whole 2x2x4 slice. The times are simulated.
32 devices in a mesh: ctx: 8 (over y, x, core), head: 4 (over z).
Axes of the slice: x: 2, y: 2, z: 4, core: 2. Of those that a mesh axis runs over, the one named last changes fastest.
Arguments:
- latent_keys: bfloat16 [1024, 576], P('ctx'), may hold values from -6 to 6
- index_keys: bfloat16 [1024, 128], P('ctx'), may hold values from -6 to 6
- main_query: bfloat16 [1024, 73728], P('ctx', 'head'), may hold values from -107 to 107
- index_query: bfloat16 [1024, 8192], P('ctx', 'head'), may hold values from -10 to 10
- index_weight: bfloat16 [1024, 64], P('ctx', 'head'), may hold values from 0.029907227 to 0.29882812
- segment_ids: int32 [1024], replicated, may hold values from 0 to 7, never falling along the last dimension, each value on 1 to 256 neighbouring positions
- block_order: int32 [16], replicated, may hold values from 0 to 15, each once
Outputs:
- kl: float32 [1024], P('ctx')
Inputs may be any that keep to these rules, and one draw needn't show every extreme that they name: `segment_ids`: never falls along the sequence; each document holds 1 to 256 positions and one holds exactly that many. `block_order`: each block number appears once.
All inputs are finite; a program needn't handle non-finite values.
Results may differ from a plain program's by a relative error of at most 0.0003.
Values may be sent and summed in bfloat16 or wider, within the bound.
No kernel may reach another device: no remote copies, remote signals or barrier semaphores. Data moves between devices by JAX's collectives and lax.ppermute only.
A program may use at most 64 MiB of HBM per device.

v0:
```python
import functools
import math

import jax
import jax.numpy as jnp
from jax import lax
from jax.experimental import pallas as pl
from jax.experimental.pallas import tpu as pltpu
from jax.sharding import PartitionSpec as P


LANES = 128
score_scale = 192.0 ** (-0.5)
hidden = -1e30


def swap(x, axis, distance):
    size = lax.axis_size(axis)
    return lax.ppermute(x, axis, [(i, i ^ distance) for i in range(size)])


def window_masks(block, reach, half, seg_ref):
    table_rows = seg_ref.shape[0]
    first = block - reach // half
    row0 = lax.div(first + 2 * table_rows, 2) - table_rows
    pieces = []
    for k in range(reach // LANES + 2):
        row = jnp.clip(row0 + k, 0, table_rows - 1)
        pieces.append(seg_ref[pl.ds(row, 1), :].astype(jnp.float32))
    wide = jnp.concatenate(pieces, axis=1)
    width = wide.shape[1]
    moved = pltpu.roll(wide, width - half, 1)
    odd = lax.rem(first + 2 * table_rows, 2)
    wide = jnp.where(odd == 1, moved, wide)
    tail_seg = jnp.broadcast_to(wide[:, reach : reach + LANES], (half, LANES))
    head_seg = jnp.broadcast_to(wide[:, :LANES], (half, LANES))
    row_id = lax.broadcasted_iota(jnp.int32, (half, LANES), 0)
    lane_id = lax.broadcasted_iota(jnp.int32, (half, LANES), 1)
    query_seg = jnp.sum(jnp.where(row_id == lane_id, tail_seg, 0.0), axis=1, keepdims=True)
    in_tail = (lane_id <= row_id) & (lane_id < half)
    key_seg = jnp.concatenate(
        [jnp.where(in_tail, tail_seg, head_seg), jnp.broadcast_to(wide[:, LANES:reach], (half, reach - LANES))], axis=1
    )
    place = lax.broadcasted_iota(jnp.int32, (half, reach), 1)
    rows_full = lax.broadcasted_iota(jnp.int32, (half, reach), 0)
    tail_full = (place <= rows_full) & (place < half)
    position = first * half + place + jnp.where(tail_full, reach, 0)
    visible = (key_seg == query_seg) & (position >= 0)
    return in_tail, visible


def ring_fold(in_tail, wide, reach):
    low = jnp.where(in_tail, wide[:, reach : reach + LANES], wide[:, :LANES])
    return jnp.concatenate([low, wide[:, LANES:reach]], axis=1)


def own_block(keep):
    bit = lax.axis_index("head") & 1
    return bit if keep else 1 - bit


def prelude_kernel(sizes, order_ref, seg_ref, weight_ref, query_hbm, index_query_hbm,
                   bias_ref, gain_ref, query_ref, index_query_ref, sems):
    half, reach, copies = sizes
    rows, _ = query_ref.shape
    waits = [pltpu.make_async_copy(index_query_hbm, index_query_ref, sems.at[copies])]
    for c in range(copies):
        part = slice(c * (rows // copies), (c + 1) * (rows // copies))
        waits.append(pltpu.make_async_copy(query_hbm.at[part, :], query_ref.at[part, :], sems.at[c]))
    for copy in waits:
        copy.start()
    me = lax.axis_index("ctx")
    for i in range(2):
        _, visible = window_masks(order_ref[me * 2 + i], reach, half, seg_ref)
        bias_ref[i] = jnp.where(visible, 0.0, hidden)
    gain_ref[...] = jnp.transpose(weight_ref[...].astype(jnp.float32), (1, 0))
    for copy in waits:
        copy.wait()


def block_kernel(sizes, keep, order_ref, bias_ref, gain_ref, query_ref, index_query_ref, *refs):
    n_ctx, half, reach, key_width = sizes
    piece_refs = refs[:n_ctx]
    out_ref, stack_ref, index_window, even_ref, odd_ref, inverse_ref = refs[n_ctx:]
    wide = even_ref.shape[1]
    key_pad = even_ref.shape[0]
    idim = index_window.shape[1]
    me = lax.axis_index("ctx")
    mine = own_block(keep)
    rows_here = pl.ds(pl.multiple_of(mine * half, half), half)
    for s in range(n_ctx):
        stack_ref[me ^ s] = piece_refs[s][...]
    for slot in range(order_ref.shape[0]):
        inverse_ref[order_ref[slot]] = slot
    block = order_ref[me * 2 + mine]
    first = block - reach // half
    slots = [inverse_ref[jnp.maximum(first + w, 0)] for w in range(reach // half + 1)]

    for w, slot in enumerate(slots):
        at = pl.multiple_of(key_width + (slot & 1) * half, half)
        index_window[w * half : (w + 1) * half, :] = stack_ref[slot >> 1, pl.ds(at, half), :]
    index_window[reach + half :, :] = jnp.zeros((wide - reach - half, idim), index_window.dtype)
    left = lax.broadcasted_iota(jnp.int32, (key_width, LANES), 1) < half
    even_ref[key_width:, :] = jnp.zeros((key_pad - key_width, wide), even_ref.dtype)
    odd_ref[: key_pad - key_width, :] = jnp.zeros((key_pad - key_width, wide), odd_ref.dtype)
    for c in range(wide // LANES):
        halves = []
        for side in (0, 1):
            w = 2 * c + side
            if w >= len(slots):
                halves.append(halves[0])
                continue
            tile = stack_ref[slots[w] >> 1, :key_width, :].astype(jnp.float32)
            turned = pltpu.roll(tile, half, 1)
            halves.append(jnp.where((slots[w] & 1) == side, tile, turned))
        both = jnp.where(left, halves[0], halves[1]).astype(even_ref.dtype)
        even_ref[:key_width, c * LANES : (c + 1) * LANES] = both
        odd_ref[key_pad - key_width :, c * LANES : (c + 1) * LANES] = both

    row_id = lax.broadcasted_iota(jnp.int32, (half, LANES), 0)
    lane_id = lax.broadcasted_iota(jnp.int32, (half, LANES), 1)
    in_tail = (lane_id <= row_id) & (lane_id < half)
    bias = bias_ref[mine]
    gains = gain_ref[rows_here, :]
    index_heads = index_query_ref.shape[1] // idim
    lhs = jnp.concatenate([index_query_ref[rows_here, j * idim : (j + 1) * idim] for j in range(index_heads)], axis=0)
    dots = lax.dot_general(lhs, index_window[...], (((1,), (1,)), ((), ())), preferred_element_type=jnp.float32)
    total = jnp.zeros((half, reach), jnp.float32)
    for j in range(index_heads):
        folded = ring_fold(in_tail, dots[j * half : (j + 1) * half, :], reach)
        total = total + gains[:, j : j + 1] * jnp.maximum(folded, 0.0)
    out_ref[1] = jnp.where(bias == 0.0, total, 0.0)

    heads = query_ref.shape[1] // key_width
    total = jnp.zeros((half, reach), jnp.float32)
    for parity, keys_ref in ((0, even_ref), (1, odd_ref)):
        starts = [g * 2 * key_width + parity * (2 * key_width - key_pad) for g in range(heads // 2)]
        lhs = jnp.concatenate([query_ref[rows_here, at : at + key_pad] for at in starts], axis=0)
        raw = lax.dot_general(lhs, keys_ref[...], (((1,), (0,)), ((), ())), preferred_element_type=jnp.float32)
        for g in range(heads // 2):
            scores = ring_fold(in_tail, raw[g * half : (g + 1) * half, :], reach) + bias
            row_max = jnp.max(scores, axis=1, keepdims=True)
            powers = jnp.exp2((scores - row_max) * (score_scale * math.log2(math.e)))
            share = 1.0 / jnp.sum(powers, axis=1, keepdims=True)
            total = total + powers * share
    out_ref[0] = total


def loss_kernel(sizes, bias_ref, *refs):
    half, total_heads = sizes
    value_refs, out_ref = refs[:-1], refs[-1]
    mine = own_block(True)
    visible = bias_ref[mine] == 0.0
    target = functools.reduce(jnp.add, [ref[0] for ref in value_refs]) * (1.0 / total_heads)
    index_score = functools.reduce(jnp.add, [ref[1] for ref in value_refs])
    masked = jnp.where(visible, index_score, hidden)
    row_max = jnp.max(masked, axis=1, keepdims=True)
    exp_sum = jnp.sum(jnp.where(visible, jnp.exp(masked - row_max), 0.0), axis=1, keepdims=True)
    positive = target > 0.0
    logs = jnp.log(jnp.where(positive, target, 1.0))
    entropy_sum = jnp.sum(jnp.where(positive, target * logs, 0.0), axis=1, keepdims=True)
    cross_sum = jnp.sum(jnp.where(visible, target * index_score, 0.0), axis=1, keepdims=True)
    target_sum = jnp.sum(target, axis=1, keepdims=True)
    column = entropy_sum - cross_sum + (row_max + jnp.log(exp_sum)) * target_sum
    rows = out_ref.shape[1]
    row_id = lax.broadcasted_iota(jnp.int32, (half, rows), 0)
    lane_id = lax.broadcasted_iota(jnp.int32, (half, rows), 1)
    out_ref[...] = jnp.sum(jnp.where(row_id + mine * half == lane_id, column, 0.0), axis=0, keepdims=True)


def per_device(
    latent_keys, index_keys, main_query, index_query, index_weight, segment_ids, block_order
):
    n_ctx, n_head = lax.axis_size("ctx"), lax.axis_size("head")
    rows, key_width = latent_keys.shape
    idim = index_keys.shape[1]
    seq_len = segment_ids.shape[0]
    half = seq_len // block_order.shape[0]
    reach = seq_len // 4
    heads = main_query.shape[1] // key_width
    key_pad = -(-key_width // LANES) * LANES
    wide = reach + LANES

    vmem = pl.BlockSpec(memory_space=pltpu.VMEM)
    smem = pl.BlockSpec(memory_space=pltpu.SMEM)
    hbm = pl.BlockSpec(memory_space=pltpu.HBM)
    index_heads = index_weight.shape[1]

    packed = jnp.concatenate([latent_keys.T, index_keys], axis=0)
    own_core = [packed]
    for s in reversed(range(1, n_ctx // 2)):
        own_core.append(swap(packed, "ctx", 2 * s))
    own_core = [packed] + own_core[:0:-1]
    pieces = []
    for piece in own_core:
        pieces += [piece, swap(piece, "ctx", 1)]
    seg_table = segment_ids.reshape(seq_len // LANES, LANES)

    copies = 8
    far_query = pltpu.with_memory_space_constraint(main_query, pltpu.HBM)
    far_index_query = pltpu.with_memory_space_constraint(index_query, pltpu.HBM)
    bias, gains, near_query, near_index_query = pl.pallas_call(
        functools.partial(prelude_kernel, (half, reach, copies)),
        out_shape=(
            jax.ShapeDtypeStruct((2, half, reach), jnp.float32),
            jax.ShapeDtypeStruct((rows, index_heads), jnp.float32),
            jax.ShapeDtypeStruct(main_query.shape, main_query.dtype),
            jax.ShapeDtypeStruct(index_query.shape, index_query.dtype),
        ),
        in_specs=[smem, vmem, vmem, hbm, hbm],
        out_specs=(vmem, vmem, vmem, vmem),
        scratch_shapes=[pltpu.SemaphoreType.DMA((copies + 1,))],
        compiler_params=pltpu.CompilerParams(vmem_limit_bytes=12 << 20),
        cost_estimate=pl.CostEstimate(flops=1 << 20, bytes_accessed=10 << 20, transcendentals=0),
        name="prelude",
    )(block_order, seg_table, index_weight.T, far_query, far_index_query)

    def block_sums(keep):
        return pl.pallas_call(
            functools.partial(block_kernel, (n_ctx, half, reach, key_width), keep),
            out_shape=jax.ShapeDtypeStruct((2, half, reach), jnp.float32),
            in_specs=[smem] + [vmem] * (4 + n_ctx),
            out_specs=vmem,
            scratch_shapes=[
                pltpu.VMEM((n_ctx, key_width + idim, LANES), jnp.bfloat16),
                pltpu.VMEM((wide, idim), jnp.bfloat16),
                pltpu.VMEM((key_pad, wide), jnp.bfloat16),
                pltpu.VMEM((key_pad, wide), jnp.bfloat16),
                pltpu.SMEM((block_order.shape[0],), jnp.int32),
            ],
            compiler_params=pltpu.CompilerParams(vmem_limit_bytes=28 << 20),
            cost_estimate=pl.CostEstimate(
                flops=2 * half * wide * (heads * key_pad + index_heads * idim), bytes_accessed=4 << 20, transcendentals=0
            ),
            name="keep_sums" if keep else "give_sums",
        )(block_order, bias, gains, near_query, near_index_query, *pieces)

    given = block_sums(False)
    kept = block_sums(True)
    value = kept + swap(given, "head", 1)
    distances = [1 << k for k in range(1, n_head.bit_length() - 1)]
    for distance in distances[:-1]:
        value = value + swap(value, "head", distance)
    values = [value] + [swap(value, "head", distance) for distance in distances[-1:]]
    loss = pl.pallas_call(
        functools.partial(loss_kernel, (half, heads * n_head)),
        out_shape=jax.ShapeDtypeStruct((1, rows), jnp.float32),
        in_specs=[vmem] * (1 + len(values)),
        out_specs=vmem,
        compiler_params=pltpu.CompilerParams(vmem_limit_bytes=8 << 20),
        name="row_losses",
    )(bias, *values)
    return (loss + swap(loss, "head", 1)).reshape(rows)


def solution(mesh):
    in_specs = (
        P("ctx", None),
        P("ctx", None),
        P("ctx", "head"),
        P("ctx", "head"),
        P("ctx", "head"),
        P(),
        P(),
    )
    return jax.shard_map(per_device, mesh=mesh, in_specs=in_specs, out_specs=P("ctx"), check_vma=False)
```

profile of v0, /device:TPU:0, one launch (start us, length us, event | category | flops | bytes accessed | tf_op | source)
XLA Modules:
  0.0 40.8 jit_solution(3402840290351616260)
XLA Ops:
  0.0 0.0 copy-start.1
  0.0 1.0 %pad_maximum_fusion.refs_0_ = bf16[704,128]{1,0:T(8,128)(2,1)S(1)} fusion(bf16[128,128]{1,0:T(8,128)(2,1)} %param.8, bf16[576,128]{1,0:T(8,128)(2,1)} %bitcast.7), kind=kLoop, calls=%fused_computation | loop fusion | flops 360448 | bytes 360448 | tf_op jit(solution)/shard_map/concatenate | solution.py:189
  1.0 4.0 %collective-permute-start.5 = (bf16[704,128]{1,0:T(8,128)(2,1)S(1)}, bf16[704,128]{1,0:T(8,128)(2,1)S(1)}, u32[]{:S(2)}, u32[]{:S(2)}) collective-permute-start(bf16[704,128]{1,0:T(8,128)(2,1)S(1)} %pad_maximum_fusion.refs_0_), channel_id=1, source_target_pairs={{0,24},{4,28},{8,16},{12,20},{16,8},{20,12},{24,0},{28,4},{1,25},{... | collective-permute-start | bytes 540680 | tf_op jit(solution)/shard_map/ppermute | solution.py:19
  4.9 0.5 %collective-permute-start.3 = (bf16[704,128]{1,0:T(8,128)(2,1)S(1)}, bf16[704,128]{1,0:T(8,128)(2,1)S(1)}, u32[]{:S(2)}, u32[]{:S(2)}) collective-permute-start(bf16[704,128]{1,0:T(8,128)(2,1)S(1)} %pad_maximum_fusion.refs_0_), channel_id=1, source_target_pairs={{0,16},{4,20},{8,24},{12,28},{16,0},{20,4},{24,8},{28,12},{1,17},{... | collective-permute-start | bytes 540680 | tf_op jit(solution)/shard_map/ppermute | solution.py:19
  5.5 0.1 collective-permute-start.1
  5.6 0.0 collective-permute-start
  5.6 4.8 %collective-permute-done.5.refs_6_ = bf16[704,128]{1,0:T(8,128)(2,1)S(1)} collective-permute-done((bf16[704,128]{1,0:T(8,128)(2,1)S(1)}, bf16[704,128]{1,0:T(8,128)(2,1)S(1)}, u32[]{:S(2)}, u32[]{:S(2)}) %collective-permute-start.5) | collective-permute-done | bytes 180256 | tf_op jit(solution)/shard_map/ppermute | solution.py:19
  10.4 0.0 collective-permute-start.6
  10.4 3.0 %collective-permute-done.3.refs_4_ = bf16[704,128]{1,0:T(8,128)(2,1)S(1)} collective-permute-done((bf16[704,128]{1,0:T(8,128)(2,1)S(1)}, bf16[704,128]{1,0:T(8,128)(2,1)S(1)}, u32[]{:S(2)}, u32[]{:S(2)}) %collective-permute-start.3) | collective-permute-done | bytes 180256 | tf_op jit(solution)/shard_map/ppermute | solution.py:19
  13.4 0.0 collective-permute-start.4
  13.4 0.3 collective-permute-done.1.refs_2_
  13.7 0.2 collective-permute-start.2
  13.9 0.0 copy-start
  13.9 0.7 %copy-done = s32[16]{0:T(128)S(1)} copy-done((s32[16]{0:T(128)S(1)}, s32[16]{0:T(128)}, u32[]{:S(2)}) %copy-start) | copy-done | bytes 88
  14.5 0.0 copy-start.2
  14.5 0.7 %copy-done.2 = s32[1024]{0:T(1024)S(1)} copy-done((s32[1024]{0:T(1024)S(1)}, s32[1024]{0:T(1024)}, u32[]{:S(2)}) %copy-start.2) | copy-done | bytes 4120
  15.2 0.0 copy-start.3
  15.2 0.7 %copy-done.3 = bf16[128,16]{0,1:T(8,128)(2,1)S(1)} copy-done((bf16[128,16]{0,1:T(8,128)(2,1)S(1)}, bf16[128,16]{0,1:T(8,128)(2,1)}, u32[]{:S(2)}) %copy-start.3) | copy-done | bytes 4120
  15.9 3.1 %prelude.1 = (f32[2,64,256]{2,1,0:T(8,128)S(1)}, f32[128,16]{1,0:T(8,128)S(1)}, bf16[128,18432]{1,0:T(8,128)(2,1)S(1)}, bf16[128,2048]{1,0:T(8,128)(2,1)S(1)}) custom-call(s32[16]{0:T(128)S(1)} %copy-done, s32[8,128]{1,0:T(8,128)S(1)} %bitcast.5, bf16[16,128]{1,0:T(8,128)(2,1)S(1)} %bitcast.6, bf16[128,18432]{1,0:T(8,128)(2,1)} %query_hbm.1, ...), custom_call_target="tpu_custom_call" | custom-call | flops 1048576 | bytes 10485760 | tf_op jit(solution)/shard_map/prelude/pallas_call | solution.py:202
  19.1 0.0 collective-permute-done.refs_1_
  19.1 0.0 collective-permute-done.6.refs_7_
  19.1 0.0 collective-permute-done.4.refs_5_
  19.1 0.0 collective-permute-done.2.refs_3_
  19.1 0.0 copy-done.1
  19.1 3.0 %give_sums.1 = f32[2,64,256]{2,1,0:T(8,128)S(1)} custom-call(s32[16]{0:T(128)S(1)} %copy-done.1, f32[2,64,256]{2,1,0:T(8,128)S(1)} %get-tuple-element.9.bias_ref, f32[128,16]{1,0:T(8,128)S(1)} %get-tuple-element.10.gain_ref, bf16[128,18432]{1,0:T(8,128)(2,1)S(1)} %get-tuple-element.11.query_ref, bf16[128,2048]{1,0:T(8,128)(2,1)S(1)} %get-tuple-element.12.index_query_ref, ...), custom_call_target="tpu_custom_call" | custom-call | flops 1107296256 | bytes 4194304 | tf_op jit(solution)/shard_map/give_sums/pallas_call | solution.py:219
  22.1 1.8 %collective-permute-start.7 = (f32[2,64,256]{2,1,0:T(8,128)S(1)}, f32[2,64,256]{2,1,0:T(8,128)S(1)}, u32[]{:S(2)}, u32[]{:S(2)}) collective-permute-start(f32[2,64,256]{2,1,0:T(8,128)S(1)} %give_sums.1), channel_id=1, source_target_pairs={{0,1},{1,0},{2,3},{3,2},{4,5},{5,4},{6,7},{7,6},{8,9},{9,8},{10,11... | collective-permute-start | bytes 393224 | tf_op jit(solution)/shard_map/ppermute | solution.py:19
  23.9 3.0 %keep_sums.1 = f32[2,64,256]{2,1,0:T(8,128)S(1)} custom-call(s32[16]{0:T(128)S(1)} %copy-done.1, f32[2,64,256]{2,1,0:T(8,128)S(1)} %get-tuple-element.9.bias_ref, f32[128,16]{1,0:T(8,128)S(1)} %get-tuple-element.10.gain_ref, bf16[128,18432]{1,0:T(8,128)(2,1)S(1)} %get-tuple-element.11.query_ref, bf16[128,2048]{1,0:T(8,128)(2,1)S(1)} %get-tuple-element.12.index_query_ref, ...), custom_call_target="tpu_custom_call" | custom-call | flops 1107296256 | bytes 4194304 | tf_op jit(solution)/shard_map/keep_sums/pallas_call | solution.py:219
  26.9 0.9 %collective-permute-done.7 = f32[2,64,256]{2,1,0:T(8,128)S(1)} collective-permute-done((f32[2,64,256]{2,1,0:T(8,128)S(1)}, f32[2,64,256]{2,1,0:T(8,128)S(1)}, u32[]{:S(2)}, u32[]{:S(2)}) %collective-permute-start.7) | collective-permute-done | bytes 131104 | tf_op jit(solution)/shard_map/ppermute | solution.py:19
  27.9 2.7 %collective-permute-start.8 = (f32[2,64,256]{2,1,0:T(8,128)S(1)}, f32[2,64,256]{2,1,0:T(8,128)S(1)}, u32[]{:S(2)}, u32[]{:S(2)}) collective-permute-start(f32[2,64,256]{2,1,0:T(8,128)S(1)} %add.6.refs_0_), channel_id=1, source_target_pairs={{0,2},{1,3},{2,0},{3,1},{4,6},{5,7},{6,4},{7,5},{8,10},{9,11},{10,... | collective-permute-start | bytes 393224 | tf_op jit(solution)/shard_map/ppermute | solution.py:19
  30.5 5.9 %collective-permute-done.8.refs_1_ = f32[2,64,256]{2,1,0:T(8,128)S(1)} collective-permute-done((f32[2,64,256]{2,1,0:T(8,128)S(1)}, f32[2,64,256]{2,1,0:T(8,128)S(1)}, u32[]{:S(2)}, u32[]{:S(2)}) %collective-permute-start.8) | collective-permute-done | bytes 131104 | tf_op jit(solution)/shard_map/ppermute | solution.py:19
  36.5 0.2 row_losses.1
  36.7 0.5 %collective-permute-start.9 = (f32[1,128]{1,0:T(1,128)S(1)}, f32[1,128]{1,0:T(1,128)S(1)}, u32[]{:S(2)}, u32[]{:S(2)}) collective-permute-start(f32[1,128]{1,0:T(1,128)S(1)} %row_losses.1), channel_id=1, source_target_pairs={{0,1},{1,0},{2,3},{3,2},{4,5},{5,4},{6,7},{7,6},{8,9},{9,8},{10,11... | collective-permute-start | bytes 1544 | tf_op jit(solution)/shard_map/ppermute | solution.py:19
  37.2 3.1 %collective-permute-done.9 = f32[1,128]{1,0:T(1,128)S(1)} collective-permute-done((f32[1,128]{1,0:T(1,128)S(1)}, f32[1,128]{1,0:T(1,128)S(1)}, u32[]{:S(2)}, u32[]{:S(2)}) %collective-permute-start.9) | collective-permute-done | bytes 544 | tf_op jit(solution)/shard_map/ppermute | solution.py:19
  40.3 0.5 %add_bitcast_fusion = f32[128]{0:T(128)} fusion(f32[1,128]{1,0:T(1,128)S(1)} %row_losses.1, f32[1,128]{1,0:T(1,128)S(1)} %collective-permute-done.9), kind=kLoop, calls=%fused_computation.1 | loop fusion | flops 128 | bytes 1536 | tf_op jit(solution)/shard_map/reshape | solution.py:253
  (1 shorter events, 0.0 us)
Async XLA Ops:
  0.0 19.1 %copy-start.1 = (s32[16]{0:T(128)S(1)}, s32[16]{0:T(128)}, u32[]{:S(2)}) copy-start(s32[16]{0:T(128)} %order_ref.5) | copy-start | bytes 196
  1.0 9.4 %collective-permute-start.5 = (bf16[704,128]{1,0:T(8,128)(2,1)S(1)}, bf16[704,128]{1,0:T(8,128)(2,1)S(1)}, u32[]{:S(2)}, u32[]{:S(2)}) collective-permute-start(bf16[704,128]{1,0:T(8,128)(2,1)S(1)} %pad_maximum_fusion.refs_0_), channel_id=1, source_target_pairs={{0,24},{4,28},{8,16},{12,20},{16,8},{20,12},{24,0},{28,4},{1,25},{... | collective-permute-start | bytes 540680 | tf_op jit(solution)/shard_map/ppermute | solution.py:19
  4.9 8.4 %collective-permute-start.3 = (bf16[704,128]{1,0:T(8,128)(2,1)S(1)}, bf16[704,128]{1,0:T(8,128)(2,1)S(1)}, u32[]{:S(2)}, u32[]{:S(2)}) collective-permute-start(bf16[704,128]{1,0:T(8,128)(2,1)S(1)} %pad_maximum_fusion.refs_0_), channel_id=1, source_target_pairs={{0,16},{4,20},{8,24},{12,28},{16,0},{20,4},{24,8},{28,12},{1,17},{... | collective-permute-start | bytes 540680 | tf_op jit(solution)/shard_map/ppermute | solution.py:19
  5.5 8.2 %collective-permute-start.1 = (bf16[704,128]{1,0:T(8,128)(2,1)S(1)}, bf16[704,128]{1,0:T(8,128)(2,1)S(1)}, u32[]{:S(2)}, u32[]{:S(2)}) collective-permute-start(bf16[704,128]{1,0:T(8,128)(2,1)S(1)} %pad_maximum_fusion.refs_0_), channel_id=1, source_target_pairs={{0,8},{4,12},{8,0},{12,4},{16,24},{20,28},{24,16},{28,20},{1,9},{5... | collective-permute-start | bytes 540680 | tf_op jit(solution)/shard_map/ppermute | solution.py:19
  5.6 13.5 %collective-permute-start = (bf16[704,128]{1,0:T(8,128)(2,1)S(1)}, bf16[704,128]{1,0:T(8,128)(2,1)S(1)}, u32[]{:S(2)}, u32[]{:S(2)}) collective-permute-start(bf16[704,128]{1,0:T(8,128)(2,1)S(1)} %pad_maximum_fusion.refs_0_), channel_id=1, source_target_pairs={{0,4},{4,0},{8,12},{12,8},{16,20},{20,16},{24,28},{28,24},{1,5},{5... | collective-permute-start | bytes 540680 | tf_op jit(solution)/shard_map/ppermute | solution.py:19
  10.4 8.7 %collective-permute-start.6 = (bf16[704,128]{1,0:T(8,128)(2,1)S(1)}, bf16[704,128]{1,0:T(8,128)(2,1)S(1)}, u32[]{:S(2)}, u32[]{:S(2)}) collective-permute-start(bf16[704,128]{1,0:T(8,128)(2,1)S(1)} %collective-permute-done.5.refs_6_), channel_id=1, source_target_pairs={{0,4},{4,0},{8,12},{12,8},{16,20},{20,16},{24,28},{28,24},{1,5},{5... | collective-permute-start | bytes 540680 | tf_op jit(solution)/shard_map/ppermute | solution.py:19
  13.4 5.7 %collective-permute-start.4 = (bf16[704,128]{1,0:T(8,128)(2,1)S(1)}, bf16[704,128]{1,0:T(8,128)(2,1)S(1)}, u32[]{:S(2)}, u32[]{:S(2)}) collective-permute-start(bf16[704,128]{1,0:T(8,128)(2,1)S(1)} %collective-permute-done.3.refs_4_), channel_id=1, source_target_pairs={{0,4},{4,0},{8,12},{12,8},{16,20},{20,16},{24,28},{28,24},{1,5},{5... | collective-permute-start | bytes 540680 | tf_op jit(solution)/shard_map/ppermute | solution.py:19
  13.7 5.4 %collective-permute-start.2 = (bf16[704,128]{1,0:T(8,128)(2,1)S(1)}, bf16[704,128]{1,0:T(8,128)(2,1)S(1)}, u32[]{:S(2)}, u32[]{:S(2)}) collective-permute-start(bf16[704,128]{1,0:T(8,128)(2,1)S(1)} %collective-permute-done.1.refs_2_), channel_id=1, source_target_pairs={{0,4},{4,0},{8,12},{12,8},{16,20},{20,16},{24,28},{28,24},{1,5},{5... | collective-permute-start | bytes 540680 | tf_op jit(solution)/shard_map/ppermute | solution.py:19
  13.9 0.7 %copy-start = (s32[16]{0:T(128)S(1)}, s32[16]{0:T(128)}, u32[]{:S(2)}) copy-start(s32[16]{0:T(128)} %order_ref.5) | copy-start | bytes 196
  14.5 0.7 %copy-start.2 = (s32[1024]{0:T(1024)S(1)}, s32[1024]{0:T(1024)}, u32[]{:S(2)}) copy-start(s32[1024]{0:T(1024)} %param.12) | copy-start | bytes 12292
  15.2 0.7 %copy-start.3 = (bf16[128,16]{0,1:T(8,128)(2,1)S(1)}, bf16[128,16]{0,1:T(8,128)(2,1)}, u32[]{:S(2)}) copy-start(bf16[128,16]{0,1:T(8,128)(2,1)} %param.11) | copy-start | bytes 12292
  22.1 5.8 %collective-permute-start.7 = (f32[2,64,256]{2,1,0:T(8,128)S(1)}, f32[2,64,256]{2,1,0:T(8,128)S(1)}, u32[]{:S(2)}, u32[]{:S(2)}) collective-permute-start(f32[2,64,256]{2,1,0:T(8,128)S(1)} %give_sums.1), channel_id=1, source_target_pairs={{0,1},{1,0},{2,3},{3,2},{4,5},{5,4},{6,7},{7,6},{8,9},{9,8},{10,11... | collective-permute-start | bytes 393224 | tf_op jit(solution)/shard_map/ppermute | solution.py:19
  27.9 8.6 %collective-permute-start.8 = (f32[2,64,256]{2,1,0:T(8,128)S(1)}, f32[2,64,256]{2,1,0:T(8,128)S(1)}, u32[]{:S(2)}, u32[]{:S(2)}) collective-permute-start(f32[2,64,256]{2,1,0:T(8,128)S(1)} %add.6.refs_0_), channel_id=1, source_target_pairs={{0,2},{1,3},{2,0},{3,1},{4,6},{5,7},{6,4},{7,5},{8,10},{9,11},{10,... | collective-permute-start | bytes 393224 | tf_op jit(solution)/shard_map/ppermute | solution.py:19
  36.7 3.6 %collective-permute-start.9 = (f32[1,128]{1,0:T(1,128)S(1)}, f32[1,128]{1,0:T(1,128)S(1)}, u32[]{:S(2)}, u32[]{:S(2)}) collective-permute-start(f32[1,128]{1,0:T(1,128)S(1)} %row_losses.1), channel_id=1, source_target_pairs={{0,1},{1,0},{2,3},{3,2},{4,5},{5,4},{6,7},{7,6},{8,9},{9,8},{10,11... | collective-permute-start | bytes 1544 | tf_op jit(solution)/shard_map/ppermute | solution.py:19
where the time goes:
time: 41 us; the launch traced here: 40.8 us
  waiting for transfers between devices  18 us (44%)
  starting transfers between devices  9.91 us (24%)
  Pallas kernels  9.3 us (23%)
  local copies, waits for them, and re-layouts  2.03 us (5%)
  other arithmetic  1.49 us (4%)
    ppermute x10, waiting for transfers between devices, swap(): return lax.ppermute(x, axis, [(i, i ^ distance) for i in range(size)])  18 us
    ppermute x10, starting transfers between devices, swap(): return lax.ppermute(x, axis, [(i, i ^ distance) for i in range(size)])  9.91 us
    pallas_call x2, Pallas kernels, block_sums(): pl.pallas_call(functools.partial(block_kernel, (n_ctx, half, reach, key_w...  5.97 us
    pallas_call x1, Pallas kernels, per_device(): pl.pallas_call(functools.partial(prelude_kernel, (half, reach, copies)),...  3.14 us
    unnamed x8, local copies, waits for them, and re-layouts  2.03 us
    concatenate x1, other arithmetic, per_device(): packed = jnp.concatenate([latent_keys.T, index_keys], axis=0)  0.96 us
  transfers between devices with their start and end apart: 10, of which 6 were waited for; matrix products, arithmetic and copies ran while one was open for 0% of the time, Pallas kernels for 15%

commit v1 on v0

v1 whole, which is shorter than its diff:
```python
import functools
import math

import jax
import jax.numpy as jnp
from jax import lax
from jax.experimental import pallas as pl
from jax.experimental.pallas import tpu as pltpu
from jax.sharding import PartitionSpec as P


LANES = 128
score_scale = 192.0 ** (-0.5)
hidden = -1e30


def swap(x, axis, distance):
    size = lax.axis_size(axis)
    return lax.ppermute(x, axis, [(i, i ^ distance) for i in range(size)])


def window_masks(block, reach, half, seg_ref):
    table_rows = seg_ref.shape[0]
    first = block - reach // half
    row0 = lax.div(first + 2 * table_rows, 2) - table_rows
    pieces = []
    for k in range(reach // LANES + 2):
        row = jnp.clip(row0 + k, 0, table_rows - 1)
        pieces.append(seg_ref[pl.ds(row, 1), :].astype(jnp.float32))
    wide = jnp.concatenate(pieces, axis=1)
    width = wide.shape[1]
    moved = pltpu.roll(wide, width - half, 1)
    odd = lax.rem(first + 2 * table_rows, 2)
    wide = jnp.where(odd == 1, moved, wide)
    tail_seg = jnp.broadcast_to(wide[:, reach : reach + LANES], (half, LANES))
    head_seg = jnp.broadcast_to(wide[:, :LANES], (half, LANES))
    row_id = lax.broadcasted_iota(jnp.int32, (half, LANES), 0)
    lane_id = lax.broadcasted_iota(jnp.int32, (half, LANES), 1)
    query_seg = jnp.sum(jnp.where(row_id == lane_id, tail_seg, 0.0), axis=1, keepdims=True)
    in_tail = (lane_id <= row_id) & (lane_id < half)
    key_seg = jnp.concatenate(
        [jnp.where(in_tail, tail_seg, head_seg), jnp.broadcast_to(wide[:, LANES:reach], (half, reach - LANES))], axis=1
    )
    place = lax.broadcasted_iota(jnp.int32, (half, reach), 1)
    rows_full = lax.broadcasted_iota(jnp.int32, (half, reach), 0)
    tail_full = (place <= rows_full) & (place < half)
    position = first * half + place + jnp.where(tail_full, reach, 0)
    visible = (key_seg == query_seg) & (position >= 0)
    return in_tail, visible


def ring_fold(own_low, main, tail):
    low = jnp.where(own_low, main[:, :LANES], tail)
    return jnp.concatenate([low, main[:, LANES:]], axis=1)


def own_block(keep):
    bit = lax.axis_index("head") & 1
    return bit if keep else 1 - bit


def block_rows(keep, half):
    return pl.ds(pl.multiple_of(own_block(keep) * half, half), half)


def pack_kernel(latent_hbm, index_hbm, out_ref, sems):
    width = latent_hbm.shape[0]
    copies = [
        pltpu.make_async_copy(latent_hbm, out_ref.at[:width, :], sems.at[0]),
        pltpu.make_async_copy(index_hbm, out_ref.at[width:, :], sems.at[1]),
    ]
    for copy in copies:
        copy.start()
    for copy in copies:
        copy.wait()


def prelude_kernel(sizes, order_hbm, seg_hbm, weight_hbm, query_hbm, index_query_hbm,
                   bias_ref, query_ref, keep_ref, give_ref, order_ref, seg_ref, weight_ref, sems):
    half, reach, copies = sizes
    rows = query_ref.shape[0]
    width = index_query_hbm.shape[1]
    small = [
        pltpu.make_async_copy(order_hbm, order_ref, sems.at[0]),
        pltpu.make_async_copy(seg_hbm, seg_ref, sems.at[1]),
        pltpu.make_async_copy(weight_hbm, weight_ref, sems.at[2]),
    ]
    large = [
        pltpu.make_async_copy(index_query_hbm.at[block_rows(False, half), :], give_ref.at[:, :width], sems.at[3]),
        pltpu.make_async_copy(index_query_hbm.at[block_rows(True, half), :], keep_ref.at[:, :width], sems.at[4]),
    ]
    for c in range(copies):
        part = slice(c * (rows // copies), (c + 1) * (rows // copies))
        large.append(pltpu.make_async_copy(query_hbm.at[part, :], query_ref.at[part, :], sems.at[5 + c]))
    for copy in small + large:
        copy.start()
    for copy in small:
        copy.wait()
    me = lax.axis_index("ctx")
    for i in range(2):
        _, visible = window_masks(order_ref[me * 2 + i], reach, half, seg_ref)
        bias_ref[i] = jnp.where(visible, 0.0, hidden)
    gains = jnp.transpose(weight_ref[...].astype(jnp.float32), (1, 0))
    gains = jnp.concatenate([gains, jnp.zeros((rows, LANES - gains.shape[1]), gains.dtype)], axis=1)
    gains = gains.astype(keep_ref.dtype)
    first_kept = own_block(True) == 0
    keep_ref[:, width:] = jnp.where(first_kept, gains[:half], gains[half:])
    give_ref[:, width:] = jnp.where(first_kept, gains[half:], gains[:half])
    for copy in large:
        copy.wait()


def block_kernel(sizes, keep, order_ref, seg_ref, bias_ref, query_ref, *refs):
    n_ctx, half, reach, key_width, idim = sizes
    n_index = 2 if keep else 0
    index_query_refs, refs = refs[:n_index], refs[n_index:]
    piece_refs, out_refs = refs[:n_ctx], refs[n_ctx : n_ctx + 1 + (n_index > 0)]
    refs = refs[n_ctx + len(out_refs) :]
    stack_ref, main_ref, tail_ref, index_main, index_tail, raw_ref, index_raw, inverse_ref = refs
    key_pad = main_ref.shape[1]
    me = lax.axis_index("ctx")
    mine = own_block(keep)
    rows_here = block_rows(keep, half)
    for s in range(n_ctx):
        stack_ref[me ^ s] = piece_refs[s][...]
    for slot in range(order_ref.shape[0]):
        inverse_ref[order_ref[slot]] = slot
    block = order_ref[me * 2 + mine]
    reach_blocks = reach // half
    first = block - reach_blocks
    oldest = jnp.maximum(first, 0) * half + half - 1
    needed = (first >= 0) & (seg_ref[block * half] == seg_ref[oldest])
    order = [reach_blocks] + list(range(1, reach_blocks)) + [0]
    slots = [inverse_ref[jnp.maximum(first + w, 0)] for w in order]

    left = lax.broadcasted_iota(jnp.int32, (key_width, LANES), 1) < half

    def keys_into(target_ref, c, lanes):
        halves = []
        for side in (0, 1):
            slot = slots[min(2 * c + side, reach_blocks)]
            tile = stack_ref[slot >> 1, :key_width, :].astype(jnp.float32)
            turned = pltpu.roll(tile, half, 1)
            halves.append(jnp.where((slot & 1) == side, tile, turned))
        both = jnp.where(left, halves[0], halves[1]).astype(target_ref.dtype)
        target_ref[0, :key_width, lanes] = both
        target_ref[1, key_pad - key_width :, lanes] = both

    def index_keys_into(target_ref, w, at):
        start = pl.multiple_of(key_width + (slots[w] & 1) * half, half)
        target_ref[at : at + half, :] = stack_ref[slots[w] >> 1, pl.ds(start, half), :]

    main_ref[0, key_width:, :] = jnp.zeros((key_pad - key_width, reach), main_ref.dtype)
    main_ref[1, : key_pad - key_width, :] = jnp.zeros((key_pad - key_width, reach), main_ref.dtype)
    for c in range(reach // LANES):
        keys_into(main_ref, c, slice(c * LANES, (c + 1) * LANES))

    row_id = lax.broadcasted_iota(jnp.int32, (half, LANES), 0)
    lane_id = lax.broadcasted_iota(jnp.int32, (half, LANES), 1)
    own_low = (lane_id <= row_id) | (lane_id >= half) | jnp.logical_not(needed)
    bias = bias_ref[mine]

    heads = query_ref.shape[1] // key_width
    stacked_queries = []
    for parity in (0, 1):
        starts = [g * 2 * key_width + parity * (2 * key_width - key_pad) for g in range(heads // 2)]
        stacked_queries.append(lambda starts=starts: jnp.concatenate([query_ref[rows_here, at : at + key_pad] for at in starts], axis=0))

    def index_lhs(ref):
        return jnp.concatenate([ref[:, j * idim : (j + 1) * idim] for j in range(ref.shape[1] // idim - 1)], axis=0)

    if keep:
        for w in range(reach_blocks):
            index_keys_into(index_main, w, w * half)

    @pl.when(needed)
    def _():
        tail_ref[0, key_width:, :] = jnp.zeros((key_pad - key_width, LANES), tail_ref.dtype)
        tail_ref[1, : key_pad - key_width, :] = jnp.zeros((key_pad - key_width, LANES), tail_ref.dtype)
        keys_into(tail_ref, reach // LANES, slice(0, LANES))
        for parity in (0, 1):
            raw_ref[parity] = lax.dot_general(
                stacked_queries[parity](), tail_ref[parity], (((1,), (0,)), ((), ())), preferred_element_type=jnp.float32
            )
        if keep:
            index_keys_into(index_tail, reach_blocks, 0)
            index_tail[half:, :] = jnp.zeros((LANES - half, idim), index_tail.dtype)
            for k, ref in enumerate(index_query_refs):
                index_raw[k] = lax.dot_general(
                    index_lhs(ref), index_tail[...], (((1,), (1,)), ((), ())), preferred_element_type=jnp.float32
                )

    total = jnp.zeros((half, reach), jnp.float32)
    for parity in (0, 1):
        raw = lax.dot_general(
            stacked_queries[parity](), main_ref[parity], (((1,), (0,)), ((), ())), preferred_element_type=jnp.float32
        )
        for g in range(heads // 2):
            here = slice(g * half, (g + 1) * half)
            scores = ring_fold(own_low, raw[here, :], raw_ref[parity, here, :]) + bias
            row_max = jnp.max(scores, axis=1, keepdims=True)
            powers = jnp.exp2((scores - row_max) * (score_scale * math.log2(math.e)))
            share = 1.0 / jnp.sum(powers, axis=1, keepdims=True)
            total = total + powers * share
    out_refs[0][...] = total

    if keep:
        total = jnp.zeros((half, reach), jnp.float32)
        for k, ref in enumerate(index_query_refs):
            lhs = index_lhs(ref)
            dots = lax.dot_general(lhs, index_main[...], (((1,), (1,)), ((), ())), preferred_element_type=jnp.float32)
            gains = ref[:, lhs.shape[0] // half * idim :].astype(jnp.float32)
            for j in range(lhs.shape[0] // half):
                here = slice(j * half, (j + 1) * half)
                folded = ring_fold(own_low, dots[here, :], index_raw[k, here, :])
                total = total + gains[:, j : j + 1] * jnp.maximum(folded, 0.0)
        out_refs[1][...] = jnp.where(bias == 0.0, total, 0.0)


def loss_kernel(sizes, bias_ref, *refs):
    half, total_heads = sizes
    value_refs, out_ref = refs[:-1], refs[-1]
    mine = own_block(True)
    visible = bias_ref[mine] == 0.0
    target = functools.reduce(jnp.add, [ref[0] for ref in value_refs]) * (1.0 / total_heads)
    index_score = functools.reduce(jnp.add, [ref[1] for ref in value_refs])
    masked = jnp.where(visible, index_score, hidden)
    row_max = jnp.max(masked, axis=1, keepdims=True)
    exp_sum = jnp.sum(jnp.where(visible, jnp.exp(masked - row_max), 0.0), axis=1, keepdims=True)
    positive = target > 0.0
    logs = jnp.log(jnp.where(positive, target, 1.0))
    entropy_sum = jnp.sum(jnp.where(positive, target * logs, 0.0), axis=1, keepdims=True)
    cross_sum = jnp.sum(jnp.where(visible, target * index_score, 0.0), axis=1, keepdims=True)
    target_sum = jnp.sum(target, axis=1, keepdims=True)
    column = entropy_sum - cross_sum + (row_max + jnp.log(exp_sum)) * target_sum
    rows = out_ref.shape[1]
    row_id = lax.broadcasted_iota(jnp.int32, (half, rows), 0)
    lane_id = lax.broadcasted_iota(jnp.int32, (half, rows), 1)
    out_ref[...] = jnp.sum(jnp.where(row_id + mine * half == lane_id, column, 0.0), axis=0, keepdims=True)


def per_device(
    latent_keys, index_keys, main_query, index_query, index_weight, segment_ids, block_order
):
    n_ctx, n_head = lax.axis_size("ctx"), lax.axis_size("head")
    rows, key_width = latent_keys.shape
    idim = index_keys.shape[1]
    seq_len = segment_ids.shape[0]
    half = seq_len // block_order.shape[0]
    reach = seq_len // 4
    heads = main_query.shape[1] // key_width
    key_pad = -(-key_width // LANES) * LANES
    vmem = pl.BlockSpec(memory_space=pltpu.VMEM)
    smem = pl.BlockSpec(memory_space=pltpu.SMEM)
    hbm = pl.BlockSpec(memory_space=pltpu.HBM)
    index_heads = index_weight.shape[1]

    def far(x):
        return pltpu.with_memory_space_constraint(x, pltpu.HBM)

    packed = pl.pallas_call(
        pack_kernel,
        out_shape=jax.ShapeDtypeStruct((key_width + idim, rows), latent_keys.dtype),
        in_specs=[hbm, hbm],
        out_specs=vmem,
        scratch_shapes=[pltpu.SemaphoreType.DMA((2,))],
        compiler_params=pltpu.CompilerParams(vmem_limit_bytes=2 << 20),
        name="pack",
    )(far(latent_keys.T), far(index_keys))
    own_core = [packed]
    for s in reversed(range(1, n_ctx // 2)):
        own_core.append(swap(packed, "ctx", 2 * s))
    own_core = [packed] + own_core[:0:-1]
    pieces = []
    for piece in own_core:
        pieces += [piece, swap(piece, "ctx", 1)]
    seg_table = segment_ids.reshape(seq_len // LANES, LANES)

    copies = 8
    index_row = (half, index_query.shape[1] + LANES)
    bias, near_query, keep_query, give_query = pl.pallas_call(
        functools.partial(prelude_kernel, (half, reach, copies)),
        out_shape=(
            jax.ShapeDtypeStruct((2, half, reach), jnp.float32),
            jax.ShapeDtypeStruct(main_query.shape, main_query.dtype),
            jax.ShapeDtypeStruct(index_row, index_query.dtype),
            jax.ShapeDtypeStruct(index_row, index_query.dtype),
        ),
        in_specs=[hbm] * 5,
        out_specs=(vmem,) * 4,
        scratch_shapes=[
            pltpu.SMEM(block_order.shape, jnp.int32),
            pltpu.VMEM(seg_table.shape, jnp.int32),
            pltpu.VMEM((index_heads, rows), index_weight.dtype),
            pltpu.SemaphoreType.DMA((copies + 5,)),
        ],
        compiler_params=pltpu.CompilerParams(vmem_limit_bytes=12 << 20),
        cost_estimate=pl.CostEstimate(flops=1 << 20, bytes_accessed=10 << 20, transcendentals=0),
        name="prelude",
    )(far(block_order), far(seg_table), far(index_weight.T), far(main_query), far(index_query))
    taken_query = swap(give_query, "head", 1)

    def block_sums(keep):
        sums = jax.ShapeDtypeStruct((half, reach), jnp.float32)
        index_queries = [keep_query, taken_query] if keep else []
        return pl.pallas_call(
            functools.partial(block_kernel, (n_ctx, half, reach, key_width, idim), keep),
            out_shape=(sums, sums) if keep else (sums,),
            in_specs=[smem, smem] + [vmem] * (2 + len(index_queries) + n_ctx),
            out_specs=(vmem, vmem) if keep else (vmem,),
            scratch_shapes=[
                pltpu.VMEM((n_ctx, key_width + idim, LANES), jnp.bfloat16),
                pltpu.VMEM((2, key_pad, reach), jnp.bfloat16),
                pltpu.VMEM((2, key_pad, LANES), jnp.bfloat16),
                pltpu.VMEM((reach, idim), jnp.bfloat16),
                pltpu.VMEM((LANES, idim), jnp.bfloat16),
                pltpu.VMEM((2, heads // 2 * half, LANES), jnp.float32),
                pltpu.VMEM((2, index_heads * half, LANES), jnp.float32),
                pltpu.SMEM((block_order.shape[0],), jnp.int32),
            ],
            compiler_params=pltpu.CompilerParams(vmem_limit_bytes=28 << 20),
            cost_estimate=pl.CostEstimate(
                flops=2 * half * reach * heads * key_pad, bytes_accessed=4 << 20, transcendentals=0
            ),
            name="keep_sums" if keep else "give_sums",
        )(block_order, segment_ids, bias, near_query, *index_queries, *pieces)

    given = block_sums(False)[0]
    kept, index_sums = block_sums(True)
    value = jnp.stack([kept + swap(given, "head", 1), index_sums])
    distances = [1 << k for k in range(1, n_head.bit_length() - 1)]
    for distance in distances[:-1]:
        value = value + swap(value, "head", distance)
    values = [value] + [swap(value, "head", distance) for distance in distances[-1:]]
    loss = pl.pallas_call(
        functools.partial(loss_kernel, (half, heads * n_head)),
        out_shape=jax.ShapeDtypeStruct((1, rows), jnp.float32),
        in_specs=[vmem] * (1 + len(values)),
        out_specs=vmem,
        compiler_params=pltpu.CompilerParams(vmem_limit_bytes=8 << 20),
        name="row_losses",
    )(bias, *values)
    return (loss + swap(loss, "head", 1)).reshape(rows)


def solution(mesh):
    in_specs = (
        P("ctx", None),
        P("ctx", None),
        P("ctx", "head"),
        P("ctx", "head"),
        P("ctx", "head"),
        P(),
        P(),
    )
    return jax.shard_map(per_device, mesh=mesh, in_specs=in_specs, out_specs=P("ctx"), check_vma=False)
```

time: 41 us -> 36.2 us (0.88)
  waiting for transfers between devices: 18 us -> 14.3 us
  starting transfers between devices: 9.91 us -> 12.1 us
  local copies, waits for them, and re-layouts: 2.03 us -> 0.01 us
  other arithmetic: 1.49 us -> 0.54 us
    ppermute x10 -> x11, waiting for transfers between devices: 18 us -> 14.3 us  [swap(): return lax.ppermute(x, axis, [(i, i ^ distance) for i in range(size)])]
    ppermute x10 -> x11, starting transfers between devices: 9.91 us -> 12.1 us  [swap(): return lax.ppermute(x, axis, [(i, i ^ distance) for i in range(size)])]
    unnamed x8 -> x4, local copies, waits for them, and re-layouts: 2.03 us -> 0.01 us
    pallas_call x0 -> x1, Pallas kernels: none -> 0.96 us  [per_device(): pl.pallas_call(pack_kernel, out_shape=jax.ShapeDtypeStruct((key_width + i...]
    concatenate x1 -> x0, other arithmetic: 0.96 us -> none  [per_device(): packed = jnp.concatenate([latent_keys.T, index_keys], axis=0)]
    pallas_call x2, Pallas kernels: 5.97 us -> 5.28 us  [block_sums(): pl.pallas_call(functools.partial(block_kernel, (n_ctx, half, reach, key_w...]
    pallas_call x1, Pallas kernels: 3.14 us -> 2.61 us  [per_device(): pl.pallas_call(functools.partial(prelude_kernel, (half, reach, copies)),...]
  transfers between devices with their start and end apart: 10 -> 11, of which waited for: 6 -> 5; matrix products, arithmetic and copies ran while one was open for 0% -> 0% of each run, Pallas kernels for 15% -> 22%
where the time goes in v1:
time: 36.2 us; the launch traced here: 36 us
  waiting for transfers between devices  14.3 us (40%)
  starting transfers between devices  12.1 us (33%)
  Pallas kernels  9.05 us (25%)
  other arithmetic  0.54 us (1%)
    ppermute x11, waiting for transfers between devices, swap(): return lax.ppermute(x, axis, [(i, i ^ distance) for i in range(size)])  14.3 us
    ppermute x11, starting transfers between devices, swap(): return lax.ppermute(x, axis, [(i, i ^ distance) for i in range(size)])  12.1 us
    pallas_call x2, Pallas kernels, block_sums(): pl.pallas_call(functools.partial(block_kernel, (n_ctx, half, reach, key_w...  5.28 us
    pallas_call x1, Pallas kernels, per_device(): pl.pallas_call(functools.partial(prelude_kernel, (half, reach, copies)),...  2.61 us
    pallas_call x1, Pallas kernels, per_device(): pl.pallas_call(pack_kernel, out_shape=jax.ShapeDtypeStruct((key_width + i...  0.96 us
  transfers between devices with their start and end apart: 11, of which 5 were waited for; matrix products, arithmetic and copies ran while one was open for 0% of the time, Pallas kernels for 22%

profile of v1, /device:TPU:0, one launch (start us, length us, event | category | flops | bytes accessed | tf_op | source)
XLA Modules:
  0.0 36.0 jit_solution(12166748301525692511)
XLA Ops:
  0.0 0.0 copy-start.1
  0.0 0.0 copy-start
  0.0 1.0 %pack.1.refs_2_.refs_0_ = bf16[704,128]{1,0:T(8,128)(2,1)S(1)} custom-call(bf16[576,128]{1,0:T(8,128)(2,1)} %bitcast.10, bf16[128,128]{1,0:T(8,128)(2,1)} %index_hbm.1), custom_call_target="tpu_custom_call" | custom-call | tf_op jit(solution)/shard_map/pack/pallas_call | solution.py:261
  1.0 3.0 %collective-permute-start.2 = (bf16[704,128]{1,0:T(8,128)(2,1)S(1)}, bf16[704,128]{1,0:T(8,128)(2,1)S(1)}, u32[]{:S(2)}, u32[]{:S(2)}) collective-permute-start(bf16[704,128]{1,0:T(8,128)(2,1)S(1)} %pack.1.refs_2_.refs_0_), channel_id=1, source_target_pairs={{0,8},{4,12},{8,0},{12,4},{16,24},{20,28},{24,16},{28,20},{1,9},{5... | collective-permute-start | bytes 540680 | tf_op jit(solution)/shard_map/ppermute | solution.py:19
  4.0 1.5 %collective-permute-start.4 = (bf16[704,128]{1,0:T(8,128)(2,1)S(1)}, bf16[704,128]{1,0:T(8,128)(2,1)S(1)}, u32[]{:S(2)}, u32[]{:S(2)}) collective-permute-start(bf16[704,128]{1,0:T(8,128)(2,1)S(1)} %pack.1.refs_2_.refs_0_), channel_id=1, source_target_pairs={{0,16},{4,20},{8,24},{12,28},{16,0},{20,4},{24,8},{28,12},{1,17},{... | collective-permute-start | bytes 540680 | tf_op jit(solution)/shard_map/ppermute | solution.py:19
  5.5 0.0 collective-permute-start.6
  5.5 2.6 %prelude.1 = (f32[2,64,256]{2,1,0:T(8,128)S(1)}, bf16[128,18432]{1,0:T(8,128)(2,1)S(1)}, bf16[64,2176]{1,0:T(8,128)(2,1)S(1)}, bf16[64,2176]{1,0:T(8,128)(2,1)S(1)}) custom-call(s32[16]{0:T(128)} %order_ref.3, s32[8,128]{1,0:T(8,128)} %bitcast.9, bf16[16,128]{1,0:T(8,128)(2,1)} %bitcast.11, bf16[128,18432]{1,0:T(8,128)(2,1)} %query_hbm.1, ...), custom_call_target="tpu_custom_call" | custom-call | flops 1048576 | bytes 10485760 | tf_op jit(solution)/shard_map/prelude/pallas_call | solution.py:281
  8.2 2.1 %collective-permute-start = (bf16[64,2176]{1,0:T(8,128)(2,1)S(1)}, bf16[64,2176]{1,0:T(8,128)(2,1)S(1)}, u32[]{:S(2)}, u32[]{:S(2)}) collective-permute-start(bf16[64,2176]{1,0:T(8,128)(2,1)S(1)} %get-tuple-element.14), channel_id=1, source_target_pairs={{0,1},{1,0},{2,3},{3,2},{4,5},{5,4},{6,7},{7,6},{8,9},{9,8},{10,11... | collective-permute-start | bytes 835592 | tf_op jit(solution)/shard_map/ppermute | solution.py:19
  10.3 0.0 collective-permute-start.1
  10.3 0.0 collective-permute-done.2.refs_4_.refs_2_
  10.3 0.5 %collective-permute-start.3 = (bf16[704,128]{1,0:T(8,128)(2,1)S(1)}, bf16[704,128]{1,0:T(8,128)(2,1)S(1)}, u32[]{:S(2)}, u32[]{:S(2)}) collective-permute-start(bf16[704,128]{1,0:T(8,128)(2,1)S(1)} %collective-permute-done.2.refs_4_.refs_2_), channel_id=1, source_target_pairs={{0,4},{4,0},{8,12},{12,8},{16,20},{20,16},{24,28},{28,24},{1,5},{5... | collective-permute-start | bytes 540680 | tf_op jit(solution)/shard_map/ppermute | solution.py:19
  10.8 3.1 %collective-permute-done.4.refs_6_.refs_4_ = bf16[704,128]{1,0:T(8,128)(2,1)S(1)} collective-permute-done((bf16[704,128]{1,0:T(8,128)(2,1)S(1)}, bf16[704,128]{1,0:T(8,128)(2,1)S(1)}, u32[]{:S(2)}, u32[]{:S(2)}) %collective-permute-start.4) | collective-permute-done | bytes 180256 | tf_op jit(solution)/shard_map/ppermute | solution.py:19
  13.9 0.0 collective-permute-start.5
  13.9 0.0 collective-permute-done.6.refs_8_.refs_6_
  13.9 0.5 %collective-permute-start.7 = (bf16[704,128]{1,0:T(8,128)(2,1)S(1)}, bf16[704,128]{1,0:T(8,128)(2,1)S(1)}, u32[]{:S(2)}, u32[]{:S(2)}) collective-permute-start(bf16[704,128]{1,0:T(8,128)(2,1)S(1)} %collective-permute-done.6.refs_8_.refs_6_), channel_id=1, source_target_pairs={{0,4},{4,0},{8,12},{12,8},{16,20},{20,16},{24,28},{28,24},{1,5},{5... | collective-permute-start | bytes 540680 | tf_op jit(solution)/shard_map/ppermute | solution.py:19
  14.4 0.0 collective-permute-done.1.refs_3_.refs_1_
  14.4 0.0 collective-permute-done.3.refs_5_.refs_3_
  14.4 0.9 %collective-permute-done.5.refs_7_.refs_5_ = bf16[704,128]{1,0:T(8,128)(2,1)S(1)} collective-permute-done((bf16[704,128]{1,0:T(8,128)(2,1)S(1)}, bf16[704,128]{1,0:T(8,128)(2,1)S(1)}, u32[]{:S(2)}, u32[]{:S(2)}) %collective-permute-start.5) | collective-permute-done | bytes 180256 | tf_op jit(solution)/shard_map/ppermute | solution.py:19
  15.3 0.3 collective-permute-done.7.refs_9_.refs_7_
  15.6 0.0 copy-done.1
  15.6 0.0 copy-done
  15.6 2.4 %give_sums.1 = f32[64,256]{1,0:T(8,128)S(1)} custom-call(s32[16]{0:T(128)S(1)} %copy-done.1, s32[1024]{0:T(1024)S(1)} %copy-done, f32[2,64,256]{2,1,0:T(8,128)S(1)} %get-tuple-element.11.bias_ref, bf16[128,18432]{1,0:T(8,128)(2,1)S(1)} %get-tuple-element.12.query_ref, bf16[704,128]{1,0:T(8,128)(2,1)S(1)} %pack.1.refs_2_.refs_0_, ...), custom_call_target="tpu_custom_call" | custom-call | flops 671088640 | bytes 4194304 | tf_op jit(solution)/shard_map/give_sums/pallas_call | solution.py:306
  18.0 1.6 %collective-permute-start.8 = (f32[64,256]{1,0:T(8,128)S(1)}, f32[64,256]{1,0:T(8,128)S(1)}, u32[]{:S(2)}, u32[]{:S(2)}) collective-permute-start(f32[64,256]{1,0:T(8,128)S(1)} %give_sums.1), channel_id=1, source_target_pairs={{0,1},{1,0},{2,3},{3,2},{4,5},{5,4},{6,7},{7,6},{8,9},{9,8},{10,11... | collective-permute-start | bytes 196616 | tf_op jit(solution)/shard_map/ppermute | solution.py:19
  19.6 0.0 collective-permute-done.refs_1_
  19.6 2.9 %keep_sums.1 = (f32[64,256]{1,0:T(8,128)S(1)}, f32[64,256]{1,0:T(8,128)S(1)}) custom-call(s32[16]{0:T(128)S(1)} %copy-done.1, s32[1024]{0:T(1024)S(1)} %copy-done, f32[2,64,256]{2,1,0:T(8,128)S(1)} %get-tuple-element.11.bias_ref, bf16[128,18432]{1,0:T(8,128)(2,1)S(1)} %get-tuple-element.12.query_ref, bf16[64,2176]{1,0:T(8,128)(2,1)S(1)} %get-tuple-element.13.refs_0_, ...), custom_call_target="tpu_custom_call" | custom-call | flops 671088640 | bytes 4194304 | tf_op jit(solution)/shard_map/keep_sums/pallas_call | solution.py:306
  22.5 0.0 collective-permute-done.8
  22.6 2.7 %collective-permute-start.9 = (f32[2,64,256]{2,1,0:T(8,128)S(1)}, f32[2,64,256]{2,1,0:T(8,128)S(1)}, u32[]{:S(2)}, u32[]{:S(2)}) collective-permute-start(f32[2,64,256]{2,1,0:T(8,128)S(1)} %pad_maximum_fusion.refs_0_), channel_id=1, source_target_pairs={{0,2},{1,3},{2,0},{3,1},{4,6},{5,7},{6,4},{7,5},{8,10},{9,11},{10,... | collective-permute-start | bytes 393224 | tf_op jit(solution)/shard_map/ppermute | solution.py:19
  25.2 6.5 %collective-permute-done.9.refs_1_ = f32[2,64,256]{2,1,0:T(8,128)S(1)} collective-permute-done((f32[2,64,256]{2,1,0:T(8,128)S(1)}, f32[2,64,256]{2,1,0:T(8,128)S(1)}, u32[]{:S(2)}, u32[]{:S(2)}) %collective-permute-start.9) | collective-permute-done | bytes 131104 | tf_op jit(solution)/shard_map/ppermute | solution.py:19
  31.7 0.2 row_losses.1
  31.9 0.1 collective-permute-start.10
  31.9 3.6 %collective-permute-done.10 = f32[1,128]{1,0:T(1,128)S(1)} collective-permute-done((f32[1,128]{1,0:T(1,128)S(1)}, f32[1,128]{1,0:T(1,128)S(1)}, u32[]{:S(2)}, u32[]{:S(2)}) %collective-permute-start.10) | collective-permute-done | bytes 544 | tf_op jit(solution)/shard_map/ppermute | solution.py:19
  35.5 0.5 %add_bitcast_fusion.1 = f32[128]{0:T(128)} fusion(f32[1,128]{1,0:T(1,128)S(1)} %row_losses.1, f32[1,128]{1,0:T(1,128)S(1)} %collective-permute-done.10), kind=kLoop, calls=%fused_computation.2 | loop fusion | flops 128 | bytes 1536 | tf_op jit(solution)/shard_map/reshape | solution.py:343
  (2 shorter events, 0.0 us)
Async XLA Ops:
  0.0 15.6 %copy-start.1 = (s32[16]{0:T(128)S(1)}, s32[16]{0:T(128)}, u32[]{:S(2)}) copy-start(s32[16]{0:T(128)} %order_ref.3) | copy-start | bytes 196
  0.0 15.6 %copy-start = (s32[1024]{0:T(1024)S(1)}, s32[1024]{0:T(1024)}, u32[]{:S(2)}) copy-start(s32[1024]{0:T(1024)} %seg_ref.3) | copy-start | bytes 12292
  1.0 9.3 %collective-permute-start.2 = (bf16[704,128]{1,0:T(8,128)(2,1)S(1)}, bf16[704,128]{1,0:T(8,128)(2,1)S(1)}, u32[]{:S(2)}, u32[]{:S(2)}) collective-permute-start(bf16[704,128]{1,0:T(8,128)(2,1)S(1)} %pack.1.refs_2_.refs_0_), channel_id=1, source_target_pairs={{0,8},{4,12},{8,0},{12,4},{16,24},{20,28},{24,16},{28,20},{1,9},{5... | collective-permute-start | bytes 540680 | tf_op jit(solution)/shard_map/ppermute | solution.py:19
  4.0 9.9 %collective-permute-start.4 = (bf16[704,128]{1,0:T(8,128)(2,1)S(1)}, bf16[704,128]{1,0:T(8,128)(2,1)S(1)}, u32[]{:S(2)}, u32[]{:S(2)}) collective-permute-start(bf16[704,128]{1,0:T(8,128)(2,1)S(1)} %pack.1.refs_2_.refs_0_), channel_id=1, source_target_pairs={{0,16},{4,20},{8,24},{12,28},{16,0},{20,4},{24,8},{28,12},{1,17},{... | collective-permute-start | bytes 540680 | tf_op jit(solution)/shard_map/ppermute | solution.py:19
  5.5 8.4 %collective-permute-start.6 = (bf16[704,128]{1,0:T(8,128)(2,1)S(1)}, bf16[704,128]{1,0:T(8,128)(2,1)S(1)}, u32[]{:S(2)}, u32[]{:S(2)}) collective-permute-start(bf16[704,128]{1,0:T(8,128)(2,1)S(1)} %pack.1.refs_2_.refs_0_), channel_id=1, source_target_pairs={{0,24},{4,28},{8,16},{12,20},{16,8},{20,12},{24,0},{28,4},{1,25},{... | collective-permute-start | bytes 540680 | tf_op jit(solution)/shard_map/ppermute | solution.py:19
  8.2 11.5 %collective-permute-start = (bf16[64,2176]{1,0:T(8,128)(2,1)S(1)}, bf16[64,2176]{1,0:T(8,128)(2,1)S(1)}, u32[]{:S(2)}, u32[]{:S(2)}) collective-permute-start(bf16[64,2176]{1,0:T(8,128)(2,1)S(1)} %get-tuple-element.14), channel_id=1, source_target_pairs={{0,1},{1,0},{2,3},{3,2},{4,5},{5,4},{6,7},{7,6},{8,9},{9,8},{10,11... | collective-permute-start | bytes 835592 | tf_op jit(solution)/shard_map/ppermute | solution.py:19
  10.3 4.1 %collective-permute-start.1 = (bf16[704,128]{1,0:T(8,128)(2,1)S(1)}, bf16[704,128]{1,0:T(8,128)(2,1)S(1)}, u32[]{:S(2)}, u32[]{:S(2)}) collective-permute-start(bf16[704,128]{1,0:T(8,128)(2,1)S(1)} %pack.1.refs_2_.refs_0_), channel_id=1, source_target_pairs={{0,4},{4,0},{8,12},{12,8},{16,20},{20,16},{24,28},{28,24},{1,5},{5... | collective-permute-start | bytes 540680 | tf_op jit(solution)/shard_map/ppermute | solution.py:19
  10.3 4.1 %collective-permute-start.3 = (bf16[704,128]{1,0:T(8,128)(2,1)S(1)}, bf16[704,128]{1,0:T(8,128)(2,1)S(1)}, u32[]{:S(2)}, u32[]{:S(2)}) collective-permute-start(bf16[704,128]{1,0:T(8,128)(2,1)S(1)} %collective-permute-done.2.refs_4_.refs_2_), channel_id=1, source_target_pairs={{0,4},{4,0},{8,12},{12,8},{16,20},{20,16},{24,28},{28,24},{1,5},{5... | collective-permute-start | bytes 540680 | tf_op jit(solution)/shard_map/ppermute | solution.py:19
  13.9 1.4 %collective-permute-start.5 = (bf16[704,128]{1,0:T(8,128)(2,1)S(1)}, bf16[704,128]{1,0:T(8,128)(2,1)S(1)}, u32[]{:S(2)}, u32[]{:S(2)}) collective-permute-start(bf16[704,128]{1,0:T(8,128)(2,1)S(1)} %collective-permute-done.4.refs_6_.refs_4_), channel_id=1, source_target_pairs={{0,4},{4,0},{8,12},{12,8},{16,20},{20,16},{24,28},{28,24},{1,5},{5... | collective-permute-start | bytes 540680 | tf_op jit(solution)/shard_map/ppermute | solution.py:19
  13.9 1.7 %collective-permute-start.7 = (bf16[704,128]{1,0:T(8,128)(2,1)S(1)}, bf16[704,128]{1,0:T(8,128)(2,1)S(1)}, u32[]{:S(2)}, u32[]{:S(2)}) collective-permute-start(bf16[704,128]{1,0:T(8,128)(2,1)S(1)} %collective-permute-done.6.refs_8_.refs_6_), channel_id=1, source_target_pairs={{0,4},{4,0},{8,12},{12,8},{16,20},{20,16},{24,28},{28,24},{1,5},{5... | collective-permute-start | bytes 540680 | tf_op jit(solution)/shard_map/ppermute | solution.py:19
  18.0 4.5 %collective-permute-start.8 = (f32[64,256]{1,0:T(8,128)S(1)}, f32[64,256]{1,0:T(8,128)S(1)}, u32[]{:S(2)}, u32[]{:S(2)}) collective-permute-start(f32[64,256]{1,0:T(8,128)S(1)} %give_sums.1), channel_id=1, source_target_pairs={{0,1},{1,0},{2,3},{3,2},{4,5},{5,4},{6,7},{7,6},{8,9},{9,8},{10,11... | collective-permute-start | bytes 196616 | tf_op jit(solution)/shard_map/ppermute | solution.py:19
  22.6 9.1 %collective-permute-start.9 = (f32[2,64,256]{2,1,0:T(8,128)S(1)}, f32[2,64,256]{2,1,0:T(8,128)S(1)}, u32[]{:S(2)}, u32[]{:S(2)}) collective-permute-start(f32[2,64,256]{2,1,0:T(8,128)S(1)} %pad_maximum_fusion.refs_0_), channel_id=1, source_target_pairs={{0,2},{1,3},{2,0},{3,1},{4,6},{5,7},{6,4},{7,5},{8,10},{9,11},{10,... | collective-permute-start | bytes 393224 | tf_op jit(solution)/shard_map/ppermute | solution.py:19
  31.9 3.6 %collective-permute-start.10 = (f32[1,128]{1,0:T(1,128)S(1)}, f32[1,128]{1,0:T(1,128)S(1)}, u32[]{:S(2)}, u32[]{:S(2)}) collective-permute-start(f32[1,128]{1,0:T(1,128)S(1)} %row_losses.1), channel_id=1, source_target_pairs={{0,1},{1,0},{2,3},{3,2},{4,5},{5,4},{6,7},{7,6},{8,9},{9,8},{10,11... | collective-permute-start | bytes 1544 | tf_op jit(solution)/shard_map/ppermute | solution.py:19

commit v2 on v1

--- a/solution.py
+++ b/solution.py
@@ -63,16 +63,28 @@
     return pl.ds(pl.multiple_of(own_block(keep) * half, half), half)
 
 
-def pack_kernel(latent_hbm, index_hbm, out_ref, sems):
+def pack_kernel(latent_hbm, index_hbm, out_ref, part_ref, sems):
     width = latent_hbm.shape[0]
-    copies = [
+    part = part_ref.shape[0]
+    bit = own_block(True)
+    whole = [
         pltpu.make_async_copy(latent_hbm, out_ref.at[:width, :], sems.at[0]),
         pltpu.make_async_copy(index_hbm, out_ref.at[width:, :], sems.at[1]),
     ]
-    for copy in copies:
-        copy.start()
-    for copy in copies:
-        copy.wait()
+    low = [pltpu.make_async_copy(latent_hbm.at[:part, :], part_ref, sems.at[2])]
+    high = [
+        pltpu.make_async_copy(latent_hbm.at[part:, :], part_ref.at[: width - part, :], sems.at[2]),
+        pltpu.make_async_copy(index_hbm, part_ref.at[width - part :, :], sems.at[3]),
+    ]
+
+    def each(copies, act):
+        for copy in copies:
+            act(copy)
+
+    for act in (lambda copy: copy.start(), lambda copy: copy.wait()):
+        each(whole, act)
+        pl.when(bit == 0)(functools.partial(each, low, act))
+        pl.when(bit == 1)(functools.partial(each, high, act))
 
 
 def prelude_kernel(sizes, order_hbm, seg_hbm, weight_hbm, query_hbm, index_query_hbm,
@@ -114,15 +126,25 @@
     n_ctx, half, reach, key_width, idim = sizes
     n_index = 2 if keep else 0
     index_query_refs, refs = refs[:n_index], refs[n_index:]
-    piece_refs, out_refs = refs[:n_ctx], refs[n_ctx : n_ctx + 1 + (n_index > 0)]
-    refs = refs[n_ctx + len(out_refs) :]
-    stack_ref, main_ref, tail_ref, index_main, index_tail, raw_ref, index_raw, inverse_ref = refs
+    if keep:
+        stack_ref, refs = refs[0], refs[1:]
+    else:
+        piece_refs, half_refs, refs = refs[: n_ctx - 2], refs[n_ctx - 2 : n_ctx + 2], refs[n_ctx + 2 :]
+    out_refs, refs = refs[:2], refs[2:]
+    main_ref, tail_ref, index_main, index_tail, raw_ref, index_raw, main_raw, inverse_ref = refs
     key_pad = main_ref.shape[1]
     me = lax.axis_index("ctx")
     mine = own_block(keep)
     rows_here = block_rows(keep, half)
-    for s in range(n_ctx):
-        stack_ref[me ^ s] = piece_refs[s][...]
+    if not keep:
+        stack_ref = out_refs[1]
+        bit = own_block(True)
+        for s in range(n_ctx - 2):
+            stack_ref[me ^ s] = piece_refs[s][...]
+        part = stack_ref.shape[1] // 2
+        for k, ref in enumerate(half_refs):
+            at = pl.multiple_of((bit if k % 2 == 0 else 1 - bit) * part, part)
+            stack_ref[me ^ (n_ctx - 2 + k // 2), pl.ds(at, part), :] = ref[...]
     for slot in range(order_ref.shape[0]):
         inverse_ref[order_ref[slot]] = slot
     block = order_ref[me * 2 + mine]
@@ -136,13 +158,13 @@
     left = lax.broadcasted_iota(jnp.int32, (key_width, LANES), 1) < half
 
     def keys_into(target_ref, c, lanes):
-        halves = []
-        for side in (0, 1):
-            slot = slots[min(2 * c + side, reach_blocks)]
-            tile = stack_ref[slot >> 1, :key_width, :].astype(jnp.float32)
-            turned = pltpu.roll(tile, half, 1)
-            halves.append(jnp.where((slot & 1) == side, tile, turned))
-        both = jnp.where(left, halves[0], halves[1]).astype(target_ref.dtype)
+        near, away = [slots[min(2 * c + side, reach_blocks)] for side in (0, 1)]
+        first_tile = stack_ref[near >> 1, :key_width, :]
+        second_tile = stack_ref[away >> 1, :key_width, :]
+        turned = pltpu.roll(jnp.where(left, second_tile, first_tile), half, 1)
+        both = jnp.where(
+            left, jnp.where((near & 1) == 0, first_tile, turned), jnp.where((away & 1) == 1, second_tile, turned)
+        )
         target_ref[0, :key_width, lanes] = both
         target_ref[1, key_pad - key_width :, lanes] = both
 
@@ -190,18 +212,33 @@
                     index_lhs(ref), index_tail[...], (((1,), (1,)), ((), ())), preferred_element_type=jnp.float32
                 )
 
-    total = jnp.zeros((half, reach), jnp.float32)
-    for parity in (0, 1):
-        raw = lax.dot_general(
-            stacked_queries[parity](), main_ref[parity], (((1,), (0,)), ((), ())), preferred_element_type=jnp.float32
+    groups = 2 * max(1, heads // 2 // 4)
+    each = heads // groups
+
+    def matmul(k):
+        parity = k % 2
+        starts = [(g + k // 2 * each) * 2 * key_width + parity * (2 * key_width - key_pad) for g in range(each)]
+        lhs = jnp.concatenate([query_ref[rows_here, at : at + key_pad] for at in starts], axis=0)
+        main_raw[k % 2] = lax.dot_general(
+            lhs, main_ref[parity], (((1,), (0,)), ((), ())), preferred_element_type=jnp.float32
         )
-        for g in range(heads // 2):
-            here = slice(g * half, (g + 1) * half)
-            scores = ring_fold(own_low, raw[here, :], raw_ref[parity, here, :]) + bias
+
+    def softmax(k, total):
+        for g in range(each):
+            tail = raw_ref[k % 2, (g + k // 2 * each) * half : (g + k // 2 * each + 1) * half, :]
+            scores = ring_fold(own_low, main_raw[k % 2, g * half : (g + 1) * half, :], tail) + bias
             row_max = jnp.max(scores, axis=1, keepdims=True)
             powers = jnp.exp2((scores - row_max) * (score_scale * math.log2(math.e)))
             share = 1.0 / jnp.sum(powers, axis=1, keepdims=True)
             total = total + powers * share
+        return total
+
+    total = jnp.zeros((half, reach), jnp.float32)
+    matmul(0)
+    for k in range(1, groups + 1):
+        if k < groups:
+            matmul(k)
+        total = softmax(k - 1, total)
     out_refs[0][...] = total
 
     if keep:
@@ -258,22 +295,28 @@
     def far(x):
         return pltpu.with_memory_space_constraint(x, pltpu.HBM)
 
-    packed = pl.pallas_call(
+    packed, part = pl.pallas_call(
         pack_kernel,
-        out_shape=jax.ShapeDtypeStruct((key_width + idim, rows), latent_keys.dtype),
+        out_shape=(
+            jax.ShapeDtypeStruct((key_width + idim, rows), latent_keys.dtype),
+            jax.ShapeDtypeStruct(((key_width + idim) // 2, rows), latent_keys.dtype),
+        ),
         in_specs=[hbm, hbm],
-        out_specs=vmem,
-        scratch_shapes=[pltpu.SemaphoreType.DMA((2,))],
+        out_specs=(vmem, vmem),
+        scratch_shapes=[pltpu.SemaphoreType.DMA((4,))],
         compiler_params=pltpu.CompilerParams(vmem_limit_bytes=2 << 20),
         name="pack",
     )(far(latent_keys.T), far(index_keys))
-    own_core = [packed]
-    for s in reversed(range(1, n_ctx // 2)):
+    last = n_ctx // 2 - 1
+    corner = swap(part, "ctx", 2 * last)
+    own_core = []
+    for s in reversed(range(1, last)):
         own_core.append(swap(packed, "ctx", 2 * s))
-    own_core = [packed] + own_core[:0:-1]
+    corner_rest = swap(corner, "head", 1)
     pieces = []
-    for piece in own_core:
+    for piece in [packed] + own_core[::-1]:
         pieces += [piece, swap(piece, "ctx", 1)]
+    pieces += [corner, corner_rest, swap(corner, "ctx", 1), swap(corner_rest, "ctx", 1)]
     seg_table = segment_ids.reshape(seq_len // LANES, LANES)
 
     copies = 8
@@ -300,22 +343,24 @@
     )(far(block_order), far(seg_table), far(index_weight.T), far(main_query), far(index_query))
     taken_query = swap(give_query, "head", 1)
 
-    def block_sums(keep):
+    stack = jax.ShapeDtypeStruct((n_ctx, key_width + idim, rows), packed.dtype)
+
+    def block_sums(keep, keys):
         sums = jax.ShapeDtypeStruct((half, reach), jnp.float32)
         index_queries = [keep_query, taken_query] if keep else []
         return pl.pallas_call(
             functools.partial(block_kernel, (n_ctx, half, reach, key_width, idim), keep),
-            out_shape=(sums, sums) if keep else (sums,),
-            in_specs=[smem, smem] + [vmem] * (2 + len(index_queries) + n_ctx),
-            out_specs=(vmem, vmem) if keep else (vmem,),
+            out_shape=(sums, sums) if keep else (sums, stack),
+            in_specs=[smem, smem] + [vmem] * (2 + len(index_queries) + len(keys)),
+            out_specs=(vmem, vmem),
             scratch_shapes=[
-                pltpu.VMEM((n_ctx, key_width + idim, LANES), jnp.bfloat16),
                 pltpu.VMEM((2, key_pad, reach), jnp.bfloat16),
                 pltpu.VMEM((2, key_pad, LANES), jnp.bfloat16),
                 pltpu.VMEM((reach, idim), jnp.bfloat16),
                 pltpu.VMEM((LANES, idim), jnp.bfloat16),
                 pltpu.VMEM((2, heads // 2 * half, LANES), jnp.float32),
                 pltpu.VMEM((2, index_heads * half, LANES), jnp.float32),
+                pltpu.VMEM((2, min(4, heads // 2) * half, reach), jnp.float32),
                 pltpu.SMEM((block_order.shape[0],), jnp.int32),
             ],
             compiler_params=pltpu.CompilerParams(vmem_limit_bytes=28 << 20),
@@ -323,10 +368,10 @@
                 flops=2 * half * reach * heads * key_pad, bytes_accessed=4 << 20, transcendentals=0
             ),
             name="keep_sums" if keep else "give_sums",
-        )(block_order, segment_ids, bias, near_query, *index_queries, *pieces)
-
-    given = block_sums(False)[0]
-    kept, index_sums = block_sums(True)
+        )(block_order, segment_ids, bias, near_query, *index_queries, *keys)
+
+    given, key_stack = block_sums(False, pieces)
+    kept, index_sums = block_sums(True, [key_stack])
     value = jnp.stack([kept + swap(given, "head", 1), index_sums])
     distances = [1 << k for k in range(1, n_head.bit_length() - 1)]
     for distance in distances[:-1]:

time: 36.2 us -> 43.4 us (1.20); the launches traced: 36 us -> 42.7 us
  waiting for transfers between devices: 14.3 us -> 21.7 us
  Pallas kernels: 9.05 us -> 8.44 us
    ppermute x11 -> x13, waiting for transfers between devices: 14.3 us -> 21.7 us  [swap(): return lax.ppermute(x, axis, [(i, i ^ distance) for i in range(size)])]
    pallas_call x2, Pallas kernels: 5.28 us -> 4.59 us  [block_sums(): pl.pallas_call(functools.partial(block_kernel, (n_ctx, half, reach, key_w...]
    ppermute x11 -> x13, starting transfers between devices: 12.1 us -> 12 us  [swap(): return lax.ppermute(x, axis, [(i, i ^ distance) for i in range(size)])]
  transfers between devices with their start and end apart: 11 -> 13, of which waited for: 5 -> 6; matrix products, arithmetic and copies ran while one was open for 0% -> 0% of each run, Pallas kernels for 22% -> 17%
where the time goes in v2:
time: 43.4 us; the launch traced here: 42.7 us
  waiting for transfers between devices  21.7 us (50%)
  starting transfers between devices  12 us (28%)
  Pallas kernels  8.44 us (19%)
  other arithmetic  0.53 us (1%)
    ppermute x13, waiting for transfers between devices, swap(): return lax.ppermute(x, axis, [(i, i ^ distance) for i in range(size)])  21.7 us
    ppermute x13, starting transfers between devices, swap(): return lax.ppermute(x, axis, [(i, i ^ distance) for i in range(size)])  12 us
    pallas_call x2, Pallas kernels, block_sums(): pl.pallas_call(functools.partial(block_kernel, (n_ctx, half, reach, key_w...  4.59 us
    pallas_call x1, Pallas kernels, per_device(): pl.pallas_call(functools.partial(prelude_kernel, (half, reach, copies)),...  2.61 us
    pallas_call x1, Pallas kernels, per_device(): pl.pallas_call(pack_kernel, out_shape=(jax.ShapeDtypeStruct((key_width +...  1.04 us
  transfers between devices with their start and end apart: 13, of which 6 were waited for; matrix products, arithmetic and copies ran while one was open for 0% of the time, Pallas kernels for 17%

profile of v2, /device:TPU:0, one launch (start us, length us, event | category | flops | bytes accessed | tf_op | source)
XLA Modules:
  0.0 42.7 jit_solution(12487589816884891636)
XLA Ops:
  0.0 0.0 copy-start.1
  0.0 0.0 copy-start
  0.0 1.0 %pack.1 = (bf16[704,128]{1,0:T(8,128)(2,1)S(1)}, bf16[352,128]{1,0:T(8,128)(2,1)S(1)}) custom-call(bf16[576,128]{1,0:T(8,128)(2,1)} %bitcast.10, bf16[128,128]{1,0:T(8,128)(2,1)} %index_hbm.1), custom_call_target="tpu_custom_call" | custom-call | tf_op jit(solution)/shard_map/pack/pallas_call | solution.py:298
  1.1 4.0 %collective-permute-start.6 = (bf16[352,128]{1,0:T(8,128)(2,1)S(1)}, bf16[352,128]{1,0:T(8,128)(2,1)S(1)}, u32[]{:S(2)}, u32[]{:S(2)}) collective-permute-start(bf16[352,128]{1,0:T(8,128)(2,1)S(1)} %get-tuple-element.20), channel_id=1, source_target_pairs={{0,24},{4,28},{8,16},{12,20},{16,8},{20,12},{24,0},{28,4},{1,25},{... | collective-permute-start | bytes 270344 | tf_op jit(solution)/shard_map/ppermute | solution.py:19
  5.0 0.5 %collective-permute-start.4 = (bf16[704,128]{1,0:T(8,128)(2,1)S(1)}, bf16[704,128]{1,0:T(8,128)(2,1)S(1)}, u32[]{:S(2)}, u32[]{:S(2)}) collective-permute-start(bf16[704,128]{1,0:T(8,128)(2,1)S(1)} %get-tuple-element.19.refs_0_), channel_id=1, source_target_pairs={{0,16},{4,20},{8,24},{12,28},{16,0},{20,4},{24,8},{28,12},{1,17},{... | collective-permute-start | bytes 540680 | tf_op jit(solution)/shard_map/ppermute | solution.py:19
  5.5 0.1 collective-permute-start.2
  5.7 2.4 %collective-permute-done.6.refs_6_ = bf16[352,128]{1,0:T(8,128)(2,1)S(1)} collective-permute-done((bf16[352,128]{1,0:T(8,128)(2,1)S(1)}, bf16[352,128]{1,0:T(8,128)(2,1)S(1)}, u32[]{:S(2)}, u32[]{:S(2)}) %collective-permute-start.6) | collective-permute-done | bytes 90144 | tf_op jit(solution)/shard_map/ppermute | solution.py:19
  8.1 0.0 collective-permute-start.8
  8.1 2.6 %prelude.1 = (f32[2,64,256]{2,1,0:T(8,128)S(1)}, bf16[128,18432]{1,0:T(8,128)(2,1)S(1)}, bf16[64,2176]{1,0:T(8,128)(2,1)S(1)}, bf16[64,2176]{1,0:T(8,128)(2,1)S(1)}) custom-call(s32[16]{0:T(128)} %order_ref.3, s32[8,128]{1,0:T(8,128)} %bitcast.9, bf16[16,128]{1,0:T(8,128)(2,1)} %bitcast.11, bf16[128,18432]{1,0:T(8,128)(2,1)} %query_hbm.1, ...), custom_call_target="tpu_custom_call" | custom-call | flops 1048576 | bytes 10485760 | tf_op jit(solution)/shard_map/prelude/pallas_call | solution.py:324
  10.7 1.6 %collective-permute-start = (bf16[64,2176]{1,0:T(8,128)(2,1)S(1)}, bf16[64,2176]{1,0:T(8,128)(2,1)S(1)}, u32[]{:S(2)}, u32[]{:S(2)}) collective-permute-start(bf16[64,2176]{1,0:T(8,128)(2,1)S(1)} %get-tuple-element.18), channel_id=1, source_target_pairs={{0,1},{1,0},{2,3},{3,2},{4,5},{5,4},{6,7},{7,6},{8,9},{9,8},{10,11... | collective-permute-start | bytes 835592 | tf_op jit(solution)/shard_map/ppermute | solution.py:19
  12.3 0.2 collective-permute-start.1
  12.5 0.0 collective-permute-done.8.refs_8_
  12.5 0.5 %collective-permute-start.7 = (bf16[352,128]{1,0:T(8,128)(2,1)S(1)}, bf16[352,128]{1,0:T(8,128)(2,1)S(1)}, u32[]{:S(2)}, u32[]{:S(2)}) collective-permute-start(bf16[352,128]{1,0:T(8,128)(2,1)S(1)} %collective-permute-done.6.refs_6_), channel_id=1, source_target_pairs={{0,1},{1,0},{2,3},{3,2},{4,5},{5,4},{6,7},{7,6},{8,9},{9,8},{10,11... | collective-permute-start | bytes 270344 | tf_op jit(solution)/shard_map/ppermute | solution.py:19
  13.0 0.0 collective-permute-done.4.refs_4_
  13.0 0.0 collective-permute-start.5
  13.0 0.0 collective-permute-done.2.refs_2_
  13.0 0.5 %collective-permute-start.3 = (bf16[704,128]{1,0:T(8,128)(2,1)S(1)}, bf16[704,128]{1,0:T(8,128)(2,1)S(1)}, u32[]{:S(2)}, u32[]{:S(2)}) collective-permute-start(bf16[704,128]{1,0:T(8,128)(2,1)S(1)} %collective-permute-done.2.refs_2_), channel_id=1, source_target_pairs={{0,4},{4,0},{8,12},{12,8},{16,20},{20,16},{24,28},{28,24},{1,5},{5... | collective-permute-start | bytes 540680 | tf_op jit(solution)/shard_map/ppermute | solution.py:19
  13.5 8.2 %collective-permute-done.7.refs_7_ = bf16[352,128]{1,0:T(8,128)(2,1)S(1)} collective-permute-done((bf16[352,128]{1,0:T(8,128)(2,1)S(1)}, bf16[352,128]{1,0:T(8,128)(2,1)S(1)}, u32[]{:S(2)}, u32[]{:S(2)}) %collective-permute-start.7) | collective-permute-done | bytes 90144 | tf_op jit(solution)/shard_map/ppermute | solution.py:19
  21.7 0.0 collective-permute-start.9
  21.7 0.0 collective-permute-done.1.refs_1_
  21.7 1.3 %collective-permute-done.9.refs_9_ = bf16[352,128]{1,0:T(8,128)(2,1)S(1)} collective-permute-done((bf16[352,128]{1,0:T(8,128)(2,1)S(1)}, bf16[352,128]{1,0:T(8,128)(2,1)S(1)}, u32[]{:S(2)}, u32[]{:S(2)}) %collective-permute-start.9) | collective-permute-done | bytes 90144 | tf_op jit(solution)/shard_map/ppermute | solution.py:19
  23.0 0.0 collective-permute-done.5.refs_5_
  23.0 0.0 collective-permute-done.3.refs_3_
  23.0 0.0 copy-done.1
  23.0 0.0 copy-done
  23.0 2.2 %give_sums.1 = (f32[64,256]{1,0:T(8,128)S(1)}, bf16[8,704,128]{2,1,0:T(8,128)(2,1)S(1)}) custom-call(s32[16]{0:T(128)S(1)} %copy-done.1, s32[1024]{0:T(1024)S(1)} %copy-done, f32[2,64,256]{2,1,0:T(8,128)S(1)} %get-tuple-element.15.bias_ref, bf16[128,18432]{1,0:T(8,128)(2,1)S(1)} %get-tuple-element.16.query_ref, ...), custom_call_target="tpu_custom_call" | custom-call | flops 671088640 | bytes 4194304 | tf_op jit(solution)/shard_map/give_sums/pallas_call | solution.py:351
  25.2 1.6 %collective-permute-start.10 = (f32[64,256]{1,0:T(8,128)S(1)}, f32[64,256]{1,0:T(8,128)S(1)}, u32[]{:S(2)}, u32[]{:S(2)}) collective-permute-start(f32[64,256]{1,0:T(8,128)S(1)} %get-tuple-element.23), channel_id=1, source_target_pairs={{0,1},{1,0},{2,3},{3,2},{4,5},{5,4},{6,7},{7,6},{8,9},{9,8},{10,11... | collective-permute-start | bytes 196616 | tf_op jit(solution)/shard_map/ppermute | solution.py:19
  26.9 0.0 collective-permute-done.refs_1_
  26.9 2.4 %keep_sums.1 = (f32[64,256]{1,0:T(8,128)S(1)}, f32[64,256]{1,0:T(8,128)S(1)}) custom-call(s32[16]{0:T(128)S(1)} %copy-done.1, s32[1024]{0:T(1024)S(1)} %copy-done, f32[2,64,256]{2,1,0:T(8,128)S(1)} %get-tuple-element.15.bias_ref, bf16[128,18432]{1,0:T(8,128)(2,1)S(1)} %get-tuple-element.16.query_ref, bf16[64,2176]{1,0:T(8,128)(2,1)S(1)} %get-tuple-element.17.refs_0_, ...), custom_call_target="tpu_custom_call" | custom-call | flops 671088640 | bytes 4194304 | tf_op jit(solution)/shard_map/keep_sums/pallas_call | solution.py:351
  29.3 0.3 collective-permute-done.10
  29.6 2.7 %collective-permute-start.11 = (f32[2,64,256]{2,1,0:T(8,128)S(1)}, f32[2,64,256]{2,1,0:T(8,128)S(1)}, u32[]{:S(2)}, u32[]{:S(2)}) collective-permute-start(f32[2,64,256]{2,1,0:T(8,128)S(1)} %pad_maximum_fusion.refs_0_), channel_id=1, source_target_pairs={{0,2},{1,3},{2,0},{3,1},{4,6},{5,7},{6,4},{7,5},{8,10},{9,11},{10,... | collective-permute-start | bytes 393224 | tf_op jit(solution)/shard_map/ppermute | solution.py:19
  32.3 6.1 %collective-permute-done.11.refs_1_ = f32[2,64,256]{2,1,0:T(8,128)S(1)} collective-permute-done((f32[2,64,256]{2,1,0:T(8,128)S(1)}, f32[2,64,256]{2,1,0:T(8,128)S(1)}, u32[]{:S(2)}, u32[]{:S(2)}) %collective-permute-start.11) | collective-permute-done | bytes 131104 | tf_op jit(solution)/shard_map/ppermute | solution.py:19
  38.4 0.2 row_losses.1
  38.6 0.2 collective-permute-start.12
  38.8 3.4 %collective-permute-done.12 = f32[1,128]{1,0:T(1,128)S(1)} collective-permute-done((f32[1,128]{1,0:T(1,128)S(1)}, f32[1,128]{1,0:T(1,128)S(1)}, u32[]{:S(2)}, u32[]{:S(2)}) %collective-permute-start.12) | collective-permute-done | bytes 544 | tf_op jit(solution)/shard_map/ppermute | solution.py:19
  42.2 0.5 %add_bitcast_fusion.1 = f32[128]{0:T(128)} fusion(f32[1,128]{1,0:T(1,128)S(1)} %row_losses.1, f32[1,128]{1,0:T(1,128)S(1)} %collective-permute-done.12), kind=kLoop, calls=%fused_computation.2 | loop fusion | flops 128 | bytes 1536 | tf_op jit(solution)/shard_map/reshape | solution.py:388
  (2 shorter events, 0.0 us)
Async XLA Ops:
  0.0 23.0 %copy-start.1 = (s32[16]{0:T(128)S(1)}, s32[16]{0:T(128)}, u32[]{:S(2)}) copy-start(s32[16]{0:T(128)} %order_ref.3) | copy-start | bytes 196
  0.0 23.0 %copy-start = (s32[1024]{0:T(1024)S(1)}, s32[1024]{0:T(1024)}, u32[]{:S(2)}) copy-start(s32[1024]{0:T(1024)} %seg_ref.3) | copy-start | bytes 12292
  1.1 7.0 %collective-permute-start.6 = (bf16[352,128]{1,0:T(8,128)(2,1)S(1)}, bf16[352,128]{1,0:T(8,128)(2,1)S(1)}, u32[]{:S(2)}, u32[]{:S(2)}) collective-permute-start(bf16[352,128]{1,0:T(8,128)(2,1)S(1)} %get-tuple-element.20), channel_id=1, source_target_pairs={{0,24},{4,28},{8,16},{12,20},{16,8},{20,12},{24,0},{28,4},{1,25},{... | collective-permute-start | bytes 270344 | tf_op jit(solution)/shard_map/ppermute | solution.py:19
  5.0 8.0 %collective-permute-start.4 = (bf16[704,128]{1,0:T(8,128)(2,1)S(1)}, bf16[704,128]{1,0:T(8,128)(2,1)S(1)}, u32[]{:S(2)}, u32[]{:S(2)}) collective-permute-start(bf16[704,128]{1,0:T(8,128)(2,1)S(1)} %get-tuple-element.19.refs_0_), channel_id=1, source_target_pairs={{0,16},{4,20},{8,24},{12,28},{16,0},{20,4},{24,8},{28,12},{1,17},{... | collective-permute-start | bytes 540680 | tf_op jit(solution)/shard_map/ppermute | solution.py:19
  5.5 7.5 %collective-permute-start.2 = (bf16[704,128]{1,0:T(8,128)(2,1)S(1)}, bf16[704,128]{1,0:T(8,128)(2,1)S(1)}, u32[]{:S(2)}, u32[]{:S(2)}) collective-permute-start(bf16[704,128]{1,0:T(8,128)(2,1)S(1)} %get-tuple-element.19.refs_0_), channel_id=1, source_target_pairs={{0,8},{4,12},{8,0},{12,4},{16,24},{20,28},{24,16},{28,20},{1,9},{5... | collective-permute-start | bytes 540680 | tf_op jit(solution)/shard_map/ppermute | solution.py:19
  8.1 4.5 %collective-permute-start.8 = (bf16[352,128]{1,0:T(8,128)(2,1)S(1)}, bf16[352,128]{1,0:T(8,128)(2,1)S(1)}, u32[]{:S(2)}, u32[]{:S(2)}) collective-permute-start(bf16[352,128]{1,0:T(8,128)(2,1)S(1)} %collective-permute-done.6.refs_6_), channel_id=1, source_target_pairs={{0,4},{4,0},{8,12},{12,8},{16,20},{20,16},{24,28},{28,24},{1,5},{5... | collective-permute-start | bytes 270344 | tf_op jit(solution)/shard_map/ppermute | solution.py:19
  10.7 16.2 %collective-permute-start = (bf16[64,2176]{1,0:T(8,128)(2,1)S(1)}, bf16[64,2176]{1,0:T(8,128)(2,1)S(1)}, u32[]{:S(2)}, u32[]{:S(2)}) collective-permute-start(bf16[64,2176]{1,0:T(8,128)(2,1)S(1)} %get-tuple-element.18), channel_id=1, source_target_pairs={{0,1},{1,0},{2,3},{3,2},{4,5},{5,4},{6,7},{7,6},{8,9},{9,8},{10,11... | collective-permute-start | bytes 835592 | tf_op jit(solution)/shard_map/ppermute | solution.py:19
  12.3 9.4 %collective-permute-start.1 = (bf16[704,128]{1,0:T(8,128)(2,1)S(1)}, bf16[704,128]{1,0:T(8,128)(2,1)S(1)}, u32[]{:S(2)}, u32[]{:S(2)}) collective-permute-start(bf16[704,128]{1,0:T(8,128)(2,1)S(1)} %get-tuple-element.19.refs_0_), channel_id=1, source_target_pairs={{0,4},{4,0},{8,12},{12,8},{16,20},{20,16},{24,28},{28,24},{1,5},{5... | collective-permute-start | bytes 540680 | tf_op jit(solution)/shard_map/ppermute | solution.py:19
  12.5 9.2 %collective-permute-start.7 = (bf16[352,128]{1,0:T(8,128)(2,1)S(1)}, bf16[352,128]{1,0:T(8,128)(2,1)S(1)}, u32[]{:S(2)}, u32[]{:S(2)}) collective-permute-start(bf16[352,128]{1,0:T(8,128)(2,1)S(1)} %collective-permute-done.6.refs_6_), channel_id=1, source_target_pairs={{0,1},{1,0},{2,3},{3,2},{4,5},{5,4},{6,7},{7,6},{8,9},{9,8},{10,11... | collective-permute-start | bytes 270344 | tf_op jit(solution)/shard_map/ppermute | solution.py:19
  13.0 10.0 %collective-permute-start.5 = (bf16[704,128]{1,0:T(8,128)(2,1)S(1)}, bf16[704,128]{1,0:T(8,128)(2,1)S(1)}, u32[]{:S(2)}, u32[]{:S(2)}) collective-permute-start(bf16[704,128]{1,0:T(8,128)(2,1)S(1)} %collective-permute-done.4.refs_4_), channel_id=1, source_target_pairs={{0,4},{4,0},{8,12},{12,8},{16,20},{20,16},{24,28},{28,24},{1,5},{5... | collective-permute-start | bytes 540680 | tf_op jit(solution)/shard_map/ppermute | solution.py:19
  13.0 10.0 %collective-permute-start.3 = (bf16[704,128]{1,0:T(8,128)(2,1)S(1)}, bf16[704,128]{1,0:T(8,128)(2,1)S(1)}, u32[]{:S(2)}, u32[]{:S(2)}) collective-permute-start(bf16[704,128]{1,0:T(8,128)(2,1)S(1)} %collective-permute-done.2.refs_2_), channel_id=1, source_target_pairs={{0,4},{4,0},{8,12},{12,8},{16,20},{20,16},{24,28},{28,24},{1,5},{5... | collective-permute-start | bytes 540680 | tf_op jit(solution)/shard_map/ppermute | solution.py:19
  21.7 1.3 %collective-permute-start.9 = (bf16[352,128]{1,0:T(8,128)(2,1)S(1)}, bf16[352,128]{1,0:T(8,128)(2,1)S(1)}, u32[]{:S(2)}, u32[]{:S(2)}) collective-permute-start(bf16[352,128]{1,0:T(8,128)(2,1)S(1)} %collective-permute-done.7.refs_7_), channel_id=1, source_target_pairs={{0,4},{4,0},{8,12},{12,8},{16,20},{20,16},{24,28},{28,24},{1,5},{5... | collective-permute-start | bytes 270344 | tf_op jit(solution)/shard_map/ppermute | solution.py:19
  25.2 4.3 %collective-permute-start.10 = (f32[64,256]{1,0:T(8,128)S(1)}, f32[64,256]{1,0:T(8,128)S(1)}, u32[]{:S(2)}, u32[]{:S(2)}) collective-permute-start(f32[64,256]{1,0:T(8,128)S(1)} %get-tuple-element.23), channel_id=1, source_target_pairs={{0,1},{1,0},{2,3},{3,2},{4,5},{5,4},{6,7},{7,6},{8,9},{9,8},{10,11... | collective-permute-start | bytes 196616 | tf_op jit(solution)/shard_map/ppermute | solution.py:19
  29.6 8.8 %collective-permute-start.11 = (f32[2,64,256]{2,1,0:T(8,128)S(1)}, f32[2,64,256]{2,1,0:T(8,128)S(1)}, u32[]{:S(2)}, u32[]{:S(2)}) collective-permute-start(f32[2,64,256]{2,1,0:T(8,128)S(1)} %pad_maximum_fusion.refs_0_), channel_id=1, source_target_pairs={{0,2},{1,3},{2,0},{3,1},{4,6},{5,7},{6,4},{7,5},{8,10},{9,11},{10,... | collective-permute-start | bytes 393224 | tf_op jit(solution)/shard_map/ppermute | solution.py:19
  38.6 3.6 %collective-permute-start.12 = (f32[1,128]{1,0:T(1,128)S(1)}, f32[1,128]{1,0:T(1,128)S(1)}, u32[]{:S(2)}, u32[]{:S(2)}) collective-permute-start(f32[1,128]{1,0:T(1,128)S(1)} %row_losses.1), channel_id=1, source_target_pairs={{0,1},{1,0},{2,3},{3,2},{4,5},{5,4},{6,7},{7,6},{8,9},{9,8},{10,11... | collective-permute-start | bytes 1544 | tf_op jit(solution)/shard_map/ppermute | solution.py:19

commit v3 on v2

--- a/solution.py
+++ b/solution.py
@@ -67,10 +67,11 @@
     width = latent_hbm.shape[0]
     part = part_ref.shape[0]
     bit = own_block(True)
-    whole = [
-        pltpu.make_async_copy(latent_hbm, out_ref.at[:width, :], sems.at[0]),
-        pltpu.make_async_copy(index_hbm, out_ref.at[width:, :], sems.at[1]),
-    ]
+    quarter = width // 4
+    whole = [pltpu.make_async_copy(index_hbm, out_ref.at[width:, :], sems.at[0])]
+    for c in range(4):
+        here = slice(c * quarter, (c + 1) * quarter)
+        whole.append(pltpu.make_async_copy(latent_hbm.at[here, :], out_ref.at[here, :], sems.at[4 + c]))
     low = [pltpu.make_async_copy(latent_hbm.at[:part, :], part_ref, sems.at[2])]
     high = [
         pltpu.make_async_copy(latent_hbm.at[part:, :], part_ref.at[: width - part, :], sems.at[2]),
@@ -303,7 +304,7 @@
         ),
         in_specs=[hbm, hbm],
         out_specs=(vmem, vmem),
-        scratch_shapes=[pltpu.SemaphoreType.DMA((4,))],
+        scratch_shapes=[pltpu.SemaphoreType.DMA((8,))],
         compiler_params=pltpu.CompilerParams(vmem_limit_bytes=2 << 20),
         name="pack",
     )(far(latent_keys.T), far(index_keys))

time: 43.4 us -> 43.5 us (level)
  no operation moved by 1% of the time
where the time goes in v3:
time: 43.5 us; the launch traced here: 42.8 us
  waiting for transfers between devices  21.7 us (50%)
  starting transfers between devices  12 us (28%)
  Pallas kernels  8.49 us (20%)
  other arithmetic  0.53 us (1%)
    ppermute x13, waiting for transfers between devices, swap(): return lax.ppermute(x, axis, [(i, i ^ distance) for i in range(size)])  21.7 us
    ppermute x13, starting transfers between devices, swap(): return lax.ppermute(x, axis, [(i, i ^ distance) for i in range(size)])  12 us
    pallas_call x2, Pallas kernels, block_sums(): pl.pallas_call(functools.partial(block_kernel, (n_ctx, half, reach, key_w...  4.59 us
    pallas_call x1, Pallas kernels, per_device(): pl.pallas_call(functools.partial(prelude_kernel, (half, reach, copies)),...  2.61 us
    pallas_call x1, Pallas kernels, per_device(): pl.pallas_call(pack_kernel, out_shape=(jax.ShapeDtypeStruct((key_width +...  1.09 us
  transfers between devices with their start and end apart: 13, of which 6 were waited for; matrix products, arithmetic and copies ran while one was open for 0% of the time, Pallas kernels for 17%

profile of v3, /device:TPU:0, one launch (start us, length us, event | category | flops | bytes accessed | tf_op | source)
XLA Modules:
  0.0 42.8 jit_solution(7970715560384400907)
XLA Ops:
  0.0 0.0 copy-start.1
  0.0 0.0 copy-start
  0.0 1.1 %pack.1 = (bf16[704,128]{1,0:T(8,128)(2,1)S(1)}, bf16[352,128]{1,0:T(8,128)(2,1)S(1)}) custom-call(bf16[576,128]{1,0:T(8,128)(2,1)} %bitcast.10, bf16[128,128]{1,0:T(8,128)(2,1)} %index_hbm.1), custom_call_target="tpu_custom_call" | custom-call | tf_op jit(solution)/shard_map/pack/pallas_call | solution.py:299
  1.1 4.0 %collective-permute-start.6 = (bf16[352,128]{1,0:T(8,128)(2,1)S(1)}, bf16[352,128]{1,0:T(8,128)(2,1)S(1)}, u32[]{:S(2)}, u32[]{:S(2)}) collective-permute-start(bf16[352,128]{1,0:T(8,128)(2,1)S(1)} %get-tuple-element.20), channel_id=1, source_target_pairs={{0,24},{4,28},{8,16},{12,20},{16,8},{20,12},{24,0},{28,4},{1,25},{... | collective-permute-start | bytes 270344 | tf_op jit(solution)/shard_map/ppermute | solution.py:19
  5.1 0.5 %collective-permute-start.4 = (bf16[704,128]{1,0:T(8,128)(2,1)S(1)}, bf16[704,128]{1,0:T(8,128)(2,1)S(1)}, u32[]{:S(2)}, u32[]{:S(2)}) collective-permute-start(bf16[704,128]{1,0:T(8,128)(2,1)S(1)} %get-tuple-element.19.refs_0_), channel_id=1, source_target_pairs={{0,16},{4,20},{8,24},{12,28},{16,0},{20,4},{24,8},{28,12},{1,17},{... | collective-permute-start | bytes 540680 | tf_op jit(solution)/shard_map/ppermute | solution.py:19
  5.6 0.1 collective-permute-start.2
  5.7 2.4 %collective-permute-done.6.refs_6_ = bf16[352,128]{1,0:T(8,128)(2,1)S(1)} collective-permute-done((bf16[352,128]{1,0:T(8,128)(2,1)S(1)}, bf16[352,128]{1,0:T(8,128)(2,1)S(1)}, u32[]{:S(2)}, u32[]{:S(2)}) %collective-permute-start.6) | collective-permute-done | bytes 90144 | tf_op jit(solution)/shard_map/ppermute | solution.py:19
  8.1 0.0 collective-permute-start.8
  8.1 2.6 %prelude.1 = (f32[2,64,256]{2,1,0:T(8,128)S(1)}, bf16[128,18432]{1,0:T(8,128)(2,1)S(1)}, bf16[64,2176]{1,0:T(8,128)(2,1)S(1)}, bf16[64,2176]{1,0:T(8,128)(2,1)S(1)}) custom-call(s32[16]{0:T(128)} %order_ref.3, s32[8,128]{1,0:T(8,128)} %bitcast.9, bf16[16,128]{1,0:T(8,128)(2,1)} %bitcast.11, bf16[128,18432]{1,0:T(8,128)(2,1)} %query_hbm.1, ...), custom_call_target="tpu_custom_call" | custom-call | flops 1048576 | bytes 10485760 | tf_op jit(solution)/shard_map/prelude/pallas_call | solution.py:325
  10.7 1.6 %collective-permute-start = (bf16[64,2176]{1,0:T(8,128)(2,1)S(1)}, bf16[64,2176]{1,0:T(8,128)(2,1)S(1)}, u32[]{:S(2)}, u32[]{:S(2)}) collective-permute-start(bf16[64,2176]{1,0:T(8,128)(2,1)S(1)} %get-tuple-element.18), channel_id=1, source_target_pairs={{0,1},{1,0},{2,3},{3,2},{4,5},{5,4},{6,7},{7,6},{8,9},{9,8},{10,11... | collective-permute-start | bytes 835592 | tf_op jit(solution)/shard_map/ppermute | solution.py:19
  12.3 0.2 collective-permute-start.1
  12.6 0.0 collective-permute-done.8.refs_8_
  12.6 0.5 %collective-permute-start.7 = (bf16[352,128]{1,0:T(8,128)(2,1)S(1)}, bf16[352,128]{1,0:T(8,128)(2,1)S(1)}, u32[]{:S(2)}, u32[]{:S(2)}) collective-permute-start(bf16[352,128]{1,0:T(8,128)(2,1)S(1)} %collective-permute-done.6.refs_6_), channel_id=1, source_target_pairs={{0,1},{1,0},{2,3},{3,2},{4,5},{5,4},{6,7},{7,6},{8,9},{9,8},{10,11... | collective-permute-start | bytes 270344 | tf_op jit(solution)/shard_map/ppermute | solution.py:19
  13.0 0.0 collective-permute-done.4.refs_4_
  13.0 0.0 collective-permute-start.5
  13.1 0.0 collective-permute-done.2.refs_2_
  13.1 0.5 %collective-permute-start.3 = (bf16[704,128]{1,0:T(8,128)(2,1)S(1)}, bf16[704,128]{1,0:T(8,128)(2,1)S(1)}, u32[]{:S(2)}, u32[]{:S(2)}) collective-permute-start(bf16[704,128]{1,0:T(8,128)(2,1)S(1)} %collective-permute-done.2.refs_2_), channel_id=1, source_target_pairs={{0,4},{4,0},{8,12},{12,8},{16,20},{20,16},{24,28},{28,24},{1,5},{5... | collective-permute-start | bytes 540680 | tf_op jit(solution)/shard_map/ppermute | solution.py:19
  13.6 8.2 %collective-permute-done.7.refs_7_ = bf16[352,128]{1,0:T(8,128)(2,1)S(1)} collective-permute-done((bf16[352,128]{1,0:T(8,128)(2,1)S(1)}, bf16[352,128]{1,0:T(8,128)(2,1)S(1)}, u32[]{:S(2)}, u32[]{:S(2)}) %collective-permute-start.7) | collective-permute-done | bytes 90144 | tf_op jit(solution)/shard_map/ppermute | solution.py:19
  21.8 0.0 collective-permute-start.9
  21.8 0.0 collective-permute-done.1.refs_1_
  21.8 1.3 %collective-permute-done.9.refs_9_ = bf16[352,128]{1,0:T(8,128)(2,1)S(1)} collective-permute-done((bf16[352,128]{1,0:T(8,128)(2,1)S(1)}, bf16[352,128]{1,0:T(8,128)(2,1)S(1)}, u32[]{:S(2)}, u32[]{:S(2)}) %collective-permute-start.9) | collective-permute-done | bytes 90144 | tf_op jit(solution)/shard_map/ppermute | solution.py:19
  23.1 0.0 collective-permute-done.5.refs_5_
  23.1 0.0 collective-permute-done.3.refs_3_
  23.1 0.0 copy-done.1
  23.1 0.0 copy-done
  23.1 2.2 %give_sums.1 = (f32[64,256]{1,0:T(8,128)S(1)}, bf16[8,704,128]{2,1,0:T(8,128)(2,1)S(1)}) custom-call(s32[16]{0:T(128)S(1)} %copy-done.1, s32[1024]{0:T(1024)S(1)} %copy-done, f32[2,64,256]{2,1,0:T(8,128)S(1)} %get-tuple-element.15.bias_ref, bf16[128,18432]{1,0:T(8,128)(2,1)S(1)} %get-tuple-element.16.query_ref, ...), custom_call_target="tpu_custom_call" | custom-call | flops 671088640 | bytes 4194304 | tf_op jit(solution)/shard_map/give_sums/pallas_call | solution.py:352
  25.3 1.6 %collective-permute-start.10 = (f32[64,256]{1,0:T(8,128)S(1)}, f32[64,256]{1,0:T(8,128)S(1)}, u32[]{:S(2)}, u32[]{:S(2)}) collective-permute-start(f32[64,256]{1,0:T(8,128)S(1)} %get-tuple-element.23), channel_id=1, source_target_pairs={{0,1},{1,0},{2,3},{3,2},{4,5},{5,4},{6,7},{7,6},{8,9},{9,8},{10,11... | collective-permute-start | bytes 196616 | tf_op jit(solution)/shard_map/ppermute | solution.py:19
  26.9 0.0 collective-permute-done.refs_1_
  26.9 2.4 %keep_sums.1 = (f32[64,256]{1,0:T(8,128)S(1)}, f32[64,256]{1,0:T(8,128)S(1)}) custom-call(s32[16]{0:T(128)S(1)} %copy-done.1, s32[1024]{0:T(1024)S(1)} %copy-done, f32[2,64,256]{2,1,0:T(8,128)S(1)} %get-tuple-element.15.bias_ref, bf16[128,18432]{1,0:T(8,128)(2,1)S(1)} %get-tuple-element.16.query_ref, bf16[64,2176]{1,0:T(8,128)(2,1)S(1)} %get-tuple-element.17.refs_0_, ...), custom_call_target="tpu_custom_call" | custom-call | flops 671088640 | bytes 4194304 | tf_op jit(solution)/shard_map/keep_sums/pallas_call | solution.py:352
  29.3 0.3 collective-permute-done.10
  29.6 2.7 %collective-permute-start.11 = (f32[2,64,256]{2,1,0:T(8,128)S(1)}, f32[2,64,256]{2,1,0:T(8,128)S(1)}, u32[]{:S(2)}, u32[]{:S(2)}) collective-permute-start(f32[2,64,256]{2,1,0:T(8,128)S(1)} %pad_maximum_fusion.refs_0_), channel_id=1, source_target_pairs={{0,2},{1,3},{2,0},{3,1},{4,6},{5,7},{6,4},{7,5},{8,10},{9,11},{10,... | collective-permute-start | bytes 393224 | tf_op jit(solution)/shard_map/ppermute | solution.py:19
  32.3 6.1 %collective-permute-done.11.refs_1_ = f32[2,64,256]{2,1,0:T(8,128)S(1)} collective-permute-done((f32[2,64,256]{2,1,0:T(8,128)S(1)}, f32[2,64,256]{2,1,0:T(8,128)S(1)}, u32[]{:S(2)}, u32[]{:S(2)}) %collective-permute-start.11) | collective-permute-done | bytes 131104 | tf_op jit(solution)/shard_map/ppermute | solution.py:19
  38.4 0.2 row_losses.1
  38.6 0.2 collective-permute-start.12
  38.8 3.4 %collective-permute-done.12 = f32[1,128]{1,0:T(1,128)S(1)} collective-permute-done((f32[1,128]{1,0:T(1,128)S(1)}, f32[1,128]{1,0:T(1,128)S(1)}, u32[]{:S(2)}, u32[]{:S(2)}) %collective-permute-start.12) | collective-permute-done | bytes 544 | tf_op jit(solution)/shard_map/ppermute | solution.py:19
  42.3 0.5 %add_bitcast_fusion.1 = f32[128]{0:T(128)} fusion(f32[1,128]{1,0:T(1,128)S(1)} %row_losses.1, f32[1,128]{1,0:T(1,128)S(1)} %collective-permute-done.12), kind=kLoop, calls=%fused_computation.2 | loop fusion | flops 128 | bytes 1536 | tf_op jit(solution)/shard_map/reshape | solution.py:389
  (2 shorter events, 0.0 us)
Async XLA Ops:
  0.0 23.1 %copy-start.1 = (s32[16]{0:T(128)S(1)}, s32[16]{0:T(128)}, u32[]{:S(2)}) copy-start(s32[16]{0:T(128)} %order_ref.3) | copy-start | bytes 196
  0.0 23.1 %copy-start = (s32[1024]{0:T(1024)S(1)}, s32[1024]{0:T(1024)}, u32[]{:S(2)}) copy-start(s32[1024]{0:T(1024)} %seg_ref.3) | copy-start | bytes 12292
  1.1 7.0 %collective-permute-start.6 = (bf16[352,128]{1,0:T(8,128)(2,1)S(1)}, bf16[352,128]{1,0:T(8,128)(2,1)S(1)}, u32[]{:S(2)}, u32[]{:S(2)}) collective-permute-start(bf16[352,128]{1,0:T(8,128)(2,1)S(1)} %get-tuple-element.20), channel_id=1, source_target_pairs={{0,24},{4,28},{8,16},{12,20},{16,8},{20,12},{24,0},{28,4},{1,25},{... | collective-permute-start | bytes 270344 | tf_op jit(solution)/shard_map/ppermute | solution.py:19
  5.1 8.0 %collective-permute-start.4 = (bf16[704,128]{1,0:T(8,128)(2,1)S(1)}, bf16[704,128]{1,0:T(8,128)(2,1)S(1)}, u32[]{:S(2)}, u32[]{:S(2)}) collective-permute-start(bf16[704,128]{1,0:T(8,128)(2,1)S(1)} %get-tuple-element.19.refs_0_), channel_id=1, source_target_pairs={{0,16},{4,20},{8,24},{12,28},{16,0},{20,4},{24,8},{28,12},{1,17},{... | collective-permute-start | bytes 540680 | tf_op jit(solution)/shard_map/ppermute | solution.py:19
  5.6 7.5 %collective-permute-start.2 = (bf16[704,128]{1,0:T(8,128)(2,1)S(1)}, bf16[704,128]{1,0:T(8,128)(2,1)S(1)}, u32[]{:S(2)}, u32[]{:S(2)}) collective-permute-start(bf16[704,128]{1,0:T(8,128)(2,1)S(1)} %get-tuple-element.19.refs_0_), channel_id=1, source_target_pairs={{0,8},{4,12},{8,0},{12,4},{16,24},{20,28},{24,16},{28,20},{1,9},{5... | collective-permute-start | bytes 540680 | tf_op jit(solution)/shard_map/ppermute | solution.py:19
  8.1 4.5 %collective-permute-start.8 = (bf16[352,128]{1,0:T(8,128)(2,1)S(1)}, bf16[352,128]{1,0:T(8,128)(2,1)S(1)}, u32[]{:S(2)}, u32[]{:S(2)}) collective-permute-start(bf16[352,128]{1,0:T(8,128)(2,1)S(1)} %collective-permute-done.6.refs_6_), channel_id=1, source_target_pairs={{0,4},{4,0},{8,12},{12,8},{16,20},{20,16},{24,28},{28,24},{1,5},{5... | collective-permute-start | bytes 270344 | tf_op jit(solution)/shard_map/ppermute | solution.py:19
  10.7 16.2 %collective-permute-start = (bf16[64,2176]{1,0:T(8,128)(2,1)S(1)}, bf16[64,2176]{1,0:T(8,128)(2,1)S(1)}, u32[]{:S(2)}, u32[]{:S(2)}) collective-permute-start(bf16[64,2176]{1,0:T(8,128)(2,1)S(1)} %get-tuple-element.18), channel_id=1, source_target_pairs={{0,1},{1,0},{2,3},{3,2},{4,5},{5,4},{6,7},{7,6},{8,9},{9,8},{10,11... | collective-permute-start | bytes 835592 | tf_op jit(solution)/shard_map/ppermute | solution.py:19
  12.3 9.5 %collective-permute-start.1 = (bf16[704,128]{1,0:T(8,128)(2,1)S(1)}, bf16[704,128]{1,0:T(8,128)(2,1)S(1)}, u32[]{:S(2)}, u32[]{:S(2)}) collective-permute-start(bf16[704,128]{1,0:T(8,128)(2,1)S(1)} %get-tuple-element.19.refs_0_), channel_id=1, source_target_pairs={{0,4},{4,0},{8,12},{12,8},{16,20},{20,16},{24,28},{28,24},{1,5},{5... | collective-permute-start | bytes 540680 | tf_op jit(solution)/shard_map/ppermute | solution.py:19
  12.6 9.2 %collective-permute-start.7 = (bf16[352,128]{1,0:T(8,128)(2,1)S(1)}, bf16[352,128]{1,0:T(8,128)(2,1)S(1)}, u32[]{:S(2)}, u32[]{:S(2)}) collective-permute-start(bf16[352,128]{1,0:T(8,128)(2,1)S(1)} %collective-permute-done.6.refs_6_), channel_id=1, source_target_pairs={{0,1},{1,0},{2,3},{3,2},{4,5},{5,4},{6,7},{7,6},{8,9},{9,8},{10,11... | collective-permute-start | bytes 270344 | tf_op jit(solution)/shard_map/ppermute | solution.py:19
  13.0 10.0 %collective-permute-start.5 = (bf16[704,128]{1,0:T(8,128)(2,1)S(1)}, bf16[704,128]{1,0:T(8,128)(2,1)S(1)}, u32[]{:S(2)}, u32[]{:S(2)}) collective-permute-start(bf16[704,128]{1,0:T(8,128)(2,1)S(1)} %collective-permute-done.4.refs_4_), channel_id=1, source_target_pairs={{0,4},{4,0},{8,12},{12,8},{16,20},{20,16},{24,28},{28,24},{1,5},{5... | collective-permute-start | bytes 540680 | tf_op jit(solution)/shard_map/ppermute | solution.py:19
  13.1 10.0 %collective-permute-start.3 = (bf16[704,128]{1,0:T(8,128)(2,1)S(1)}, bf16[704,128]{1,0:T(8,128)(2,1)S(1)}, u32[]{:S(2)}, u32[]{:S(2)}) collective-permute-start(bf16[704,128]{1,0:T(8,128)(2,1)S(1)} %collective-permute-done.2.refs_2_), channel_id=1, source_target_pairs={{0,4},{4,0},{8,12},{12,8},{16,20},{20,16},{24,28},{28,24},{1,5},{5... | collective-permute-start | bytes 540680 | tf_op jit(solution)/shard_map/ppermute | solution.py:19
  21.8 1.3 %collective-permute-start.9 = (bf16[352,128]{1,0:T(8,128)(2,1)S(1)}, bf16[352,128]{1,0:T(8,128)(2,1)S(1)}, u32[]{:S(2)}, u32[]{:S(2)}) collective-permute-start(bf16[352,128]{1,0:T(8,128)(2,1)S(1)} %collective-permute-done.7.refs_7_), channel_id=1, source_target_pairs={{0,4},{4,0},{8,12},{12,8},{16,20},{20,16},{24,28},{28,24},{1,5},{5... | collective-permute-start | bytes 270344 | tf_op jit(solution)/shard_map/ppermute | solution.py:19
  25.3 4.3 %collective-permute-start.10 = (f32[64,256]{1,0:T(8,128)S(1)}, f32[64,256]{1,0:T(8,128)S(1)}, u32[]{:S(2)}, u32[]{:S(2)}) collective-permute-start(f32[64,256]{1,0:T(8,128)S(1)} %get-tuple-element.23), channel_id=1, source_target_pairs={{0,1},{1,0},{2,3},{3,2},{4,5},{5,4},{6,7},{7,6},{8,9},{9,8},{10,11... | collective-permute-start | bytes 196616 | tf_op jit(solution)/shard_map/ppermute | solution.py:19
  29.6 8.8 %collective-permute-start.11 = (f32[2,64,256]{2,1,0:T(8,128)S(1)}, f32[2,64,256]{2,1,0:T(8,128)S(1)}, u32[]{:S(2)}, u32[]{:S(2)}) collective-permute-start(f32[2,64,256]{2,1,0:T(8,128)S(1)} %pad_maximum_fusion.refs_0_), channel_id=1, source_target_pairs={{0,2},{1,3},{2,0},{3,1},{4,6},{5,7},{6,4},{7,5},{8,10},{9,11},{10,... | collective-permute-start | bytes 393224 | tf_op jit(solution)/shard_map/ppermute | solution.py:19
  38.6 3.6 %collective-permute-start.12 = (f32[1,128]{1,0:T(1,128)S(1)}, f32[1,128]{1,0:T(1,128)S(1)}, u32[]{:S(2)}, u32[]{:S(2)}) collective-permute-start(f32[1,128]{1,0:T(1,128)S(1)} %row_losses.1), channel_id=1, source_target_pairs={{0,1},{1,0},{2,3},{3,2},{4,5},{5,4},{6,7},{7,6},{8,9},{9,8},{10,11... | collective-permute-start | bytes 1544 | tf_op jit(solution)/shard_map/ppermute | solution.py:19

commit v4 on v3

--- a/solution.py
+++ b/solution.py
@@ -125,20 +125,20 @@
 
 def block_kernel(sizes, keep, order_ref, seg_ref, bias_ref, query_ref, *refs):
     n_ctx, half, reach, key_width, idim = sizes
-    n_index = 2 if keep else 0
-    index_query_refs, refs = refs[:n_index], refs[n_index:]
+    index_query_refs, refs = refs[:1], refs[1:]
     if keep:
         stack_ref, refs = refs[0], refs[1:]
     else:
         piece_refs, half_refs, refs = refs[: n_ctx - 2], refs[n_ctx - 2 : n_ctx + 2], refs[n_ctx + 2 :]
-    out_refs, refs = refs[:2], refs[2:]
+    out_ref, refs = refs[0], refs[1:]
+    if not keep:
+        stack_ref, refs = refs[0], refs[1:]
     main_ref, tail_ref, index_main, index_tail, raw_ref, index_raw, main_raw, inverse_ref = refs
     key_pad = main_ref.shape[1]
     me = lax.axis_index("ctx")
     mine = own_block(keep)
     rows_here = block_rows(keep, half)
     if not keep:
-        stack_ref = out_refs[1]
         bit = own_block(True)
         for s in range(n_ctx - 2):
             stack_ref[me ^ s] = piece_refs[s][...]
@@ -192,9 +192,8 @@
     def index_lhs(ref):
         return jnp.concatenate([ref[:, j * idim : (j + 1) * idim] for j in range(ref.shape[1] // idim - 1)], axis=0)
 
-    if keep:
-        for w in range(reach_blocks):
-            index_keys_into(index_main, w, w * half)
+    for w in range(reach_blocks):
+        index_keys_into(index_main, w, w * half)
 
     @pl.when(needed)
     def _():
@@ -205,13 +204,12 @@
             raw_ref[parity] = lax.dot_general(
                 stacked_queries[parity](), tail_ref[parity], (((1,), (0,)), ((), ())), preferred_element_type=jnp.float32
             )
-        if keep:
-            index_keys_into(index_tail, reach_blocks, 0)
-            index_tail[half:, :] = jnp.zeros((LANES - half, idim), index_tail.dtype)
-            for k, ref in enumerate(index_query_refs):
-                index_raw[k] = lax.dot_general(
-                    index_lhs(ref), index_tail[...], (((1,), (1,)), ((), ())), preferred_element_type=jnp.float32
-                )
+        index_keys_into(index_tail, reach_blocks, 0)
+        index_tail[half:, :] = jnp.zeros((LANES - half, idim), index_tail.dtype)
+        for k, ref in enumerate(index_query_refs):
+            index_raw[k] = lax.dot_general(
+                index_lhs(ref), index_tail[...], (((1,), (1,)), ((), ())), preferred_element_type=jnp.float32
+            )
 
     groups = 2 * max(1, heads // 2 // 4)
     each = heads // groups
@@ -240,19 +238,18 @@
         if k < groups:
             matmul(k)
         total = softmax(k - 1, total)
-    out_refs[0][...] = total
-
-    if keep:
-        total = jnp.zeros((half, reach), jnp.float32)
-        for k, ref in enumerate(index_query_refs):
-            lhs = index_lhs(ref)
-            dots = lax.dot_general(lhs, index_main[...], (((1,), (1,)), ((), ())), preferred_element_type=jnp.float32)
-            gains = ref[:, lhs.shape[0] // half * idim :].astype(jnp.float32)
-            for j in range(lhs.shape[0] // half):
-                here = slice(j * half, (j + 1) * half)
-                folded = ring_fold(own_low, dots[here, :], index_raw[k, here, :])
-                total = total + gains[:, j : j + 1] * jnp.maximum(folded, 0.0)
-        out_refs[1][...] = jnp.where(bias == 0.0, total, 0.0)
+    out_ref[0] = total
+
+    total = jnp.zeros((half, reach), jnp.float32)
+    for k, ref in enumerate(index_query_refs):
+        lhs = index_lhs(ref)
+        dots = lax.dot_general(lhs, index_main[...], (((1,), (1,)), ((), ())), preferred_element_type=jnp.float32)
+        gains = ref[:, lhs.shape[0] // half * idim :].astype(jnp.float32)
+        for j in range(lhs.shape[0] // half):
+            here = slice(j * half, (j + 1) * half)
+            folded = ring_fold(own_low, dots[here, :], index_raw[k, here, :])
+            total = total + gains[:, j : j + 1] * jnp.maximum(folded, 0.0)
+    out_ref[1] = jnp.where(bias == 0.0, total, 0.0)
 
 
 def loss_kernel(sizes, bias_ref, *refs):
@@ -342,25 +339,24 @@
         cost_estimate=pl.CostEstimate(flops=1 << 20, bytes_accessed=10 << 20, transcendentals=0),
         name="prelude",
     )(far(block_order), far(seg_table), far(index_weight.T), far(main_query), far(index_query))
-    taken_query = swap(give_query, "head", 1)
 
     stack = jax.ShapeDtypeStruct((n_ctx, key_width + idim, rows), packed.dtype)
 
     def block_sums(keep, keys):
-        sums = jax.ShapeDtypeStruct((half, reach), jnp.float32)
-        index_queries = [keep_query, taken_query] if keep else []
+        sums = jax.ShapeDtypeStruct((2, half, reach), jnp.float32)
+        index_query_here = keep_query if keep else give_query
         return pl.pallas_call(
             functools.partial(block_kernel, (n_ctx, half, reach, key_width, idim), keep),
-            out_shape=(sums, sums) if keep else (sums, stack),
-            in_specs=[smem, smem] + [vmem] * (2 + len(index_queries) + len(keys)),
-            out_specs=(vmem, vmem),
+            out_shape=sums if keep else (sums, stack),
+            in_specs=[smem, smem] + [vmem] * (3 + len(keys)),
+            out_specs=vmem if keep else (vmem, vmem),
             scratch_shapes=[
                 pltpu.VMEM((2, key_pad, reach), jnp.bfloat16),
                 pltpu.VMEM((2, key_pad, LANES), jnp.bfloat16),
                 pltpu.VMEM((reach, idim), jnp.bfloat16),
                 pltpu.VMEM((LANES, idim), jnp.bfloat16),
                 pltpu.VMEM((2, heads // 2 * half, LANES), jnp.float32),
-                pltpu.VMEM((2, index_heads * half, LANES), jnp.float32),
+                pltpu.VMEM((1, index_heads * half, LANES), jnp.float32),
                 pltpu.VMEM((2, min(4, heads // 2) * half, reach), jnp.float32),
                 pltpu.SMEM((block_order.shape[0],), jnp.int32),
             ],
@@ -369,11 +365,11 @@
                 flops=2 * half * reach * heads * key_pad, bytes_accessed=4 << 20, transcendentals=0
             ),
             name="keep_sums" if keep else "give_sums",
-        )(block_order, segment_ids, bias, near_query, *index_queries, *keys)
+        )(block_order, segment_ids, bias, near_query, index_query_here, *keys)
 
     given, key_stack = block_sums(False, pieces)
-    kept, index_sums = block_sums(True, [key_stack])
-    value = jnp.stack([kept + swap(given, "head", 1), index_sums])
+    kept = block_sums(True, [key_stack])
+    value = kept + swap(given, "head", 1)
     distances = [1 << k for k in range(1, n_head.bit_length() - 1)]
     for distance in distances[:-1]:
         value = value + swap(value, "head", distance)

time: 43.5 us -> 40.9 us (0.940); the launches traced: 42.8 us -> 40.7 us
  waiting for transfers between devices: 21.7 us -> 19.5 us
    ppermute x13 -> x12, waiting for transfers between devices: 21.7 us -> 19.5 us  [swap(): return lax.ppermute(x, axis, [(i, i ^ distance) for i in range(size)])]
    ppermute x13 -> x12, starting transfers between devices: 12 us -> 12.1 us  [swap(): return lax.ppermute(x, axis, [(i, i ^ distance) for i in range(size)])]
  transfers between devices with their start and end apart: 13 -> 12, of which waited for: 6 -> 5; matrix products, arithmetic and copies ran while one was open for 0% -> 0% of each run, Pallas kernels for 17% -> 12%
where the time goes in v4:
time: 40.9 us; the launch traced here: 40.7 us
  waiting for transfers between devices  19.5 us (48%)
  starting transfers between devices  12.1 us (30%)
  Pallas kernels  8.43 us (21%)
  other arithmetic  0.53 us (1%)
    ppermute x12, waiting for transfers between devices, swap(): return lax.ppermute(x, axis, [(i, i ^ distance) for i in range(size)])  19.5 us
    ppermute x12, starting transfers between devices, swap(): return lax.ppermute(x, axis, [(i, i ^ distance) for i in range(size)])  12.1 us
    pallas_call x2, Pallas kernels, block_sums(): pl.pallas_call(functools.partial(block_kernel, (n_ctx, half, reach, key_w...  4.53 us
    pallas_call x1, Pallas kernels, per_device(): pl.pallas_call(functools.partial(prelude_kernel, (half, reach, copies)),...  2.61 us
    pallas_call x1, Pallas kernels, per_device(): pl.pallas_call(pack_kernel, out_shape=(jax.ShapeDtypeStruct((key_width +...  1.09 us
  transfers between devices with their start and end apart: 12, of which 5 were waited for; matrix products, arithmetic and copies ran while one was open for 0% of the time, Pallas kernels for 12%

profile of v4, /device:TPU:0, one launch (start us, length us, event | category | flops | bytes accessed | tf_op | source)
XLA Modules:
  0.0 40.7 jit_solution(16360606943064922559)
XLA Ops:
  0.0 0.0 copy-start.1
  0.0 0.0 copy-start
  0.0 1.1 %pack.1 = (bf16[704,128]{1,0:T(8,128)(2,1)S(1)}, bf16[352,128]{1,0:T(8,128)(2,1)S(1)}) custom-call(bf16[576,128]{1,0:T(8,128)(2,1)} %bitcast.6, bf16[128,128]{1,0:T(8,128)(2,1)} %index_hbm.1), custom_call_target="tpu_custom_call" | custom-call | tf_op jit(solution)/shard_map/pack/pallas_call | solution.py:296
  1.1 3.1 %collective-permute-start.3 = (bf16[704,128]{1,0:T(8,128)(2,1)S(1)}, bf16[704,128]{1,0:T(8,128)(2,1)S(1)}, u32[]{:S(2)}, u32[]{:S(2)}) collective-permute-start(bf16[704,128]{1,0:T(8,128)(2,1)S(1)} %get-tuple-element.17.refs_1_), channel_id=1, source_target_pairs={{0,16},{4,20},{8,24},{12,28},{16,0},{20,4},{24,8},{28,12},{1,17},{... | collective-permute-start | bytes 540680 | tf_op jit(solution)/shard_map/ppermute | solution.py:19
  4.2 1.5 %collective-permute-start.1 = (bf16[704,128]{1,0:T(8,128)(2,1)S(1)}, bf16[704,128]{1,0:T(8,128)(2,1)S(1)}, u32[]{:S(2)}, u32[]{:S(2)}) collective-permute-start(bf16[704,128]{1,0:T(8,128)(2,1)S(1)} %get-tuple-element.17.refs_1_), channel_id=1, source_target_pairs={{0,8},{4,12},{8,0},{12,4},{16,24},{20,28},{24,16},{28,20},{1,9},{5... | collective-permute-start | bytes 540680 | tf_op jit(solution)/shard_map/ppermute | solution.py:19
  5.7 0.0 collective-permute-start.5
  5.7 0.0 collective-permute-start
  5.7 6.2 %collective-permute-done.5.refs_7_ = bf16[352,128]{1,0:T(8,128)(2,1)S(1)} collective-permute-done((bf16[352,128]{1,0:T(8,128)(2,1)S(1)}, bf16[352,128]{1,0:T(8,128)(2,1)S(1)}, u32[]{:S(2)}, u32[]{:S(2)}) %collective-permute-start.5) | collective-permute-done | bytes 90144 | tf_op jit(solution)/shard_map/ppermute | solution.py:19
  11.9 1.6 %collective-permute-start.6 = (bf16[352,128]{1,0:T(8,128)(2,1)S(1)}, bf16[352,128]{1,0:T(8,128)(2,1)S(1)}, u32[]{:S(2)}, u32[]{:S(2)}) collective-permute-start(bf16[352,128]{1,0:T(8,128)(2,1)S(1)} %collective-permute-done.5.refs_7_), channel_id=1, source_target_pairs={{0,1},{1,0},{2,3},{3,2},{4,5},{5,4},{6,7},{7,6},{8,9},{9,8},{10,11... | collective-permute-start | bytes 270344 | tf_op jit(solution)/shard_map/ppermute | solution.py:19
  13.5 0.0 collective-permute-done.3.refs_5_
  13.5 0.0 collective-permute-start.4
  13.6 0.0 collective-permute-done.1.refs_3_
  13.6 0.5 %collective-permute-start.2 = (bf16[704,128]{1,0:T(8,128)(2,1)S(1)}, bf16[704,128]{1,0:T(8,128)(2,1)S(1)}, u32[]{:S(2)}, u32[]{:S(2)}) collective-permute-start(bf16[704,128]{1,0:T(8,128)(2,1)S(1)} %collective-permute-done.1.refs_3_), channel_id=1, source_target_pairs={{0,4},{4,0},{8,12},{12,8},{16,20},{20,16},{24,28},{28,24},{1,5},{5... | collective-permute-start | bytes 540680 | tf_op jit(solution)/shard_map/ppermute | solution.py:19
  14.1 0.1 collective-permute-start.7
  14.1 2.3 %collective-permute-done.6.refs_8_ = bf16[352,128]{1,0:T(8,128)(2,1)S(1)} collective-permute-done((bf16[352,128]{1,0:T(8,128)(2,1)S(1)}, bf16[352,128]{1,0:T(8,128)(2,1)S(1)}, u32[]{:S(2)}, u32[]{:S(2)}) %collective-permute-start.6) | collective-permute-done | bytes 90144 | tf_op jit(solution)/shard_map/ppermute | solution.py:19
  16.4 0.0 collective-permute-start.8
  16.4 2.6 %prelude.1 = (f32[2,64,256]{2,1,0:T(8,128)S(1)}, bf16[128,18432]{1,0:T(8,128)(2,1)S(1)}, bf16[64,2176]{1,0:T(8,128)(2,1)S(1)}, bf16[64,2176]{1,0:T(8,128)(2,1)S(1)}) custom-call(s32[16]{0:T(128)} %order_ref.3, s32[8,128]{1,0:T(8,128)} %bitcast.5, bf16[16,128]{1,0:T(8,128)(2,1)} %bitcast.7, bf16[128,18432]{1,0:T(8,128)(2,1)} %query_hbm.1, ...), custom_call_target="tpu_custom_call" | custom-call | flops 1048576 | bytes 10485760 | tf_op jit(solution)/shard_map/prelude/pallas_call | solution.py:322
  19.1 0.0 collective-permute-done.7.refs_9_
  19.1 0.0 collective-permute-done.refs_2_
  19.1 0.0 collective-permute-done.8.refs_10_
  19.1 0.0 collective-permute-done.4.refs_6_
  19.1 0.0 collective-permute-done.2.refs_4_
  19.1 0.0 copy-done.1
  19.1 0.0 copy-done
  19.1 2.3 %give_sums.1 = (f32[2,64,256]{2,1,0:T(8,128)S(1)}, bf16[8,704,128]{2,1,0:T(8,128)(2,1)S(1)}) custom-call(s32[16]{0:T(128)S(1)} %copy-done.1, s32[1024]{0:T(1024)S(1)} %copy-done, f32[2,64,256]{2,1,0:T(8,128)S(1)} %get-tuple-element.13.bias_ref, bf16[128,18432]{1,0:T(8,128)(2,1)S(1)} %get-tuple-element.14.query_ref, ...), custom_call_target="tpu_custom_call" | custom-call | flops 671088640 | bytes 4194304 | tf_op jit(solution)/shard_map/give_sums/pallas_call | solution.py:348
  21.4 1.7 %collective-permute-start.9 = (f32[2,64,256]{2,1,0:T(8,128)S(1)}, f32[2,64,256]{2,1,0:T(8,128)S(1)}, u32[]{:S(2)}, u32[]{:S(2)}) collective-permute-start(f32[2,64,256]{2,1,0:T(8,128)S(1)} %get-tuple-element.20), channel_id=1, source_target_pairs={{0,1},{1,0},{2,3},{3,2},{4,5},{5,4},{6,7},{7,6},{8,9},{9,8},{10,11... | collective-permute-start | bytes 393224 | tf_op jit(solution)/shard_map/ppermute | solution.py:19
  23.1 2.2 %keep_sums.1 = f32[2,64,256]{2,1,0:T(8,128)S(1)} custom-call(s32[16]{0:T(128)S(1)} %copy-done.1, s32[1024]{0:T(1024)S(1)} %copy-done, f32[2,64,256]{2,1,0:T(8,128)S(1)} %get-tuple-element.13.bias_ref, bf16[128,18432]{1,0:T(8,128)(2,1)S(1)} %get-tuple-element.14.query_ref, bf16[64,2176]{1,0:T(8,128)(2,1)S(1)} %get-tuple-element.15.refs_0_, ...), custom_call_target="tpu_custom_call" | custom-call | flops 671088640 | bytes 4194304 | tf_op jit(solution)/shard_map/keep_sums/pallas_call | solution.py:348
  25.4 2.0 %collective-permute-done.9 = f32[2,64,256]{2,1,0:T(8,128)S(1)} collective-permute-done((f32[2,64,256]{2,1,0:T(8,128)S(1)}, f32[2,64,256]{2,1,0:T(8,128)S(1)}, u32[]{:S(2)}, u32[]{:S(2)}) %collective-permute-start.9) | collective-permute-done | bytes 131104 | tf_op jit(solution)/shard_map/ppermute | solution.py:19
  27.4 2.8 %collective-permute-start.10 = (f32[2,64,256]{2,1,0:T(8,128)S(1)}, f32[2,64,256]{2,1,0:T(8,128)S(1)}, u32[]{:S(2)}, u32[]{:S(2)}) collective-permute-start(f32[2,64,256]{2,1,0:T(8,128)S(1)} %add.6.refs_0_), channel_id=1, source_target_pairs={{0,2},{1,3},{2,0},{3,1},{4,6},{5,7},{6,4},{7,5},{8,10},{9,11},{10,... | collective-permute-start | bytes 393224 | tf_op jit(solution)/shard_map/ppermute | solution.py:19
  30.2 6.1 %collective-permute-done.10.refs_1_ = f32[2,64,256]{2,1,0:T(8,128)S(1)} collective-permute-done((f32[2,64,256]{2,1,0:T(8,128)S(1)}, f32[2,64,256]{2,1,0:T(8,128)S(1)}, u32[]{:S(2)}, u32[]{:S(2)}) %collective-permute-start.10) | collective-permute-done | bytes 131104 | tf_op jit(solution)/shard_map/ppermute | solution.py:19
  36.4 0.2 row_losses.1
  36.6 0.8 %collective-permute-start.11 = (f32[1,128]{1,0:T(1,128)S(1)}, f32[1,128]{1,0:T(1,128)S(1)}, u32[]{:S(2)}, u32[]{:S(2)}) collective-permute-start(f32[1,128]{1,0:T(1,128)S(1)} %row_losses.1), channel_id=1, source_target_pairs={{0,1},{1,0},{2,3},{3,2},{4,5},{5,4},{6,7},{7,6},{8,9},{9,8},{10,11... | collective-permute-start | bytes 1544 | tf_op jit(solution)/shard_map/ppermute | solution.py:19
  37.4 2.8 %collective-permute-done.11 = f32[1,128]{1,0:T(1,128)S(1)} collective-permute-done((f32[1,128]{1,0:T(1,128)S(1)}, f32[1,128]{1,0:T(1,128)S(1)}, u32[]{:S(2)}, u32[]{:S(2)}) %collective-permute-start.11) | collective-permute-done | bytes 544 | tf_op jit(solution)/shard_map/ppermute | solution.py:19
  40.2 0.5 %add_bitcast_fusion = f32[128]{0:T(128)} fusion(f32[1,128]{1,0:T(1,128)S(1)} %row_losses.1, f32[1,128]{1,0:T(1,128)S(1)} %collective-permute-done.11), kind=kLoop, calls=%fused_computation | loop fusion | flops 128 | bytes 1536 | tf_op jit(solution)/shard_map/reshape | solution.py:385
  (1 shorter events, 0.0 us)
Async XLA Ops:
  0.0 19.1 %copy-start.1 = (s32[16]{0:T(128)S(1)}, s32[16]{0:T(128)}, u32[]{:S(2)}) copy-start(s32[16]{0:T(128)} %order_ref.3) | copy-start | bytes 196
  0.0 19.1 %copy-start = (s32[1024]{0:T(1024)S(1)}, s32[1024]{0:T(1024)}, u32[]{:S(2)}) copy-start(s32[1024]{0:T(1024)} %seg_ref.3) | copy-start | bytes 12292
  1.1 12.4 %collective-permute-start.3 = (bf16[704,128]{1,0:T(8,128)(2,1)S(1)}, bf16[704,128]{1,0:T(8,128)(2,1)S(1)}, u32[]{:S(2)}, u32[]{:S(2)}) collective-permute-start(bf16[704,128]{1,0:T(8,128)(2,1)S(1)} %get-tuple-element.17.refs_1_), channel_id=1, source_target_pairs={{0,16},{4,20},{8,24},{12,28},{16,0},{20,4},{24,8},{28,12},{1,17},{... | collective-permute-start | bytes 540680 | tf_op jit(solution)/shard_map/ppermute | solution.py:19
  4.2 9.4 %collective-permute-start.1 = (bf16[704,128]{1,0:T(8,128)(2,1)S(1)}, bf16[704,128]{1,0:T(8,128)(2,1)S(1)}, u32[]{:S(2)}, u32[]{:S(2)}) collective-permute-start(bf16[704,128]{1,0:T(8,128)(2,1)S(1)} %get-tuple-element.17.refs_1_), channel_id=1, source_target_pairs={{0,8},{4,12},{8,0},{12,4},{16,24},{20,28},{24,16},{28,20},{1,9},{5... | collective-permute-start | bytes 540680 | tf_op jit(solution)/shard_map/ppermute | solution.py:19
  5.7 6.2 %collective-permute-start.5 = (bf16[352,128]{1,0:T(8,128)(2,1)S(1)}, bf16[352,128]{1,0:T(8,128)(2,1)S(1)}, u32[]{:S(2)}, u32[]{:S(2)}) collective-permute-start(bf16[352,128]{1,0:T(8,128)(2,1)S(1)} %get-tuple-element.18), channel_id=1, source_target_pairs={{0,24},{4,28},{8,16},{12,20},{16,8},{20,12},{24,0},{28,4},{1,25},{... | collective-permute-start | bytes 270344 | tf_op jit(solution)/shard_map/ppermute | solution.py:19
  5.7 13.4 %collective-permute-start = (bf16[704,128]{1,0:T(8,128)(2,1)S(1)}, bf16[704,128]{1,0:T(8,128)(2,1)S(1)}, u32[]{:S(2)}, u32[]{:S(2)}) collective-permute-start(bf16[704,128]{1,0:T(8,128)(2,1)S(1)} %get-tuple-element.17.refs_1_), channel_id=1, source_target_pairs={{0,4},{4,0},{8,12},{12,8},{16,20},{20,16},{24,28},{28,24},{1,5},{5... | collective-permute-start | bytes 540680 | tf_op jit(solution)/shard_map/ppermute | solution.py:19
  11.9 4.5 %collective-permute-start.6 = (bf16[352,128]{1,0:T(8,128)(2,1)S(1)}, bf16[352,128]{1,0:T(8,128)(2,1)S(1)}, u32[]{:S(2)}, u32[]{:S(2)}) collective-permute-start(bf16[352,128]{1,0:T(8,128)(2,1)S(1)} %collective-permute-done.5.refs_7_), channel_id=1, source_target_pairs={{0,1},{1,0},{2,3},{3,2},{4,5},{5,4},{6,7},{7,6},{8,9},{9,8},{10,11... | collective-permute-start | bytes 270344 | tf_op jit(solution)/shard_map/ppermute | solution.py:19
  13.5 5.5 %collective-permute-start.4 = (bf16[704,128]{1,0:T(8,128)(2,1)S(1)}, bf16[704,128]{1,0:T(8,128)(2,1)S(1)}, u32[]{:S(2)}, u32[]{:S(2)}) collective-permute-start(bf16[704,128]{1,0:T(8,128)(2,1)S(1)} %collective-permute-done.3.refs_5_), channel_id=1, source_target_pairs={{0,4},{4,0},{8,12},{12,8},{16,20},{20,16},{24,28},{28,24},{1,5},{5... | collective-permute-start | bytes 540680 | tf_op jit(solution)/shard_map/ppermute | solution.py:19
  13.6 5.5 %collective-permute-start.2 = (bf16[704,128]{1,0:T(8,128)(2,1)S(1)}, bf16[704,128]{1,0:T(8,128)(2,1)S(1)}, u32[]{:S(2)}, u32[]{:S(2)}) collective-permute-start(bf16[704,128]{1,0:T(8,128)(2,1)S(1)} %collective-permute-done.1.refs_3_), channel_id=1, source_target_pairs={{0,4},{4,0},{8,12},{12,8},{16,20},{20,16},{24,28},{28,24},{1,5},{5... | collective-permute-start | bytes 540680 | tf_op jit(solution)/shard_map/ppermute | solution.py:19
  14.1 5.0 %collective-permute-start.7 = (bf16[352,128]{1,0:T(8,128)(2,1)S(1)}, bf16[352,128]{1,0:T(8,128)(2,1)S(1)}, u32[]{:S(2)}, u32[]{:S(2)}) collective-permute-start(bf16[352,128]{1,0:T(8,128)(2,1)S(1)} %collective-permute-done.5.refs_7_), channel_id=1, source_target_pairs={{0,4},{4,0},{8,12},{12,8},{16,20},{20,16},{24,28},{28,24},{1,5},{5... | collective-permute-start | bytes 270344 | tf_op jit(solution)/shard_map/ppermute | solution.py:19
  16.4 2.6 %collective-permute-start.8 = (bf16[352,128]{1,0:T(8,128)(2,1)S(1)}, bf16[352,128]{1,0:T(8,128)(2,1)S(1)}, u32[]{:S(2)}, u32[]{:S(2)}) collective-permute-start(bf16[352,128]{1,0:T(8,128)(2,1)S(1)} %collective-permute-done.6.refs_8_), channel_id=1, source_target_pairs={{0,4},{4,0},{8,12},{12,8},{16,20},{20,16},{24,28},{28,24},{1,5},{5... | collective-permute-start | bytes 270344 | tf_op jit(solution)/shard_map/ppermute | solution.py:19
  21.4 6.0 %collective-permute-start.9 = (f32[2,64,256]{2,1,0:T(8,128)S(1)}, f32[2,64,256]{2,1,0:T(8,128)S(1)}, u32[]{:S(2)}, u32[]{:S(2)}) collective-permute-start(f32[2,64,256]{2,1,0:T(8,128)S(1)} %get-tuple-element.20), channel_id=1, source_target_pairs={{0,1},{1,0},{2,3},{3,2},{4,5},{5,4},{6,7},{7,6},{8,9},{9,8},{10,11... | collective-permute-start | bytes 393224 | tf_op jit(solution)/shard_map/ppermute | solution.py:19
  27.4 8.9 %collective-permute-start.10 = (f32[2,64,256]{2,1,0:T(8,128)S(1)}, f32[2,64,256]{2,1,0:T(8,128)S(1)}, u32[]{:S(2)}, u32[]{:S(2)}) collective-permute-start(f32[2,64,256]{2,1,0:T(8,128)S(1)} %add.6.refs_0_), channel_id=1, source_target_pairs={{0,2},{1,3},{2,0},{3,1},{4,6},{5,7},{6,4},{7,5},{8,10},{9,11},{10,... | collective-permute-start | bytes 393224 | tf_op jit(solution)/shard_map/ppermute | solution.py:19
  36.6 3.6 %collective-permute-start.11 = (f32[1,128]{1,0:T(1,128)S(1)}, f32[1,128]{1,0:T(1,128)S(1)}, u32[]{:S(2)}, u32[]{:S(2)}) collective-permute-start(f32[1,128]{1,0:T(1,128)S(1)} %row_losses.1), channel_id=1, source_target_pairs={{0,1},{1,0},{2,3},{3,2},{4,5},{5,4},{6,7},{7,6},{8,9},{9,8},{10,11... | collective-permute-start | bytes 1544 | tf_op jit(solution)/shard_map/ppermute | solution.py:19

commit v5 on v2

--- a/solution.py
+++ b/solution.py
@@ -255,7 +255,7 @@
 
 
 def loss_kernel(sizes, bias_ref, *refs):
-    half, total_heads = sizes
+    half, total_heads, across = sizes
     value_refs, out_ref = refs[:-1], refs[-1]
     mine = own_block(True)
     visible = bias_ref[mine] == 0.0
@@ -273,7 +273,9 @@
     rows = out_ref.shape[1]
     row_id = lax.broadcasted_iota(jnp.int32, (half, rows), 0)
     lane_id = lax.broadcasted_iota(jnp.int32, (half, rows), 1)
-    out_ref[...] = jnp.sum(jnp.where(row_id + mine * half == lane_id, column, 0.0), axis=0, keepdims=True)
+    owner = mine != (lax.axis_index("head") // across) & 1
+    place = (row_id + mine * half == lane_id) & owner
+    out_ref[...] = jnp.sum(jnp.where(place, column, 0.0), axis=0, keepdims=True)
 
 
 def per_device(
@@ -376,16 +378,19 @@
     distances = [1 << k for k in range(1, n_head.bit_length() - 1)]
     for distance in distances[:-1]:
         value = value + swap(value, "head", distance)
-    values = [value] + [swap(value, "head", distance) for distance in distances[-1:]]
+    across = distances[-1]
+    owners = [i for i in range(n_head) if i & 1 != (i // across) & 1]
+    values = [value, lax.ppermute(value, "head", [(i ^ across, i) for i in owners])]
     loss = pl.pallas_call(
-        functools.partial(loss_kernel, (half, heads * n_head)),
+        functools.partial(loss_kernel, (half, heads * n_head, across)),
         out_shape=jax.ShapeDtypeStruct((1, rows), jnp.float32),
         in_specs=[vmem] * (1 + len(values)),
         out_specs=vmem,
         compiler_params=pltpu.CompilerParams(vmem_limit_bytes=8 << 20),
         name="row_losses",
     )(bias, *values)
-    return (loss + swap(loss, "head", 1)).reshape(rows)
+    loss = loss + lax.ppermute(loss, "head", [(i, i ^ across ^ 1) for i in owners])
+    return (loss + lax.ppermute(loss, "head", [(i, i ^ 1) for i in owners])).reshape(rows)
 
 
 def solution(mesh):

time: 43.4 us -> 48.5 us (1.12)
  starting transfers between devices: 12 us -> 15.6 us
  waiting for transfers between devices: 21.7 us -> 23.2 us
    ppermute x0 -> x3, waiting for transfers between devices: none -> 11.1 us  [the longest x1 8.55 us: per_device(): lax.ppermute(loss, 'head', [(i, i ^ 1) for i in owners])]
    ppermute x13 -> x11, waiting for transfers between devices: 21.7 us -> 12.1 us  [swap(): return lax.ppermute(x, axis, [(i, i ^ distance) for i in range(size)])]
    ppermute x0 -> x3, starting transfers between devices: none -> 6.52 us  [the longest x1 4.56 us: per_device(): lax.ppermute(value, 'head', [(i ^ across, i) for i in owners])]
    ppermute x13 -> x11, starting transfers between devices: 12 us -> 9.1 us  [swap(): return lax.ppermute(x, axis, [(i, i ^ distance) for i in range(size)])]
  transfers between devices with their start and end apart: 13 -> 14, of which waited for: 6 -> 6; matrix products, arithmetic and copies ran while one was open for 0% -> 0% of each run, Pallas kernels for 17% -> 15%
where the time goes in v5:
time: 48.5 us; the launch traced here: 47.9 us
  waiting for transfers between devices  23.2 us (48%)
  starting transfers between devices  15.6 us (32%)
  Pallas kernels  8.44 us (17%)
  other arithmetic  0.54 us (1%)
    ppermute x11, waiting for transfers between devices, swap(): return lax.ppermute(x, axis, [(i, i ^ distance) for i in range(size)])  12.1 us
    ppermute x11, starting transfers between devices, swap(): return lax.ppermute(x, axis, [(i, i ^ distance) for i in range(size)])  9.1 us
    ppermute x1, waiting for transfers between devices, per_device(): lax.ppermute(loss, 'head', [(i, i ^ 1) for i in owners])  8.55 us
    pallas_call x2, Pallas kernels, block_sums(): pl.pallas_call(functools.partial(block_kernel, (n_ctx, half, reach, key_w...  4.59 us
    ppermute x1, starting transfers between devices, per_device(): lax.ppermute(value, 'head', [(i ^ across, i) for i in owners])  4.56 us
    pallas_call x1, Pallas kernels, per_device(): pl.pallas_call(functools.partial(prelude_kernel, (half, reach, copies)),...  2.61 us
    ppermute x1, waiting for transfers between devices, per_device(): lax.ppermute(value, 'head', [(i ^ across, i) for i in owners])  2.5 us
    ppermute x1, starting transfers between devices, per_device(): lax.ppermute(loss, 'head', [(i, i ^ 1) for i in owners])  1.29 us
  transfers between devices with their start and end apart: 14, of which 6 were waited for; matrix products, arithmetic and copies ran while one was open for 0% of the time, Pallas kernels for 15%

profile of v5, /device:TPU:0, one launch (start us, length us, event | category | flops | bytes accessed | tf_op | source)
XLA Modules:
  0.0 47.9 jit_solution(17263906665898510918)
XLA Ops:
  0.0 0.0 copy-start.1
  0.0 0.0 copy-start
  0.0 1.0 %pack.1 = (bf16[704,128]{1,0:T(8,128)(2,1)S(1)}, bf16[352,128]{1,0:T(8,128)(2,1)S(1)}) custom-call(bf16[576,128]{1,0:T(8,128)(2,1)} %bitcast.10, bf16[128,128]{1,0:T(8,128)(2,1)} %index_hbm.1), custom_call_target="tpu_custom_call" | custom-call | tf_op jit(solution)/shard_map/pack/pallas_call | solution.py:300
  1.1 4.0 %collective-permute-start.6 = (bf16[352,128]{1,0:T(8,128)(2,1)S(1)}, bf16[352,128]{1,0:T(8,128)(2,1)S(1)}, u32[]{:S(2)}, u32[]{:S(2)}) collective-permute-start(bf16[352,128]{1,0:T(8,128)(2,1)S(1)} %get-tuple-element.20), channel_id=1, source_target_pairs={{0,24},{4,28},{8,16},{12,20},{16,8},{20,12},{24,0},{28,4},{1,25},{... | collective-permute-start | bytes 270344 | tf_op jit(solution)/shard_map/ppermute | solution.py:19
  5.0 0.5 %collective-permute-start.4 = (bf16[704,128]{1,0:T(8,128)(2,1)S(1)}, bf16[704,128]{1,0:T(8,128)(2,1)S(1)}, u32[]{:S(2)}, u32[]{:S(2)}) collective-permute-start(bf16[704,128]{1,0:T(8,128)(2,1)S(1)} %get-tuple-element.19.refs_0_), channel_id=1, source_target_pairs={{0,16},{4,20},{8,24},{12,28},{16,0},{20,4},{24,8},{28,12},{1,17},{... | collective-permute-start | bytes 540680 | tf_op jit(solution)/shard_map/ppermute | solution.py:19
  5.5 0.1 collective-permute-start.2
  5.7 2.4 %collective-permute-done.6.refs_6_ = bf16[352,128]{1,0:T(8,128)(2,1)S(1)} collective-permute-done((bf16[352,128]{1,0:T(8,128)(2,1)S(1)}, bf16[352,128]{1,0:T(8,128)(2,1)S(1)}, u32[]{:S(2)}, u32[]{:S(2)}) %collective-permute-start.6) | collective-permute-done | bytes 90144 | tf_op jit(solution)/shard_map/ppermute | solution.py:19
  8.1 0.0 collective-permute-start.8
  8.1 2.6 %prelude.1 = (f32[2,64,256]{2,1,0:T(8,128)S(1)}, bf16[128,18432]{1,0:T(8,128)(2,1)S(1)}, bf16[64,2176]{1,0:T(8,128)(2,1)S(1)}, bf16[64,2176]{1,0:T(8,128)(2,1)S(1)}) custom-call(s32[16]{0:T(128)} %order_ref.3, s32[8,128]{1,0:T(8,128)} %bitcast.9, bf16[16,128]{1,0:T(8,128)(2,1)} %bitcast.11, bf16[128,18432]{1,0:T(8,128)(2,1)} %query_hbm.1, ...), custom_call_target="tpu_custom_call" | custom-call | flops 1048576 | bytes 10485760 | tf_op jit(solution)/shard_map/prelude/pallas_call | solution.py:326
  10.7 1.6 %collective-permute-start = (bf16[64,2176]{1,0:T(8,128)(2,1)S(1)}, bf16[64,2176]{1,0:T(8,128)(2,1)S(1)}, u32[]{:S(2)}, u32[]{:S(2)}) collective-permute-start(bf16[64,2176]{1,0:T(8,128)(2,1)S(1)} %get-tuple-element.18), channel_id=1, source_target_pairs={{0,1},{1,0},{2,3},{3,2},{4,5},{5,4},{6,7},{7,6},{8,9},{9,8},{10,11... | collective-permute-start | bytes 835592 | tf_op jit(solution)/shard_map/ppermute | solution.py:19
  12.3 0.2 collective-permute-start.1
  12.5 0.0 collective-permute-done.8.refs_8_
  12.5 0.5 collective-permute-start.7
  13.0 0.0 collective-permute-done.4.refs_4_
  13.0 0.0 collective-permute-start.5
  13.0 0.0 collective-permute-done.2.refs_2_
  13.0 0.5 %collective-permute-start.3 = (bf16[704,128]{1,0:T(8,128)(2,1)S(1)}, bf16[704,128]{1,0:T(8,128)(2,1)S(1)}, u32[]{:S(2)}, u32[]{:S(2)}) collective-permute-start(bf16[704,128]{1,0:T(8,128)(2,1)S(1)} %collective-permute-done.2.refs_2_), channel_id=1, source_target_pairs={{0,4},{4,0},{8,12},{12,8},{16,20},{20,16},{24,28},{28,24},{1,5},{5... | collective-permute-start | bytes 540680 | tf_op jit(solution)/shard_map/ppermute | solution.py:19
  13.5 8.2 %collective-permute-done.7.refs_7_ = bf16[352,128]{1,0:T(8,128)(2,1)S(1)} collective-permute-done((bf16[352,128]{1,0:T(8,128)(2,1)S(1)}, bf16[352,128]{1,0:T(8,128)(2,1)S(1)}, u32[]{:S(2)}, u32[]{:S(2)}) %collective-permute-start.7) | collective-permute-done | bytes 90144 | tf_op jit(solution)/shard_map/ppermute | solution.py:19
  21.7 0.0 collective-permute-start.9
  21.7 0.0 collective-permute-done.1.refs_1_
  21.7 1.3 %collective-permute-done.9.refs_9_ = bf16[352,128]{1,0:T(8,128)(2,1)S(1)} collective-permute-done((bf16[352,128]{1,0:T(8,128)(2,1)S(1)}, bf16[352,128]{1,0:T(8,128)(2,1)S(1)}, u32[]{:S(2)}, u32[]{:S(2)}) %collective-permute-start.9) | collective-permute-done | bytes 90144 | tf_op jit(solution)/shard_map/ppermute | solution.py:19
  23.0 0.0 collective-permute-done.5.refs_5_
  23.0 0.0 collective-permute-done.3.refs_3_
  23.0 0.0 copy-done.1
  23.0 0.0 copy-done
  23.0 2.2 %give_sums.1 = (f32[64,256]{1,0:T(8,128)S(1)}, bf16[8,704,128]{2,1,0:T(8,128)(2,1)S(1)}) custom-call(s32[16]{0:T(128)S(1)} %copy-done.1, s32[1024]{0:T(1024)S(1)} %copy-done, f32[2,64,256]{2,1,0:T(8,128)S(1)} %get-tuple-element.15.bias_ref, bf16[128,18432]{1,0:T(8,128)(2,1)S(1)} %get-tuple-element.16.query_ref, ...), custom_call_target="tpu_custom_call" | custom-call | flops 671088640 | bytes 4194304 | tf_op jit(solution)/shard_map/give_sums/pallas_call | solution.py:353
  25.2 1.6 %collective-permute-start.10 = (f32[64,256]{1,0:T(8,128)S(1)}, f32[64,256]{1,0:T(8,128)S(1)}, u32[]{:S(2)}, u32[]{:S(2)}) collective-permute-start(f32[64,256]{1,0:T(8,128)S(1)} %get-tuple-element.23), channel_id=1, source_target_pairs={{0,1},{1,0},{2,3},{3,2},{4,5},{5,4},{6,7},{7,6},{8,9},{9,8},{10,11... | collective-permute-start | bytes 196616 | tf_op jit(solution)/shard_map/ppermute | solution.py:19
  26.9 0.0 collective-permute-done.refs_1_
  26.9 2.4 %keep_sums.1 = (f32[64,256]{1,0:T(8,128)S(1)}, f32[64,256]{1,0:T(8,128)S(1)}) custom-call(s32[16]{0:T(128)S(1)} %copy-done.1, s32[1024]{0:T(1024)S(1)} %copy-done, f32[2,64,256]{2,1,0:T(8,128)S(1)} %get-tuple-element.15.bias_ref, bf16[128,18432]{1,0:T(8,128)(2,1)S(1)} %get-tuple-element.16.query_ref, bf16[64,2176]{1,0:T(8,128)(2,1)S(1)} %get-tuple-element.17.refs_0_, ...), custom_call_target="tpu_custom_call" | custom-call | flops 671088640 | bytes 4194304 | tf_op jit(solution)/shard_map/keep_sums/pallas_call | solution.py:353
  29.3 0.3 collective-permute-done.10
  29.6 4.6 %collective-permute-start.11 = (f32[2,64,256]{2,1,0:T(8,128)S(1)}, f32[2,64,256]{2,1,0:T(8,128)S(1)}, u32[]{:S(2)}, u32[]{:S(2)}) collective-permute-start(f32[2,64,256]{2,1,0:T(8,128)S(1)} %pad_maximum_fusion.refs_0_), channel_id=1, source_target_pairs={{3,1},{0,2},{7,5},{4,6},{11,9},{8,10},{15,13},{12,14},{19,17},{16,... | collective-permute-start | bytes 393224 | tf_op jit(solution)/shard_map/ppermute | solution.py:383
  34.2 2.5 %collective-permute-done.11.refs_1_ = f32[2,64,256]{2,1,0:T(8,128)S(1)} collective-permute-done((f32[2,64,256]{2,1,0:T(8,128)S(1)}, f32[2,64,256]{2,1,0:T(8,128)S(1)}, u32[]{:S(2)}, u32[]{:S(2)}) %collective-permute-start.11) | collective-permute-done | bytes 131104 | tf_op jit(solution)/shard_map/ppermute | solution.py:383
  36.6 0.2 row_losses.1
  36.8 0.7 %collective-permute-start.12 = (f32[1,128]{1,0:T(1,128)S(1)}, f32[1,128]{1,0:T(1,128)S(1)}, u32[]{:S(2)}, u32[]{:S(2)}) collective-permute-start(f32[1,128]{1,0:T(1,128)S(1)} %row_losses.1), channel_id=1, source_target_pairs={{1,2},{2,1},{5,6},{6,5},{9,10},{10,9},{13,14},{14,13},{17,18},{18,... | collective-permute-start | bytes 1544 | tf_op jit(solution)/shard_map/ppermute | solution.py:392
  37.5 0.0 collective-permute-done.12
  37.5 1.3 %collective-permute-start.13 = (f32[1,128]{1,0:T(1,128)S(1)}, f32[1,128]{1,0:T(1,128)S(1)}, u32[]{:S(2)}, u32[]{:S(2)}) collective-permute-start(f32[1,128]{1,0:T(1,128)S(1)} %add.10), channel_id=1, source_target_pairs={{1,0},{2,3},{5,4},{6,7},{9,8},{10,11},{13,12},{14,15},{17,16},{18,... | collective-permute-start | bytes 1544 | tf_op jit(solution)/shard_map/ppermute | solution.py:393
  38.8 8.6 %collective-permute-done.13 = f32[1,128]{1,0:T(1,128)S(1)} collective-permute-done((f32[1,128]{1,0:T(1,128)S(1)}, f32[1,128]{1,0:T(1,128)S(1)}, u32[]{:S(2)}, u32[]{:S(2)}) %collective-permute-start.13) | collective-permute-done | bytes 544 | tf_op jit(solution)/shard_map/ppermute | solution.py:393
  47.4 0.5 %add_bitcast_fusion.1 = f32[128]{0:T(128)} fusion(f32[1,128]{1,0:T(1,128)S(1)} %add.10, f32[1,128]{1,0:T(1,128)S(1)} %collective-permute-done.13), kind=kLoop, calls=%fused_computation.2 | loop fusion | flops 128 | bytes 1536 | tf_op jit(solution)/shard_map/reshape | solution.py:393
  (3 shorter events, 0.0 us)
Async XLA Ops:
  0.0 23.0 %copy-start.1 = (s32[16]{0:T(128)S(1)}, s32[16]{0:T(128)}, u32[]{:S(2)}) copy-start(s32[16]{0:T(128)} %order_ref.3) | copy-start | bytes 196
  0.0 23.0 %copy-start = (s32[1024]{0:T(1024)S(1)}, s32[1024]{0:T(1024)}, u32[]{:S(2)}) copy-start(s32[1024]{0:T(1024)} %seg_ref.3) | copy-start | bytes 12292
  1.1 7.0 %collective-permute-start.6 = (bf16[352,128]{1,0:T(8,128)(2,1)S(1)}, bf16[352,128]{1,0:T(8,128)(2,1)S(1)}, u32[]{:S(2)}, u32[]{:S(2)}) collective-permute-start(bf16[352,128]{1,0:T(8,128)(2,1)S(1)} %get-tuple-element.20), channel_id=1, source_target_pairs={{0,24},{4,28},{8,16},{12,20},{16,8},{20,12},{24,0},{28,4},{1,25},{... | collective-permute-start | bytes 270344 | tf_op jit(solution)/shard_map/ppermute | solution.py:19
  5.0 8.0 %collective-permute-start.4 = (bf16[704,128]{1,0:T(8,128)(2,1)S(1)}, bf16[704,128]{1,0:T(8,128)(2,1)S(1)}, u32[]{:S(2)}, u32[]{:S(2)}) collective-permute-start(bf16[704,128]{1,0:T(8,128)(2,1)S(1)} %get-tuple-element.19.refs_0_), channel_id=1, source_target_pairs={{0,16},{4,20},{8,24},{12,28},{16,0},{20,4},{24,8},{28,12},{1,17},{... | collective-permute-start | bytes 540680 | tf_op jit(solution)/shard_map/ppermute | solution.py:19
  5.5 7.5 %collective-permute-start.2 = (bf16[704,128]{1,0:T(8,128)(2,1)S(1)}, bf16[704,128]{1,0:T(8,128)(2,1)S(1)}, u32[]{:S(2)}, u32[]{:S(2)}) collective-permute-start(bf16[704,128]{1,0:T(8,128)(2,1)S(1)} %get-tuple-element.19.refs_0_), channel_id=1, source_target_pairs={{0,8},{4,12},{8,0},{12,4},{16,24},{20,28},{24,16},{28,20},{1,9},{5... | collective-permute-start | bytes 540680 | tf_op jit(solution)/shard_map/ppermute | solution.py:19
  8.1 4.5 %collective-permute-start.8 = (bf16[352,128]{1,0:T(8,128)(2,1)S(1)}, bf16[352,128]{1,0:T(8,128)(2,1)S(1)}, u32[]{:S(2)}, u32[]{:S(2)}) collective-permute-start(bf16[352,128]{1,0:T(8,128)(2,1)S(1)} %collective-permute-done.6.refs_6_), channel_id=1, source_target_pairs={{0,4},{4,0},{8,12},{12,8},{16,20},{20,16},{24,28},{28,24},{1,5},{5... | collective-permute-start | bytes 270344 | tf_op jit(solution)/shard_map/ppermute | solution.py:19
  10.7 16.2 %collective-permute-start = (bf16[64,2176]{1,0:T(8,128)(2,1)S(1)}, bf16[64,2176]{1,0:T(8,128)(2,1)S(1)}, u32[]{:S(2)}, u32[]{:S(2)}) collective-permute-start(bf16[64,2176]{1,0:T(8,128)(2,1)S(1)} %get-tuple-element.18), channel_id=1, source_target_pairs={{0,1},{1,0},{2,3},{3,2},{4,5},{5,4},{6,7},{7,6},{8,9},{9,8},{10,11... | collective-permute-start | bytes 835592 | tf_op jit(solution)/shard_map/ppermute | solution.py:19
  12.3 9.4 %collective-permute-start.1 = (bf16[704,128]{1,0:T(8,128)(2,1)S(1)}, bf16[704,128]{1,0:T(8,128)(2,1)S(1)}, u32[]{:S(2)}, u32[]{:S(2)}) collective-permute-start(bf16[704,128]{1,0:T(8,128)(2,1)S(1)} %get-tuple-element.19.refs_0_), channel_id=1, source_target_pairs={{0,4},{4,0},{8,12},{12,8},{16,20},{20,16},{24,28},{28,24},{1,5},{5... | collective-permute-start | bytes 540680 | tf_op jit(solution)/shard_map/ppermute | solution.py:19
  12.5 9.2 %collective-permute-start.7 = (bf16[352,128]{1,0:T(8,128)(2,1)S(1)}, bf16[352,128]{1,0:T(8,128)(2,1)S(1)}, u32[]{:S(2)}, u32[]{:S(2)}) collective-permute-start(bf16[352,128]{1,0:T(8,128)(2,1)S(1)} %collective-permute-done.6.refs_6_), channel_id=1, source_target_pairs={{0,1},{1,0},{2,3},{3,2},{4,5},{5,4},{6,7},{7,6},{8,9},{9,8},{10,11... | collective-permute-start | bytes 270344 | tf_op jit(solution)/shard_map/ppermute | solution.py:19
  13.0 10.0 %collective-permute-start.5 = (bf16[704,128]{1,0:T(8,128)(2,1)S(1)}, bf16[704,128]{1,0:T(8,128)(2,1)S(1)}, u32[]{:S(2)}, u32[]{:S(2)}) collective-permute-start(bf16[704,128]{1,0:T(8,128)(2,1)S(1)} %collective-permute-done.4.refs_4_), channel_id=1, source_target_pairs={{0,4},{4,0},{8,12},{12,8},{16,20},{20,16},{24,28},{28,24},{1,5},{5... | collective-permute-start | bytes 540680 | tf_op jit(solution)/shard_map/ppermute | solution.py:19
  13.0 10.0 %collective-permute-start.3 = (bf16[704,128]{1,0:T(8,128)(2,1)S(1)}, bf16[704,128]{1,0:T(8,128)(2,1)S(1)}, u32[]{:S(2)}, u32[]{:S(2)}) collective-permute-start(bf16[704,128]{1,0:T(8,128)(2,1)S(1)} %collective-permute-done.2.refs_2_), channel_id=1, source_target_pairs={{0,4},{4,0},{8,12},{12,8},{16,20},{20,16},{24,28},{28,24},{1,5},{5... | collective-permute-start | bytes 540680 | tf_op jit(solution)/shard_map/ppermute | solution.py:19
  21.7 1.3 %collective-permute-start.9 = (bf16[352,128]{1,0:T(8,128)(2,1)S(1)}, bf16[352,128]{1,0:T(8,128)(2,1)S(1)}, u32[]{:S(2)}, u32[]{:S(2)}) collective-permute-start(bf16[352,128]{1,0:T(8,128)(2,1)S(1)} %collective-permute-done.7.refs_7_), channel_id=1, source_target_pairs={{0,4},{4,0},{8,12},{12,8},{16,20},{20,16},{24,28},{28,24},{1,5},{5... | collective-permute-start | bytes 270344 | tf_op jit(solution)/shard_map/ppermute | solution.py:19
  25.2 4.3 %collective-permute-start.10 = (f32[64,256]{1,0:T(8,128)S(1)}, f32[64,256]{1,0:T(8,128)S(1)}, u32[]{:S(2)}, u32[]{:S(2)}) collective-permute-start(f32[64,256]{1,0:T(8,128)S(1)} %get-tuple-element.23), channel_id=1, source_target_pairs={{0,1},{1,0},{2,3},{3,2},{4,5},{5,4},{6,7},{7,6},{8,9},{9,8},{10,11... | collective-permute-start | bytes 196616 | tf_op jit(solution)/shard_map/ppermute | solution.py:19
  29.6 7.1 %collective-permute-start.11 = (f32[2,64,256]{2,1,0:T(8,128)S(1)}, f32[2,64,256]{2,1,0:T(8,128)S(1)}, u32[]{:S(2)}, u32[]{:S(2)}) collective-permute-start(f32[2,64,256]{2,1,0:T(8,128)S(1)} %pad_maximum_fusion.refs_0_), channel_id=1, source_target_pairs={{3,1},{0,2},{7,5},{4,6},{11,9},{8,10},{15,13},{12,14},{19,17},{16,... | collective-permute-start | bytes 393224 | tf_op jit(solution)/shard_map/ppermute | solution.py:383
  36.8 0.7 %collective-permute-start.12 = (f32[1,128]{1,0:T(1,128)S(1)}, f32[1,128]{1,0:T(1,128)S(1)}, u32[]{:S(2)}, u32[]{:S(2)}) collective-permute-start(f32[1,128]{1,0:T(1,128)S(1)} %row_losses.1), channel_id=1, source_target_pairs={{1,2},{2,1},{5,6},{6,5},{9,10},{10,9},{13,14},{14,13},{17,18},{18,... | collective-permute-start | bytes 1544 | tf_op jit(solution)/shard_map/ppermute | solution.py:392
  37.5 9.9 %collective-permute-start.13 = (f32[1,128]{1,0:T(1,128)S(1)}, f32[1,128]{1,0:T(1,128)S(1)}, u32[]{:S(2)}, u32[]{:S(2)}) collective-permute-start(f32[1,128]{1,0:T(1,128)S(1)} %add.10), channel_id=1, source_target_pairs={{1,0},{2,3},{5,4},{6,7},{9,8},{10,11},{13,12},{14,15},{17,16},{18,... | collective-permute-start | bytes 1544 | tf_op jit(solution)/shard_map/ppermute | solution.py:393

commit v6 on v2

--- a/solution.py
+++ b/solution.py
@@ -254,11 +254,22 @@
         out_refs[1][...] = jnp.where(bias == 0.0, total, 0.0)
 
 
+def split_kernel(across, kept_ref, taken_ref, index_ref, value_ref, rest_ref):
+    count = value_ref.shape[1]
+    side = (lax.axis_index("head") // across) & 1
+    for at, ref in ((side, value_ref), (1 - side, rest_ref)):
+        here = pl.ds(pl.multiple_of(at * count, count), count)
+        ref[0] = kept_ref[here, :] + taken_ref[here, :]
+        ref[1] = index_ref[here, :]
+
+
 def loss_kernel(sizes, bias_ref, *refs):
-    half, total_heads = sizes
+    half, total_heads, across = sizes
     value_refs, out_ref = refs[:-1], refs[-1]
     mine = own_block(True)
-    visible = bias_ref[mine] == 0.0
+    count = value_refs[0].shape[1]
+    start = ((lax.axis_index("head") // across) & 1) * count
+    visible = bias_ref[mine, pl.ds(pl.multiple_of(start, count), count), :] == 0.0
     target = functools.reduce(jnp.add, [ref[0] for ref in value_refs]) * (1.0 / total_heads)
     index_score = functools.reduce(jnp.add, [ref[1] for ref in value_refs])
     masked = jnp.where(visible, index_score, hidden)
@@ -271,9 +282,10 @@
     target_sum = jnp.sum(target, axis=1, keepdims=True)
     column = entropy_sum - cross_sum + (row_max + jnp.log(exp_sum)) * target_sum
     rows = out_ref.shape[1]
-    row_id = lax.broadcasted_iota(jnp.int32, (half, rows), 0)
-    lane_id = lax.broadcasted_iota(jnp.int32, (half, rows), 1)
-    out_ref[...] = jnp.sum(jnp.where(row_id + mine * half == lane_id, column, 0.0), axis=0, keepdims=True)
+    row_id = lax.broadcasted_iota(jnp.int32, (count, rows), 0)
+    lane_id = lax.broadcasted_iota(jnp.int32, (count, rows), 1)
+    place = row_id + mine * half + start == lane_id
+    out_ref[...] = jnp.sum(jnp.where(place, column, 0.0), axis=0, keepdims=True)
 
 
 def per_device(
@@ -372,19 +384,31 @@
 
     given, key_stack = block_sums(False, pieces)
     kept, index_sums = block_sums(True, [key_stack])
-    value = jnp.stack([kept + swap(given, "head", 1), index_sums])
-    distances = [1 << k for k in range(1, n_head.bit_length() - 1)]
-    for distance in distances[:-1]:
+    across = n_head // 2
+    quarter = jax.ShapeDtypeStruct((2, half // 2, reach), jnp.float32)
+    value, rest = pl.pallas_call(
+        functools.partial(split_kernel, across),
+        out_shape=(quarter, quarter),
+        in_specs=[vmem] * 3,
+        out_specs=(vmem, vmem),
+        compiler_params=pltpu.CompilerParams(vmem_limit_bytes=16 << 20),
+        name="split_rows",
+    )(kept, swap(given, "head", 1), index_sums)
+    distance = 2
+    while distance < across:
         value = value + swap(value, "head", distance)
-    values = [value] + [swap(value, "head", distance) for distance in distances[-1:]]
+        rest = rest + swap(rest, "head", distance)
+        distance *= 2
+    values = [value, swap(rest, "head", across)]
     loss = pl.pallas_call(
-        functools.partial(loss_kernel, (half, heads * n_head)),
+        functools.partial(loss_kernel, (half, heads * n_head, across)),
         out_shape=jax.ShapeDtypeStruct((1, rows), jnp.float32),
         in_specs=[vmem] * (1 + len(values)),
         out_specs=vmem,
         compiler_params=pltpu.CompilerParams(vmem_limit_bytes=8 << 20),
         name="row_losses",
     )(bias, *values)
+    loss = loss + swap(loss, "head", across)
     return (loss + swap(loss, "head", 1)).reshape(rows)
 
 

time: 43.4 us -> 45.2 us (1.041)
  the two profiles are of different devices: /device:TPU:0 before, /device:TPU:6 now
where the time goes in v6:
time: 45.2 us; the launch traced here: 45.1 us
  waiting for transfers between devices  23.2 us (51%)
  starting transfers between devices  12.8 us (28%)
  Pallas kernels  8.46 us (19%)
  other arithmetic  0.52 us (1%)
    ppermute x14, waiting for transfers between devices, swap(): return lax.ppermute(x, axis, [(i, i ^ distance) for i in range(size)])  23.2 us
    ppermute x14, starting transfers between devices, swap(): return lax.ppermute(x, axis, [(i, i ^ distance) for i in range(size)])  12.8 us
    pallas_call x2, Pallas kernels, block_sums(): pl.pallas_call(functools.partial(block_kernel, (n_ctx, half, reach, key_w...  4.59 us
    pallas_call x1, Pallas kernels, per_device(): pl.pallas_call(functools.partial(prelude_kernel, (half, reach, copies)),...  2.61 us
    pallas_call x1, Pallas kernels, per_device(): pl.pallas_call(pack_kernel, out_shape=(jax.ShapeDtypeStruct((key_width +...  1.04 us
  transfers between devices with their start and end apart: 14, of which 7 were waited for; matrix products, arithmetic and copies ran while one was open for 0% of the time, Pallas kernels for 16%

profile of v6, /device:TPU:6, one launch (start us, length us, event | category | flops | bytes accessed | tf_op | source)
XLA Modules:
  0.0 45.1 jit_solution(8405920242646887425)
XLA Ops:
  0.0 0.0 copy-start.1
  0.0 0.0 copy-start
  0.0 1.0 %pack.1 = (bf16[704,128]{1,0:T(8,128)(2,1)S(1)}, bf16[352,128]{1,0:T(8,128)(2,1)S(1)}) custom-call(bf16[576,128]{1,0:T(8,128)(2,1)} %bitcast.6, bf16[128,128]{1,0:T(8,128)(2,1)} %index_hbm.1), custom_call_target="tpu_custom_call" | custom-call | tf_op jit(solution)/shard_map/pack/pallas_call | solution.py:310
  1.1 0.1 collective-permute-start.6
  1.1 2.0 %collective-permute-start.4 = (bf16[704,128]{1,0:T(8,128)(2,1)S(1)}, bf16[704,128]{1,0:T(8,128)(2,1)S(1)}, u32[]{:S(2)}, u32[]{:S(2)}) collective-permute-start(bf16[704,128]{1,0:T(8,128)(2,1)S(1)} %get-tuple-element.21.refs_0_), channel_id=1, source_target_pairs={{0,16},{4,20},{8,24},{12,28},{16,0},{20,4},{24,8},{28,12},{1,17},{... | collective-permute-start | bytes 540680 | tf_op jit(solution)/shard_map/ppermute | solution.py:19
  3.1 1.5 %collective-permute-start.2 = (bf16[704,128]{1,0:T(8,128)(2,1)S(1)}, bf16[704,128]{1,0:T(8,128)(2,1)S(1)}, u32[]{:S(2)}, u32[]{:S(2)}) collective-permute-start(bf16[704,128]{1,0:T(8,128)(2,1)S(1)} %get-tuple-element.21.refs_0_), channel_id=1, source_target_pairs={{0,8},{4,12},{8,0},{12,4},{16,24},{20,28},{24,16},{28,20},{1,9},{5... | collective-permute-start | bytes 540680 | tf_op jit(solution)/shard_map/ppermute | solution.py:19
  4.6 2.9 %collective-permute-done.6.refs_6_ = bf16[352,128]{1,0:T(8,128)(2,1)S(1)} collective-permute-done((bf16[352,128]{1,0:T(8,128)(2,1)S(1)}, bf16[352,128]{1,0:T(8,128)(2,1)S(1)}, u32[]{:S(2)}, u32[]{:S(2)}) %collective-permute-start.6) | collective-permute-done | bytes 90144 | tf_op jit(solution)/shard_map/ppermute | solution.py:19
  7.5 0.0 collective-permute-start.8
  7.5 2.6 %prelude.1 = (f32[2,64,256]{2,1,0:T(8,128)S(1)}, bf16[128,18432]{1,0:T(8,128)(2,1)S(1)}, bf16[64,2176]{1,0:T(8,128)(2,1)S(1)}, bf16[64,2176]{1,0:T(8,128)(2,1)S(1)}) custom-call(s32[16]{0:T(128)} %order_ref.3, s32[8,128]{1,0:T(8,128)} %bitcast.5, bf16[16,128]{1,0:T(8,128)(2,1)} %bitcast.7, bf16[128,18432]{1,0:T(8,128)(2,1)} %query_hbm.1, ...), custom_call_target="tpu_custom_call" | custom-call | flops 1048576 | bytes 10485760 | tf_op jit(solution)/shard_map/prelude/pallas_call | solution.py:336
  10.1 1.6 %collective-permute-start = (bf16[64,2176]{1,0:T(8,128)(2,1)S(1)}, bf16[64,2176]{1,0:T(8,128)(2,1)S(1)}, u32[]{:S(2)}, u32[]{:S(2)}) collective-permute-start(bf16[64,2176]{1,0:T(8,128)(2,1)S(1)} %get-tuple-element.20), channel_id=1, source_target_pairs={{0,1},{1,0},{2,3},{3,2},{4,5},{5,4},{6,7},{7,6},{8,9},{9,8},{10,11... | collective-permute-start | bytes 835592 | tf_op jit(solution)/shard_map/ppermute | solution.py:19
  11.7 0.2 collective-permute-start.1
  11.9 0.0 collective-permute-done.8.refs_8_
  11.9 0.5 %collective-permute-start.7 = (bf16[352,128]{1,0:T(8,128)(2,1)S(1)}, bf16[352,128]{1,0:T(8,128)(2,1)S(1)}, u32[]{:S(2)}, u32[]{:S(2)}) collective-permute-start(bf16[352,128]{1,0:T(8,128)(2,1)S(1)} %collective-permute-done.6.refs_6_), channel_id=1, source_target_pairs={{0,1},{1,0},{2,3},{3,2},{4,5},{5,4},{6,7},{7,6},{8,9},{9,8},{10,11... | collective-permute-start | bytes 270344 | tf_op jit(solution)/shard_map/ppermute | solution.py:19
  12.5 0.0 collective-permute-done.4.refs_4_
  12.5 0.0 collective-permute-start.5
  12.5 0.0 collective-permute-done.2.refs_2_
  12.5 0.5 %collective-permute-start.3 = (bf16[704,128]{1,0:T(8,128)(2,1)S(1)}, bf16[704,128]{1,0:T(8,128)(2,1)S(1)}, u32[]{:S(2)}, u32[]{:S(2)}) collective-permute-start(bf16[704,128]{1,0:T(8,128)(2,1)S(1)} %collective-permute-done.2.refs_2_), channel_id=1, source_target_pairs={{0,4},{4,0},{8,12},{12,8},{16,20},{20,16},{24,28},{28,24},{1,5},{5... | collective-permute-start | bytes 540680 | tf_op jit(solution)/shard_map/ppermute | solution.py:19
  13.0 8.2 %collective-permute-done.7.refs_7_ = bf16[352,128]{1,0:T(8,128)(2,1)S(1)} collective-permute-done((bf16[352,128]{1,0:T(8,128)(2,1)S(1)}, bf16[352,128]{1,0:T(8,128)(2,1)S(1)}, u32[]{:S(2)}, u32[]{:S(2)}) %collective-permute-start.7) | collective-permute-done | bytes 90144 | tf_op jit(solution)/shard_map/ppermute | solution.py:19
  21.2 0.0 collective-permute-start.9
  21.2 0.0 collective-permute-done.1.refs_1_
  21.2 1.3 %collective-permute-done.9.refs_9_ = bf16[352,128]{1,0:T(8,128)(2,1)S(1)} collective-permute-done((bf16[352,128]{1,0:T(8,128)(2,1)S(1)}, bf16[352,128]{1,0:T(8,128)(2,1)S(1)}, u32[]{:S(2)}, u32[]{:S(2)}) %collective-permute-start.9) | collective-permute-done | bytes 90144 | tf_op jit(solution)/shard_map/ppermute | solution.py:19
  22.5 0.0 collective-permute-done.5.refs_5_
  22.5 0.0 collective-permute-done.3.refs_3_
  22.5 0.0 copy-done.1
  22.5 0.0 copy-done
  22.5 2.2 %give_sums.1 = (f32[64,256]{1,0:T(8,128)S(1)}, bf16[8,704,128]{2,1,0:T(8,128)(2,1)S(1)}) custom-call(s32[16]{0:T(128)S(1)} %copy-done.1, s32[1024]{0:T(1024)S(1)} %copy-done, f32[2,64,256]{2,1,0:T(8,128)S(1)} %get-tuple-element.17.bias_ref, bf16[128,18432]{1,0:T(8,128)(2,1)S(1)} %get-tuple-element.18.query_ref, ...), custom_call_target="tpu_custom_call" | custom-call | flops 671088640 | bytes 4194304 | tf_op jit(solution)/shard_map/give_sums/pallas_call | solution.py:363
  24.7 1.6 %collective-permute-start.10 = (f32[64,256]{1,0:T(8,128)S(1)}, f32[64,256]{1,0:T(8,128)S(1)}, u32[]{:S(2)}, u32[]{:S(2)}) collective-permute-start(f32[64,256]{1,0:T(8,128)S(1)} %get-tuple-element.25), channel_id=1, source_target_pairs={{0,1},{1,0},{2,3},{3,2},{4,5},{5,4},{6,7},{7,6},{8,9},{9,8},{10,11... | collective-permute-start | bytes 196616 | tf_op jit(solution)/shard_map/ppermute | solution.py:19
  26.3 0.0 collective-permute-done.refs_1_
  26.3 2.4 %keep_sums.1 = (f32[64,256]{1,0:T(8,128)S(1)}, f32[64,256]{1,0:T(8,128)S(1)}) custom-call(s32[16]{0:T(128)S(1)} %copy-done.1, s32[1024]{0:T(1024)S(1)} %copy-done, f32[2,64,256]{2,1,0:T(8,128)S(1)} %get-tuple-element.17.bias_ref, bf16[128,18432]{1,0:T(8,128)(2,1)S(1)} %get-tuple-element.18.query_ref, bf16[64,2176]{1,0:T(8,128)(2,1)S(1)} %get-tuple-element.19.refs_0_, ...), custom_call_target="tpu_custom_call" | custom-call | flops 671088640 | bytes 4194304 | tf_op jit(solution)/shard_map/keep_sums/pallas_call | solution.py:363
  28.7 0.9 %collective-permute-done.10.taken_ref = f32[64,256]{1,0:T(8,128)S(1)} collective-permute-done((f32[64,256]{1,0:T(8,128)S(1)}, f32[64,256]{1,0:T(8,128)S(1)}, u32[]{:S(2)}, u32[]{:S(2)}) %collective-permute-start.10) | collective-permute-done | bytes 65568 | tf_op jit(solution)/shard_map/ppermute | solution.py:19
  29.6 2.7 %collective-permute-start.11 = (f32[2,32,256]{2,1,0:T(8,128)S(1)}, f32[2,32,256]{2,1,0:T(8,128)S(1)}, u32[]{:S(2)}, u32[]{:S(2)}) collective-permute-start(f32[2,32,256]{2,1,0:T(8,128)S(1)} %get-tuple-element.28), channel_id=1, source_target_pairs={{0,2},{1,3},{2,0},{3,1},{4,6},{5,7},{6,4},{7,5},{8,10},{9,11},{10,... | collective-permute-start | bytes 196616 | tf_op jit(solution)/shard_map/ppermute | solution.py:19
  32.3 4.0 %collective-permute-done.11.refs_1_ = f32[2,32,256]{2,1,0:T(8,128)S(1)} collective-permute-done((f32[2,32,256]{2,1,0:T(8,128)S(1)}, f32[2,32,256]{2,1,0:T(8,128)S(1)}, u32[]{:S(2)}, u32[]{:S(2)}) %collective-permute-start.11) | collective-permute-done | bytes 65568 | tf_op jit(solution)/shard_map/ppermute | solution.py:19
  36.2 0.2 row_losses.1
  36.4 1.3 %collective-permute-start.12 = (f32[1,128]{1,0:T(1,128)S(1)}, f32[1,128]{1,0:T(1,128)S(1)}, u32[]{:S(2)}, u32[]{:S(2)}) collective-permute-start(f32[1,128]{1,0:T(1,128)S(1)} %row_losses.1), channel_id=1, source_target_pairs={{0,2},{1,3},{2,0},{3,1},{4,6},{5,7},{6,4},{7,5},{8,10},{9,11},{10,... | collective-permute-start | bytes 1544 | tf_op jit(solution)/shard_map/ppermute | solution.py:19
  37.7 3.3 %collective-permute-done.12 = f32[1,128]{1,0:T(1,128)S(1)} collective-permute-done((f32[1,128]{1,0:T(1,128)S(1)}, f32[1,128]{1,0:T(1,128)S(1)}, u32[]{:S(2)}, u32[]{:S(2)}) %collective-permute-start.12) | collective-permute-done | bytes 544 | tf_op jit(solution)/shard_map/ppermute | solution.py:19
  41.0 0.9 %collective-permute-start.13 = (f32[1,128]{1,0:T(1,128)S(1)}, f32[1,128]{1,0:T(1,128)S(1)}, u32[]{:S(2)}, u32[]{:S(2)}) collective-permute-start(f32[1,128]{1,0:T(1,128)S(1)} %add.6), channel_id=1, source_target_pairs={{0,1},{1,0},{2,3},{3,2},{4,5},{5,4},{6,7},{7,6},{8,9},{9,8},{10,11... | collective-permute-start | bytes 1544 | tf_op jit(solution)/shard_map/ppermute | solution.py:19
  41.9 2.6 %collective-permute-done.13 = f32[1,128]{1,0:T(1,128)S(1)} collective-permute-done((f32[1,128]{1,0:T(1,128)S(1)}, f32[1,128]{1,0:T(1,128)S(1)}, u32[]{:S(2)}, u32[]{:S(2)}) %collective-permute-start.13) | collective-permute-done | bytes 544 | tf_op jit(solution)/shard_map/ppermute | solution.py:19
  44.5 0.5 %add_bitcast_fusion = f32[128]{0:T(128)} fusion(f32[1,128]{1,0:T(1,128)S(1)} %add.6, f32[1,128]{1,0:T(1,128)S(1)} %collective-permute-done.13), kind=kLoop, calls=%fused_computation | loop fusion | flops 128 | bytes 1536 | tf_op jit(solution)/shard_map/reshape | solution.py:412
  (2 shorter events, 0.0 us)
Async XLA Ops:
  0.0 22.5 %copy-start.1 = (s32[16]{0:T(128)S(1)}, s32[16]{0:T(128)}, u32[]{:S(2)}) copy-start(s32[16]{0:T(128)} %order_ref.3) | copy-start | bytes 196
  0.0 22.5 %copy-start = (s32[1024]{0:T(1024)S(1)}, s32[1024]{0:T(1024)}, u32[]{:S(2)}) copy-start(s32[1024]{0:T(1024)} %seg_ref.3) | copy-start | bytes 12292
  1.1 6.5 %collective-permute-start.6 = (bf16[352,128]{1,0:T(8,128)(2,1)S(1)}, bf16[352,128]{1,0:T(8,128)(2,1)S(1)}, u32[]{:S(2)}, u32[]{:S(2)}) collective-permute-start(bf16[352,128]{1,0:T(8,128)(2,1)S(1)} %get-tuple-element.22), channel_id=1, source_target_pairs={{0,24},{4,28},{8,16},{12,20},{16,8},{20,12},{24,0},{28,4},{1,25},{... | collective-permute-start | bytes 270344 | tf_op jit(solution)/shard_map/ppermute | solution.py:19
  1.1 11.3 %collective-permute-start.4 = (bf16[704,128]{1,0:T(8,128)(2,1)S(1)}, bf16[704,128]{1,0:T(8,128)(2,1)S(1)}, u32[]{:S(2)}, u32[]{:S(2)}) collective-permute-start(bf16[704,128]{1,0:T(8,128)(2,1)S(1)} %get-tuple-element.21.refs_0_), channel_id=1, source_target_pairs={{0,16},{4,20},{8,24},{12,28},{16,0},{20,4},{24,8},{28,12},{1,17},{... | collective-permute-start | bytes 540680 | tf_op jit(solution)/shard_map/ppermute | solution.py:19
  3.1 9.3 %collective-permute-start.2 = (bf16[704,128]{1,0:T(8,128)(2,1)S(1)}, bf16[704,128]{1,0:T(8,128)(2,1)S(1)}, u32[]{:S(2)}, u32[]{:S(2)}) collective-permute-start(bf16[704,128]{1,0:T(8,128)(2,1)S(1)} %get-tuple-element.21.refs_0_), channel_id=1, source_target_pairs={{0,8},{4,12},{8,0},{12,4},{16,24},{20,28},{24,16},{28,20},{1,9},{5... | collective-permute-start | bytes 540680 | tf_op jit(solution)/shard_map/ppermute | solution.py:19
  7.5 4.4 %collective-permute-start.8 = (bf16[352,128]{1,0:T(8,128)(2,1)S(1)}, bf16[352,128]{1,0:T(8,128)(2,1)S(1)}, u32[]{:S(2)}, u32[]{:S(2)}) collective-permute-start(bf16[352,128]{1,0:T(8,128)(2,1)S(1)} %collective-permute-done.6.refs_6_), channel_id=1, source_target_pairs={{0,4},{4,0},{8,12},{12,8},{16,20},{20,16},{24,28},{28,24},{1,5},{5... | collective-permute-start | bytes 270344 | tf_op jit(solution)/shard_map/ppermute | solution.py:19
  10.1 16.1 %collective-permute-start = (bf16[64,2176]{1,0:T(8,128)(2,1)S(1)}, bf16[64,2176]{1,0:T(8,128)(2,1)S(1)}, u32[]{:S(2)}, u32[]{:S(2)}) collective-permute-start(bf16[64,2176]{1,0:T(8,128)(2,1)S(1)} %get-tuple-element.20), channel_id=1, source_target_pairs={{0,1},{1,0},{2,3},{3,2},{4,5},{5,4},{6,7},{7,6},{8,9},{9,8},{10,11... | collective-permute-start | bytes 835592 | tf_op jit(solution)/shard_map/ppermute | solution.py:19
  11.7 9.5 %collective-permute-start.1 = (bf16[704,128]{1,0:T(8,128)(2,1)S(1)}, bf16[704,128]{1,0:T(8,128)(2,1)S(1)}, u32[]{:S(2)}, u32[]{:S(2)}) collective-permute-start(bf16[704,128]{1,0:T(8,128)(2,1)S(1)} %get-tuple-element.21.refs_0_), channel_id=1, source_target_pairs={{0,4},{4,0},{8,12},{12,8},{16,20},{20,16},{24,28},{28,24},{1,5},{5... | collective-permute-start | bytes 540680 | tf_op jit(solution)/shard_map/ppermute | solution.py:19
  11.9 9.3 %collective-permute-start.7 = (bf16[352,128]{1,0:T(8,128)(2,1)S(1)}, bf16[352,128]{1,0:T(8,128)(2,1)S(1)}, u32[]{:S(2)}, u32[]{:S(2)}) collective-permute-start(bf16[352,128]{1,0:T(8,128)(2,1)S(1)} %collective-permute-done.6.refs_6_), channel_id=1, source_target_pairs={{0,1},{1,0},{2,3},{3,2},{4,5},{5,4},{6,7},{7,6},{8,9},{9,8},{10,11... | collective-permute-start | bytes 270344 | tf_op jit(solution)/shard_map/ppermute | solution.py:19
  12.5 10.0 %collective-permute-start.5 = (bf16[704,128]{1,0:T(8,128)(2,1)S(1)}, bf16[704,128]{1,0:T(8,128)(2,1)S(1)}, u32[]{:S(2)}, u32[]{:S(2)}) collective-permute-start(bf16[704,128]{1,0:T(8,128)(2,1)S(1)} %collective-permute-done.4.refs_4_), channel_id=1, source_target_pairs={{0,4},{4,0},{8,12},{12,8},{16,20},{20,16},{24,28},{28,24},{1,5},{5... | collective-permute-start | bytes 540680 | tf_op jit(solution)/shard_map/ppermute | solution.py:19
  12.5 10.0 %collective-permute-start.3 = (bf16[704,128]{1,0:T(8,128)(2,1)S(1)}, bf16[704,128]{1,0:T(8,128)(2,1)S(1)}, u32[]{:S(2)}, u32[]{:S(2)}) collective-permute-start(bf16[704,128]{1,0:T(8,128)(2,1)S(1)} %collective-permute-done.2.refs_2_), channel_id=1, source_target_pairs={{0,4},{4,0},{8,12},{12,8},{16,20},{20,16},{24,28},{28,24},{1,5},{5... | collective-permute-start | bytes 540680 | tf_op jit(solution)/shard_map/ppermute | solution.py:19
  21.2 1.3 %collective-permute-start.9 = (bf16[352,128]{1,0:T(8,128)(2,1)S(1)}, bf16[352,128]{1,0:T(8,128)(2,1)S(1)}, u32[]{:S(2)}, u32[]{:S(2)}) collective-permute-start(bf16[352,128]{1,0:T(8,128)(2,1)S(1)} %collective-permute-done.7.refs_7_), channel_id=1, source_target_pairs={{0,4},{4,0},{8,12},{12,8},{16,20},{20,16},{24,28},{28,24},{1,5},{5... | collective-permute-start | bytes 270344 | tf_op jit(solution)/shard_map/ppermute | solution.py:19
  24.7 4.9 %collective-permute-start.10 = (f32[64,256]{1,0:T(8,128)S(1)}, f32[64,256]{1,0:T(8,128)S(1)}, u32[]{:S(2)}, u32[]{:S(2)}) collective-permute-start(f32[64,256]{1,0:T(8,128)S(1)} %get-tuple-element.25), channel_id=1, source_target_pairs={{0,1},{1,0},{2,3},{3,2},{4,5},{5,4},{6,7},{7,6},{8,9},{9,8},{10,11... | collective-permute-start | bytes 196616 | tf_op jit(solution)/shard_map/ppermute | solution.py:19
  29.6 6.6 %collective-permute-start.11 = (f32[2,32,256]{2,1,0:T(8,128)S(1)}, f32[2,32,256]{2,1,0:T(8,128)S(1)}, u32[]{:S(2)}, u32[]{:S(2)}) collective-permute-start(f32[2,32,256]{2,1,0:T(8,128)S(1)} %get-tuple-element.28), channel_id=1, source_target_pairs={{0,2},{1,3},{2,0},{3,1},{4,6},{5,7},{6,4},{7,5},{8,10},{9,11},{10,... | collective-permute-start | bytes 196616 | tf_op jit(solution)/shard_map/ppermute | solution.py:19
  36.4 4.5 %collective-permute-start.12 = (f32[1,128]{1,0:T(1,128)S(1)}, f32[1,128]{1,0:T(1,128)S(1)}, u32[]{:S(2)}, u32[]{:S(2)}) collective-permute-start(f32[1,128]{1,0:T(1,128)S(1)} %row_losses.1), channel_id=1, source_target_pairs={{0,2},{1,3},{2,0},{3,1},{4,6},{5,7},{6,4},{7,5},{8,10},{9,11},{10,... | collective-permute-start | bytes 1544 | tf_op jit(solution)/shard_map/ppermute | solution.py:19
  41.0 3.6 %collective-permute-start.13 = (f32[1,128]{1,0:T(1,128)S(1)}, f32[1,128]{1,0:T(1,128)S(1)}, u32[]{:S(2)}, u32[]{:S(2)}) collective-permute-start(f32[1,128]{1,0:T(1,128)S(1)} %add.6), channel_id=1, source_target_pairs={{0,1},{1,0},{2,3},{3,2},{4,5},{5,4},{6,7},{7,6},{8,9},{9,8},{10,11... | collective-permute-start | bytes 1544 | tf_op jit(solution)/shard_map/ppermute | solution.py:19
